TPU v7x, 32 devices: a whole 2x2x4 slice. The times are simulated.
32 devices in a mesh: groups: 1, row: 32 (over z, y, x, core), col: 1.
Axes of the slice: x: 2, y: 2, z: 4, core: 2. Of those that a mesh axis runs over, the one named last changes fastest.
Arguments:
- pair: bfloat16 [128, 128, 128], P(('groups', 'row'), 'col'), may hold values from -6 to 6
- token_mask: int32 [128], P('groups'), may hold values 0 or 1
- tri_in_weight: bfloat16 [128, 512], replicated, may hold values from -0.5 to 0.5
- tri_gate_weight: bfloat16 [128, 128], replicated, may hold values from -0.5 to 0.5
- tri_out_weight: bfloat16 [128, 128], replicated, may hold values from -0.5 to 0.5
- atom_act: bfloat16 [2048, 128], P(('groups', 'row')), may hold values from -6 to 6
- atom_cond: bfloat16 [2048, 128], P(('groups', 'row')), may hold values from -60 to 60
- atom_token: int32 [2048], P(('groups', 'row')), may hold values from 0 to 127, as said below
- atom_mask: int32 [2048], P(('groups', 'row')), may hold values from 0 to 1, as said below
- ada_weight: bfloat16 [128, 256], replicated, may hold values from -0.5 to 0.5
- qkv_weight: bfloat16 [128, 384], replicated, may hold values from -0.5 to 0.5
- bias_weight: bfloat16 [128, 4], replicated, may hold values from -0.5 to 0.5
- attn_out_weight: bfloat16 [128, 128], replicated, may hold values from -0.5 to 0.5
- ffn_in_weight: bfloat16 [128, 512], replicated, may hold values from -0.5 to 0.5
- ffn_out_weight: bfloat16 [256, 128], replicated, may hold values from -0.375 to 0.375
- agg_weight: bfloat16 [128, 384], replicated, may hold values from -0.5 to 0.5
Outputs:
- pair_out: bfloat16 [128, 128, 128], P(('groups', 'row'), 'col')
- atom_out: bfloat16 [2048, 128], P(('groups', 'row'))
- token_out: bfloat16 [128, 384], P(('groups', 'row'))
Inputs may be any that keep to these rules, and one draw needn't show every extreme that they name: `atom_token`: Nondecreasing; slots r * 64 to (r + 1) * 64 - 1 hold the atoms of tokens r * 4 to (r + 1) * 4 - 1 followed by padding slots that name the last of those tokens; every token has 1 to 24 atoms. `atom_mask`: in each slab of 64 slots the atoms come first and at most 31 padding slots follow.
All inputs are finite; a program needn't handle non-finite values.
Results may differ from a plain program's by a relative error of at most 0.012.
The roundings to bfloat16 on the way count: a program that leaves them out, or rounds other values in their place, can miss the bound.
Values may be sent and summed in bfloat16 or wider, within the bound.
No kernel may reach another device: no remote copies, remote signals or barrier semaphores. Data moves between devices by JAX's collectives and lax.ppermute only.
A program may use at most 64 MiB of HBM per device.

v0:
```python
import math

import jax
import jax.numpy as jnp
from jax import lax
from jax.sharding import PartitionSpec as P

QUERY_WINDOW = 32
KEYS = 128


EPSILON = 1e-05


def extended(shard, sides, width):
    for axis, dim in sides:
        size, length = (lax.axis_size(axis), shard.shape[dim])
        up = [(i, (i + 1) % size) for i in range(size - 1)]
        down = [(j, i) for i, j in up]
        last = lax.slice_in_dim(shard, length - width, length, axis=dim)
        first = lax.slice_in_dim(shard, 0, width, axis=dim)
        before = lax.ppermute(last, axis, up)
        after = lax.ppermute(first, axis, down)
        shard = jnp.concatenate([before, shard, after], axis=dim)
    return shard


def layer_norm(values, along):
    average = jnp.mean(values, axis=along, keepdims=True)
    centred = values - average
    spread = jnp.mean(centred * centred, axis=along, keepdims=True)
    return centred / jnp.sqrt(spread + EPSILON)


def per_device(
    pair,
    token_mask,
    tri_in_weight,
    tri_gate_weight,
    tri_out_weight,
    atom_act,
    atom_cond,
    atom_token,
    atom_mask,
    ada_weight,
    qkv_weight,
    bias_weight,
    attn_out_weight,
    ffn_in_weight,
    ffn_out_weight,
    agg_weight,
):
    tok_rows = pair.shape[0]
    col_count = pair.shape[1]
    channels = pair.shape[2]
    row_index = lax.axis_index("row")
    col_index = lax.axis_index("col")
    pair_float = pair.astype(jnp.float32)
    pair_norm = layer_norm(pair_float, 2).astype(jnp.bfloat16)
    row_live = lax.dynamic_slice_in_dim(token_mask, row_index * tok_rows, tok_rows, 0).astype(
        jnp.float32
    )
    col_live = lax.dynamic_slice_in_dim(token_mask, col_index * col_count, col_count, 0).astype(
        jnp.float32
    )
    pair_live = row_live[:, None] * col_live[None, :]
    left_terms = jnp.einsum(
        "ijd,de->eij",
        pair_norm,
        tri_in_weight[:, : 2 * channels],
        preferred_element_type=jnp.float32,
    )
    left = (jax.nn.sigmoid(left_terms[channels:]) * left_terms[:channels] * pair_live).astype(
        jnp.bfloat16
    )
    right_terms = jnp.einsum(
        "ijd,de->eij",
        pair_norm,
        tri_in_weight[:, 2 * channels :],
        preferred_element_type=jnp.float32,
    )
    right = (jax.nn.sigmoid(right_terms[channels:]) * right_terms[:channels] * pair_live).astype(
        jnp.bfloat16
    )
    tri_gate = jax.nn.sigmoid(
        jnp.einsum("ijd,de->ije", pair_norm, tri_gate_weight, preferred_element_type=jnp.float32)
    )
    left_owned, right_owned = (
        lax.all_to_all(left, "row", split_axis=0, concat_axis=1, tiled=True),
        lax.all_to_all(right, "row", split_axis=0, concat_axis=1, tiled=True),
    )
    left_full, right_rows = (
        lax.all_gather(left_owned, "col", axis=2, tiled=True),
        lax.all_gather(right_owned, "col", axis=2, tiled=True),
    )
    right_used = lax.dynamic_slice_in_dim(right_rows, col_index * col_count, col_count, 1)
    tri_sum = jnp.einsum(
        "cik,cjk->cij", left_full, right_used, preferred_element_type=jnp.float32
    ).astype(jnp.bfloat16)
    merged = lax.all_to_all(tri_sum, "row", split_axis=1, concat_axis=0, tiled=True)
    tri_norm = layer_norm(merged.astype(jnp.float32), 0).astype(jnp.bfloat16)
    update = jnp.einsum("dij,de->ije", tri_norm, tri_out_weight, preferred_element_type=jnp.float32)
    pair_out = (pair_float + tri_gate * update).astype(jnp.bfloat16)
    band_width = 3 * tok_rows
    targets = (row_index - 1) * tok_rows + jnp.arange(band_width, dtype=jnp.int32)
    columns = col_index * col_count + jnp.arange(col_count, dtype=jnp.int32)
    selector = (columns[:, None] == targets[None, :]).astype(jnp.bfloat16)
    band_part = jnp.einsum("ijd,jb->ibd", pair_out, selector, preferred_element_type=jnp.float32)
    band = lax.psum(band_part.astype(jnp.bfloat16), "col").astype(jnp.float32)
    band_norm = layer_norm(band, 2).astype(jnp.bfloat16)
    bias_table = jnp.einsum(
        "ibd,dh->ibh", band_norm, bias_weight, preferred_element_type=jnp.float32
    ).astype(jnp.bfloat16)
    slab = atom_act.shape[0]
    window_width = atom_act.shape[1]
    heads = bias_weight.shape[1]
    head_size = window_width // heads
    side = (KEYS - QUERY_WINDOW) // 2
    windows = slab // QUERY_WINDOW
    local_token = atom_token - row_index * tok_rows
    live = atom_mask.astype(jnp.float32)
    token_tag = ((local_token + 1) * atom_mask).astype(jnp.bfloat16)
    ada = jnp.dot(atom_cond, ada_weight, preferred_element_type=jnp.float32)
    atom_inputs = (
        jax.nn.sigmoid(ada[:, :window_width]) * layer_norm(atom_act.astype(jnp.float32), 1)
        + ada[:, window_width:]
    ).astype(jnp.bfloat16)
    projected = jnp.dot(atom_inputs, qkv_weight, preferred_element_type=jnp.float32).astype(
        jnp.bfloat16
    )
    queries = projected[:, :window_width]
    ext_pairs, ext_tag = (
        extended(projected[:, window_width:], (("row", 0),), side),
        extended(token_tag, (("row", 0),), side),
    )
    ext_rows = slab + 2 * side
    ext_position = jnp.arange(ext_rows, dtype=jnp.int32)
    offset = jnp.where(
        ext_position < side, 0, jnp.where(ext_position < side + slab, tok_rows, 2 * tok_rows)
    )
    tag_value = ext_tag.astype(jnp.int32)
    key_valid = tag_value > 0
    band_index = tag_value - 1 + offset
    band_slots = jnp.arange(band_width, dtype=jnp.int32)
    key_onehot = ((band_index[:, None] == band_slots[None, :]) & key_valid[:, None]).astype(
        jnp.bfloat16
    )
    query_onehot = (local_token[:, None] == jnp.arange(tok_rows, dtype=jnp.int32)[None, :]).astype(
        jnp.bfloat16
    )
    query_bias = jnp.einsum(
        "lt,tbh->lbh", query_onehot, bias_table, preferred_element_type=jnp.float32
    ).astype(jnp.bfloat16)
    query_bias = query_bias.reshape(windows, QUERY_WINDOW, band_width, heads)
    key_index = (
        jnp.arange(windows, dtype=jnp.int32)[:, None] * QUERY_WINDOW
        + jnp.arange(KEYS, dtype=jnp.int32)[None, :]
    )
    window_pairs = ext_pairs[key_index]
    window_onehot = key_onehot[key_index]
    window_valid = key_valid[key_index]
    window_bias = jnp.einsum(
        "wlbh,wmb->whlm", query_bias, window_onehot, preferred_element_type=jnp.float32
    )
    query_heads = queries.reshape(windows, QUERY_WINDOW, heads, head_size)
    key_heads = window_pairs[..., :window_width].reshape(windows, KEYS, heads, head_size)
    value_heads = window_pairs[..., window_width:].reshape(windows, KEYS, heads, head_size)
    logit_scores = (
        jnp.einsum("wlhd,wmhd->whlm", query_heads, key_heads, preferred_element_type=jnp.float32)
        / math.sqrt(head_size)
        + window_bias
    )
    logit_scores = jnp.where(window_valid[:, None, None, :], logit_scores, -1e30)
    attn_weights = jax.nn.softmax(logit_scores, axis=-1).astype(jnp.bfloat16)
    attended = (
        jnp.einsum("whlm,wmhd->wlhd", attn_weights, value_heads, preferred_element_type=jnp.float32)
        .reshape(slab, window_width)
        .astype(jnp.bfloat16)
    )
    atom_mid = atom_act.astype(jnp.float32) + jnp.dot(
        attended, attn_out_weight, preferred_element_type=jnp.float32
    )
    atom_norm = layer_norm(atom_mid, 1).astype(jnp.bfloat16)
    expanded = jnp.dot(atom_norm, ffn_in_weight, preferred_element_type=jnp.float32)
    hidden_width = ffn_out_weight.shape[0]
    inner = (jax.nn.silu(expanded[:, :hidden_width]) * expanded[:, hidden_width:]).astype(
        jnp.bfloat16
    )
    atom_out = (
        (atom_mid + jnp.dot(inner, ffn_out_weight, preferred_element_type=jnp.float32))
        * live[:, None]
    ).astype(jnp.bfloat16)
    features = jax.nn.relu(
        jnp.dot(atom_out, agg_weight, preferred_element_type=jnp.float32)
    ).astype(jnp.bfloat16)
    live_onehot = query_onehot * atom_mask.astype(jnp.bfloat16)[:, None]
    token_sums = jnp.einsum("at,ac->tc", live_onehot, features, preferred_element_type=jnp.float32)
    token_counts = jnp.sum(live_onehot.astype(jnp.float32), axis=0)
    token_out = (token_sums / token_counts[:, None]).astype(jnp.bfloat16)
    return (pair_out, atom_out, token_out)


def solution(mesh):
    in_specs = (
        P(("groups", "row"), "col", None),
        P("groups"),
        P(),
        P(),
        P(),
        P(("groups", "row"), None),
        P(("groups", "row"), None),
        P(("groups", "row")),
        P(("groups", "row")),
        P(),
        P(),
        P(),
        P(),
        P(),
        P(),
        P(),
    )
    out_specs = (
        P(("groups", "row"), "col", None),
        P(("groups", "row"), None),
        P(("groups", "row"), None),
    )
    return jax.shard_map(
        per_device, mesh=mesh, in_specs=in_specs, out_specs=out_specs, check_vma=False
    )
```

profile of v0, /device:TPU:0, one launch (start us, length us, event | category | flops | bytes accessed | tf_op | source)
XLA Modules:
  0.0 61.1 jit_solution(8596969497097267078)
XLA Ops:
  0.7 1.1 %convert_reduce_fusion = f32[4,128]{1,0:T(4,128)S(1)} fusion(bf16[4,128,128]{2,1,0:T(8,128)(2,1)} %param.16), kind=kLoop, calls=%fused_computation.38 | loop fusion | flops 130560 | bytes 133120 | tf_op jit(solution)/shard_map/reduce_sum | solution.py:29
  2.7 0.6 %copy-done.17 = s32[128]{0:T(128)S(1)} copy-done((s32[128]{0:T(128)S(1)}, s32[128]{0:T(128)}, u32[]{:S(2)}) %copy-start.17) | copy-done | bytes 536
  3.7 0.8 %copy.43 = bf16[128,4,128]{2,1,0:T(4,128)(2,1)} copy(bf16[128,4,128]{0,2,1:T(8,128)(2,1)S(1)} %get-tuple-element.11) | data formatting | bytes 262144 | tf_op jit(solution)/shard_map/convert_element_type | solution.py:82
  4.5 7.3 %all-to-all-start.1 = ((bf16[128,4,128]{2,1,0:T(4,128)(2,1)}), bf16[128,4,128]{2,1,0:T(4,128)(2,1)S(1)}, u32[]{:S(2)}, u32[]{:S(2)}) async-start(bf16[128,4,128]{2,1,0:T(4,128)(2,1)} %copy.43), calls=%async_computation.1 | async-start | bytes 262144 | tf_op jit(solution)/shard_map/all_to_all | solution.py:90
  11.9 2.1 %collective-permute-start.2 = (bf16[48]{0:T(256)(128)(2,1)S(1)}, bf16[48]{0:T(256)(128)(2,1)S(1)}, u32[]{:S(2)}, u32[]{:S(2)}) collective-permute-start(bf16[48]{0:T(256)(128)(2,1)S(1)} %get-tuple-element.15), channel_id=1, source_target_pairs={{0,1},{1,2},{2,3},{3,4},{4,5},{5,6},{6,7},{7,8},{8,9},{9,10},{10,1... | collective-permute-start | bytes 296 | tf_op jit(solution)/shard_map/ppermute | solution.py:22
  14.1 1.3 %collective-permute-start.3 = (bf16[48]{0:T(256)(128)(2,1)S(1)}, bf16[48]{0:T(256)(128)(2,1)S(1)}, u32[]{:S(2)}, u32[]{:S(2)}) collective-permute-start(bf16[48]{0:T(256)(128)(2,1)S(1)} %get-tuple-element.16), channel_id=1, source_target_pairs={{1,0},{2,1},{3,2},{4,3},{5,4},{6,5},{7,6},{8,7},{9,8},{10,9},{11,1... | collective-permute-start | bytes 296 | tf_op jit(solution)/shard_map/ppermute | solution.py:23
  16.1 4.2 %collective-permute-start = (bf16[48,256]{1,0:T(8,128)(2,1)S(1)}, bf16[48,256]{1,0:T(8,128)(2,1)S(1)}, u32[]{:S(2)}, u32[]{:S(2)}) collective-permute-start(bf16[48,256]{1,0:T(8,128)(2,1)S(1)} %get-tuple-element.9), channel_id=1, source_target_pairs={{0,1},{1,2},{2,3},{3,4},{4,5},{5,6},{6,7},{7,8},{8,9},{9,10},{10,1... | collective-permute-start | bytes 73736 | tf_op jit(solution)/shard_map/ppermute | solution.py:22
  20.3 1.3 %collective-permute-start.1 = (bf16[48,256]{1,0:T(8,128)(2,1)S(1)}, bf16[48,256]{1,0:T(8,128)(2,1)S(1)}, u32[]{:S(2)}, u32[]{:S(2)}) collective-permute-start(bf16[48,256]{1,0:T(8,128)(2,1)S(1)} %get-tuple-element.10), channel_id=1, source_target_pairs={{1,0},{2,1},{3,2},{4,3},{5,4},{6,5},{7,6},{8,7},{9,8},{10,9},{11,1... | collective-permute-start | bytes 73736 | tf_op jit(solution)/shard_map/ppermute | solution.py:23
  22.1 0.8 %copy.40 = bf16[128,4,128]{2,1,0:T(4,128)(2,1)} copy(bf16[128,4,128]{0,2,1:T(8,128)(2,1)S(1)} %get-tuple-element.12) | data formatting | bytes 262144 | tf_op jit(solution)/shard_map/convert_element_type | solution.py:73
  23.2 9.8 %all-to-all-start = ((bf16[128,4,128]{2,1,0:T(4,128)(2,1)}), bf16[128,4,128]{2,1,0:T(4,128)(2,1)S(1)}, u32[]{:S(2)}, u32[]{:S(2)}) async-start(bf16[128,4,128]{2,1,0:T(4,128)(2,1)} %copy.40), calls=%async_computation | async-start | bytes 262144 | tf_op jit(solution)/shard_map/all_to_all | solution.py:89
  33.0 1.9 %gather_fusion.1 = pred[256]{0:T(512)(128)(4,1)S(1)} fusion(pred[160]{0:T(512)(128)(4,1)S(1)} %get-tuple-element.3, s32[1024]{0:T(1024)S(1)} %pad_clamp_fusion), kind=kCustom, calls=%fused_computation.1 | custom fusion | bytes 1536 | tf_op jit(solution)/shard_map/gather | solution.py:161
  35.0 0.8 %gather_fusion.2 = pred[256,12]{1,0:T(32,128)(4,1)S(1)} fusion(pred[160,12]{1,0:T(8,128)(4,1)S(1)} %fusion.37, s32[1024]{0:T(1024)S(1)} %pad_clamp_fusion), kind=kCustom, calls=%fused_computation.2 | custom fusion | bytes 7168 | tf_op jit(solution)/shard_map/gather | solution.py:160
  35.9 5.2 %all-to-all-done = bf16[128,4,128]{2,1,0:T(4,128)(2,1)S(1)} async-done(((bf16[128,4,128]{2,1,0:T(4,128)(2,1)}), bf16[128,4,128]{2,1,0:T(4,128)(2,1)S(1)}, u32[]{:S(2)}, u32[]{:S(2)}) %all-to-all-start) | async-done | bytes 131104 | tf_op jit(solution)/shard_map/all_to_all | solution.py:89
  41.5 0.8 %copy.46 = bf16[4,128,128]{2,0,1:T(4,128)(2,1)} copy(bf16[4,128,128]{2,1,0:T(8,128)(2,1)S(1)} %convolution_convert_fusion) | data formatting | bytes 262144 | tf_op jit(solution)/shard_map/convert_element_type | solution.py:99
  42.3 2.7 %all-to-all-start.2 = ((bf16[4,128,128]{2,0,1:T(4,128)(2,1)}), bf16[4,128,128]{2,0,1:T(4,128)(2,1)S(1)}, u32[]{:S(2)}, u32[]{:S(2)}) async-start(bf16[4,128,128]{2,0,1:T(4,128)(2,1)} %copy.46), calls=%async_computation.2 | async-start | bytes 262144 | tf_op jit(solution)/shard_map/all_to_all | solution.py:100
  45.1 1.2 %gather_fusion = bf16[256,256]{1,0:T(8,128)(2,1)S(1)} fusion(bf16[160,256]{1,0:T(8,128)(2,1)S(1)} %pad_maximum_fusion, s32[1024]{0:T(1024)S(1)} %pad_clamp_fusion), kind=kCustom, calls=%fused_computation | custom fusion | bytes 263168 | tf_op jit(solution)/shard_map/gather | solution.py:159
  46.5 6.7 %all-to-all-done.2 = bf16[4,128,128]{2,0,1:T(4,128)(2,1)S(1)} async-done(((bf16[4,128,128]{2,0,1:T(4,128)(2,1)}), bf16[4,128,128]{2,0,1:T(4,128)(2,1)S(1)}, u32[]{:S(2)}, u32[]{:S(2)}) %all-to-all-start.2) | async-done | bytes 131104 | tf_op jit(solution)/shard_map/all_to_all | solution.py:100
  53.5 0.7 %copy-done.15 = bf16[128,128]{1,0:T(8,128)(2,1)S(1)} copy-done((bf16[128,128]{1,0:T(8,128)(2,1)S(1)}, bf16[128,128]{1,0:T(8,128)(2,1)}, u32[]{:S(2)}) %copy-start.15) | copy-done | bytes 32792
  54.9 0.7 %copy-done.16 = bf16[128,4]{0,1:T(4,128)(2,1)S(1)} copy-done((bf16[128,4]{0,1:T(4,128)(2,1)S(1)}, bf16[128,4]{0,1:T(4,128)(2,1)}, u32[]{:S(2)}) %copy-start.16) | copy-done | bytes 1048
  56.6 0.5 fusion.11
  57.4 0.6 %copy-done.6 = bf16[128,128]{1,0:T(8,128)(2,1)S(1)} copy-done((bf16[128,128]{1,0:T(8,128)(2,1)S(1)}, bf16[128,128]{1,0:T(8,128)(2,1)}, u32[]{:S(2)}) %copy-start.6) | copy-done | bytes 32792
  58.7 0.6 %copy-done.13 = bf16[256,128]{1,0:T(8,128)(2,1)S(1)} copy-done((bf16[256,128]{1,0:T(8,128)(2,1)S(1)}, bf16[256,128]{1,0:T(8,128)(2,1)}, u32[]{:S(2)}) %copy-start.13) | copy-done | bytes 65560
  59.5 0.7 %copy-done.12 = bf16[128,384]{1,0:T(8,128)(2,1)S(1)} copy-done((bf16[128,384]{1,0:T(8,128)(2,1)S(1)}, bf16[128,384]{1,0:T(8,128)(2,1)}, u32[]{:S(2)}) %copy-start.12) | copy-done | bytes 98328
  60.2 0.8 %fusion.18 = bf16[4,384]{1,0:T(4,128)(2,1)} fusion(bf16[64,128]{1,0:T(8,128)(2,1)S(1)} %fusion.14, bf16[128,384]{1,0:T(8,128)(2,1)S(1)} %copy-done.12, f32[4]{0:T(128)S(1)} %convert_reduce_fusion.2, s32[64]{0:T(128)S(1)} %get-tuple-element.6, bf16[64]{0:T(256)(128)(2,1)S(1)} %get-tuple-element.13), kind=kOutput, calls=%fused_computation.36 | convolution fusion | flops 6540800 | bytes 118160 | tf_op jit(solution)/shard_map/at,ac->tc/dot_general | solution.py:197
  (103 shorter events, 6.5 us)
Async XLA Ops:
  0.6 57.9 %copy-start = (bf16[128,512]{1,0:T(8,128)(2,1)S(1)}, bf16[128,512]{1,0:T(8,128)(2,1)}, u32[]{:S(2)}) copy-start(bf16[128,512]{1,0:T(8,128)(2,1)} %param.29) | copy-start | bytes 393220
  0.6 1.1 %copy-start.1 = (bf16[4,128,128]{2,1,0:T(8,128)(2,1)S(1)}, bf16[4,128,128]{2,1,0:T(8,128)(2,1)}, u32[]{:S(2)}) copy-start(bf16[4,128,128]{2,1,0:T(8,128)(2,1)} %param.16) | copy-start | bytes 393220
  0.7 1.4 %copy-start.10 = (bf16[128,512]{1,0:T(8,128)(2,1)S(1)}, bf16[128,512]{1,0:T(8,128)(2,1)}, u32[]{:S(2)}) copy-start(bf16[128,512]{1,0:T(8,128)(2,1)} %param.18) | copy-start | bytes 393220
  4.4 7.4 %copy-start.8 = (s32[64]{0:T(128)S(1)}, s32[64]{0:T(128)}, u32[]{:S(2)}) copy-start(s32[64]{0:T(128)} %param.24) | copy-start | bytes 772
  4.4 7.4 %copy-start.9 = (s32[64]{0:T(128)S(1)}, s32[64]{0:T(128)}, u32[]{:S(2)}) copy-start(s32[64]{0:T(128)} %param.23) | copy-start | bytes 772
  4.4 10.9 %copy-start.3 = (bf16[64,128]{1,0:T(8,128)(2,1)S(1)}, bf16[64,128]{1,0:T(8,128)(2,1)}, u32[]{:S(2)}) copy-start(bf16[64,128]{1,0:T(8,128)(2,1)} %param.21) | copy-start | bytes 49156
  4.5 11.3 %copy-start.5 = (bf16[128,256]{1,0:T(8,128)(2,1)S(1)}, bf16[128,256]{1,0:T(8,128)(2,1)}, u32[]{:S(2)}) copy-start(bf16[128,256]{1,0:T(8,128)(2,1)} %param.25) | copy-start | bytes 196612
  4.5 11.4 %copy-start.11 = (bf16[128,384]{1,0:T(8,128)(2,1)S(1)}, bf16[128,384]{1,0:T(8,128)(2,1)}, u32[]{:S(2)}) copy-start(bf16[128,384]{1,0:T(8,128)(2,1)} %param.26) | copy-start | bytes 294916
  4.5 18.7 %all-to-all-start.1 = ((bf16[128,4,128]{2,1,0:T(4,128)(2,1)}), bf16[128,4,128]{2,1,0:T(4,128)(2,1)S(1)}, u32[]{:S(2)}, u32[]{:S(2)}) async-start(bf16[128,4,128]{2,1,0:T(4,128)(2,1)} %copy.43), calls=%async_computation.1 | async-start | bytes 262144 | tf_op jit(solution)/shard_map/all_to_all | solution.py:90
  11.9 11.2 %collective-permute-start.2 = (bf16[48]{0:T(256)(128)(2,1)S(1)}, bf16[48]{0:T(256)(128)(2,1)S(1)}, u32[]{:S(2)}, u32[]{:S(2)}) collective-permute-start(bf16[48]{0:T(256)(128)(2,1)S(1)} %get-tuple-element.15), channel_id=1, source_target_pairs={{0,1},{1,2},{2,3},{3,4},{4,5},{5,6},{6,7},{7,8},{8,9},{9,10},{10,1... | collective-permute-start | bytes 296 | tf_op jit(solution)/shard_map/ppermute | solution.py:22
  14.1 1.6 %copy-start.7 = (bf16[64,128]{1,0:T(8,128)(2,1)S(1)}, bf16[64,128]{1,0:T(8,128)(2,1)}, u32[]{:S(2)}) copy-start(bf16[64,128]{1,0:T(8,128)(2,1)} %param.22) | copy-start | bytes 49156
  14.1 9.0 %collective-permute-start.3 = (bf16[48]{0:T(256)(128)(2,1)S(1)}, bf16[48]{0:T(256)(128)(2,1)S(1)}, u32[]{:S(2)}, u32[]{:S(2)}) collective-permute-start(bf16[48]{0:T(256)(128)(2,1)S(1)} %get-tuple-element.16), channel_id=1, source_target_pairs={{1,0},{2,1},{3,2},{4,3},{5,4},{6,5},{7,6},{8,7},{9,8},{10,9},{11,1... | collective-permute-start | bytes 296 | tf_op jit(solution)/shard_map/ppermute | solution.py:23
  16.1 6.0 %copy-start.2 = (bf16[64,384]{1,0:T(8,128)(2,1)}, bf16[64,384]{1,0:T(8,128)(2,1)S(1)}, u32[]{:S(2)}) copy-start(bf16[64,384]{1,0:T(8,128)(2,1)S(1)} %convolution_convert_fusion.2) | copy-start | bytes 147460
  16.1 5.5 %copy-start.14 = (bf16[128,128]{1,0:T(8,128)(2,1)S(1)}, bf16[128,128]{1,0:T(8,128)(2,1)}, u32[]{:S(2)}) copy-start(bf16[128,128]{1,0:T(8,128)(2,1)} %param.19) | copy-start | bytes 98308
  16.1 28.9 %collective-permute-start = (bf16[48,256]{1,0:T(8,128)(2,1)S(1)}, bf16[48,256]{1,0:T(8,128)(2,1)S(1)}, u32[]{:S(2)}, u32[]{:S(2)}) collective-permute-start(bf16[48,256]{1,0:T(8,128)(2,1)S(1)} %get-tuple-element.9), channel_id=1, source_target_pairs={{0,1},{1,2},{2,3},{3,4},{4,5},{5,6},{6,7},{7,8},{8,9},{9,10},{10,1... | collective-permute-start | bytes 73736 | tf_op jit(solution)/shard_map/ppermute | solution.py:22
  20.3 24.7 %collective-permute-start.1 = (bf16[48,256]{1,0:T(8,128)(2,1)S(1)}, bf16[48,256]{1,0:T(8,128)(2,1)S(1)}, u32[]{:S(2)}, u32[]{:S(2)}) collective-permute-start(bf16[48,256]{1,0:T(8,128)(2,1)S(1)} %get-tuple-element.10), channel_id=1, source_target_pairs={{1,0},{2,1},{3,2},{4,3},{5,4},{6,5},{7,6},{8,7},{9,8},{10,9},{11,1... | collective-permute-start | bytes 73736 | tf_op jit(solution)/shard_map/ppermute | solution.py:23
  22.1 0.9 %slice-start.1 = ((bf16[64,384]{1,0:T(8,128)(2,1)}), bf16[64,128]{1,0:T(8,128)(2,1)S(1)}, s32[]{:S(2)}) async-start(bf16[64,384]{1,0:T(8,128)(2,1)} %copy-done.2), calls=%async_computation.4 | async-start | bytes 32768 | tf_op jit(solution)/shard_map/slice | solution.py:131
  23.2 18.0 %all-to-all-start = ((bf16[128,4,128]{2,1,0:T(4,128)(2,1)}), bf16[128,4,128]{2,1,0:T(4,128)(2,1)S(1)}, u32[]{:S(2)}, u32[]{:S(2)}) async-start(bf16[128,4,128]{2,1,0:T(4,128)(2,1)} %copy.40), calls=%async_computation | async-start | bytes 262144 | tf_op jit(solution)/shard_map/all_to_all | solution.py:89
  42.3 2.7 %slice-start = ((bf16[64,384]{1,0:T(8,128)(2,1)}), bf16[64,256]{1,0:T(8,128)(2,1)S(1)}, s32[]{:S(2)}) async-start(bf16[64,384]{1,0:T(8,128)(2,1)} %copy-done.2), calls=%async_computation.3 | async-start | bytes 65536 | tf_op jit(solution)/shard_map/slice | solution.py:133
  42.3 10.9 %all-to-all-start.2 = ((bf16[4,128,128]{2,0,1:T(4,128)(2,1)}), bf16[4,128,128]{2,0,1:T(4,128)(2,1)S(1)}, u32[]{:S(2)}, u32[]{:S(2)}) async-start(bf16[4,128,128]{2,0,1:T(4,128)(2,1)} %copy.46), calls=%async_computation.2 | async-start | bytes 262144 | tf_op jit(solution)/shard_map/all_to_all | solution.py:100
  54.4 1.4 %copy-start.4 = (bf16[4,128,128]{2,1,0:T(8,128)(2,1)}, bf16[4,128,128]{2,1,0:T(8,128)(2,1)S(1)}, u32[]{:S(2)}) copy-start(bf16[4,128,128]{2,1,0:T(8,128)(2,1)S(1)} %fusion.5) | copy-start | bytes 393220
  58.5 0.8 %copy-start.13 = (bf16[256,128]{1,0:T(8,128)(2,1)S(1)}, bf16[256,128]{1,0:T(8,128)(2,1)}, u32[]{:S(2)}) copy-start(bf16[256,128]{1,0:T(8,128)(2,1)} %param.30) | copy-start | bytes 196612
  59.3 0.9 %copy-start.12 = (bf16[128,384]{1,0:T(8,128)(2,1)S(1)}, bf16[128,384]{1,0:T(8,128)(2,1)}, u32[]{:S(2)}) copy-start(bf16[128,384]{1,0:T(8,128)(2,1)} %param.31) | copy-start | bytes 294916
  60.2 0.9 %copy-start.18 = (bf16[64,128]{1,0:T(8,128)(2,1)}, bf16[64,128]{1,0:T(8,128)(2,1)S(1)}, u32[]{:S(2)}) copy-start(bf16[64,128]{1,0:T(8,128)(2,1)S(1)} %fusion.14) | copy-start | bytes 49156
  (4 other events, 2.9 us)
where the time goes:
time: 61.9 us; the launch traced here: 61.1 us
  starting transfers between devices  28.7 us (46%)
  waiting for transfers between devices  12 us (19%)
  local copies, waits for them, and re-layouts  11.3 us (18%)
  matrix products  4.74 us (8%)
  other arithmetic  3.08 us (5%)
  between operations  1.23 us (2%)
    all_to_all x1, starting transfers between devices, per_device(): lax.all_to_all(left, 'row', split_axis=0, concat_axis=1, tiled=True)  9.8 us
    all_to_all x1, starting transfers between devices, per_device(): lax.all_to_all(right, 'row', split_axis=0, concat_axis=1, tiled=True)  7.33 us
    all_to_all x1, waiting for transfers between devices, per_device(): lax.all_to_all(tri_sum, 'row', split_axis=1, concat_axis=0, tiled=True)  6.72 us
    ppermute x2, starting transfers between devices, extended(): before = lax.ppermute(last, axis, up)  6.31 us
    all_to_all x1, waiting for transfers between devices, per_device(): lax.all_to_all(left, 'row', split_axis=0, concat_axis=1, tiled=True)  5.24 us
    unnamed x40, local copies, waits for them, and re-layouts  4.36 us
    all_to_all x1, starting transfers between devices, per_device(): lax.all_to_all(tri_sum, 'row', split_axis=1, concat_axis=0, tiled=True)  2.71 us
    ppermute x2, starting transfers between devices, extended(): after = lax.ppermute(first, axis, down)  2.58 us
  transfers between devices with their start and end apart: 7, of which 2 were waited for; matrix products, arithmetic and copies ran while one was open for 13% of the time, Pallas kernels for 0%

commit v1 on v0

--- a/solution.py
+++ b/solution.py
@@ -1,8 +1,11 @@
+import functools
 import math
 
 import jax
 import jax.numpy as jnp
 from jax import lax
+from jax.experimental import pallas as pl
+from jax.experimental.pallas import tpu as pltpu
 from jax.sharding import PartitionSpec as P
 
 QUERY_WINDOW = 32
@@ -200,6 +203,340 @@
     return (pair_out, atom_out, token_out)
 
 
+LANES = 128
+SUBLANES = 8
+SIDE = (KEYS - QUERY_WINDOW) // 2
+F32 = jnp.float32
+BF16 = jnp.bfloat16
+NT = (((1,), (1,)), ((), ()))
+TN = (((0,), (0,)), ((), ()))
+TT = (((0,), (1,)), ((), ()))
+
+
+def matmul(a, b, dims=(((1,), (0,)), ((), ()))):
+    return lax.dot_general(a, b, dims, preferred_element_type=F32)
+
+
+def normalize(values, axis):
+    average = jnp.mean(values, axis=axis, keepdims=True)
+    centred = values - average
+    spread = jnp.mean(centred * centred, axis=axis, keepdims=True)
+    return centred * lax.rsqrt(spread + EPSILON)
+
+
+def iota(shape, dim):
+    return lax.broadcasted_iota(jnp.int32, shape, dim)
+
+
+def column_of(row, size):
+    eye = iota((size, size), 0) == iota((size, size), 1)
+    return jnp.sum(jnp.where(eye, row, 0.0), axis=1, keepdims=True)
+
+
+def pad_lanes(row):
+    return jnp.concatenate([row, jnp.zeros((row.shape[0], LANES - row.shape[1]), row.dtype)], axis=1)
+
+
+def spread(got_ref, taken):
+    for b in range(taken.shape[0]):
+        taken[b] = got_ref[:, b * LANES : (b + 1) * LANES].astype(F32)
+
+
+def send_kernel(
+    n_row, pair_ref, mask_ref, in_w_ref, act_ref, cond_ref, token_ref, alive_ref, ada_w_ref, qkv_w_ref,
+    out_ref, qkv_ref, staged,
+):
+    me = lax.axis_index("row")
+    rows, cols, channels = pair_ref.shape
+    part = channels // n_row
+    width = rows * cols
+    act = act_ref[...].astype(F32)
+    ada = matmul(cond_ref[...], ada_w_ref[...])
+    wide = act.shape[1]
+    inputs = (jax.nn.sigmoid(ada[:, :wide]) * normalize(act, 1) + ada[:, wide:]).astype(BF16)
+    projected = matmul(inputs, qkv_w_ref[...]).astype(BF16)
+    qkv_ref[...] = projected
+    slab = act.shape[0]
+    keys = projected[:, wide : 2 * wide].astype(F32)
+    values = projected[:, 2 * wide :].astype(F32)
+    rims = (
+        jnp.concatenate([keys[slab - SIDE :], values[slab - SIDE :]], axis=0),
+        jnp.concatenate([keys[:SIDE], values[:SIDE]], axis=0),
+    )
+    share = 2 * SIDE // n_row
+    blocks = width // LANES
+    for d, rim in enumerate(rims):
+        for s in range(share):
+            staged[blocks, pl.ds(d * share + s, n_row, stride=SUBLANES)] = rim[s * n_row : (s + 1) * n_row]
+    tag = ((token_ref[...] - me * rows + 1) * alive_ref[...]).astype(F32)
+    tag_rows = jnp.broadcast_to(pad_lanes(tag), (n_row, LANES))
+    for s in range(2 * share, SUBLANES):
+        staged[blocks, pl.ds(s, n_row, stride=SUBLANES)] = tag_rows
+    normed = normalize(pair_ref[...].reshape(width, channels).astype(F32), 1).astype(BF16)
+    live = mask_ref[...].astype(F32)
+    lane = iota(live.shape, 1)
+    both = jnp.concatenate(
+        [live * jnp.sum(jnp.where(lane == me * rows + i, live, 0.0), axis=1, keepdims=True) for i in range(rows)],
+        axis=1,
+    )
+    for side in range(2):
+        first = 2 * side * channels
+        value = matmul(in_w_ref[:, first : first + channels], normed, TT)
+        gate = matmul(in_w_ref[:, first + channels : first + 2 * channels], normed, TT)
+        term = jax.nn.sigmoid(gate) * value * both
+        for q in range(part):
+            for b in range(blocks):
+                staged[b, pl.ds(side * part + q, n_row, stride=SUBLANES)] = term[
+                    q * n_row : (q + 1) * n_row, b * LANES : (b + 1) * LANES
+                ]
+    for b in range(blocks + 1):
+        out_ref[:, b * LANES : (b + 1) * LANES] = staged[b].astype(BF16)
+
+
+def gate_kernel(pair_ref, gate_w_ref, out_ref):
+    rows, cols, channels = pair_ref.shape
+    normed = normalize(pair_ref[...].reshape(rows * cols, channels).astype(F32), 1).astype(BF16)
+    out_ref[...] = jax.nn.sigmoid(matmul(normed, gate_w_ref[...]))
+
+
+def triangle_kernel(n_row, rows, got_ref, out_ref, taken, right_terms, staged):
+    spread(got_ref, taken)
+    cols = n_row * rows
+    part = SUBLANES // 2
+    half = SUBLANES // rows
+    per = part // half
+    for q in range(part):
+        left = jnp.concatenate(
+            [taken[i, pl.ds(q, n_row, stride=SUBLANES)] for i in range(rows)], axis=0
+        ).astype(BF16)
+        for j in range(rows):
+            right_terms[q, pl.ds(j, n_row, stride=rows)] = taken[j, pl.ds(part + q, n_row, stride=SUBLANES)]
+        summed = matmul(left, right_terms[q].astype(BF16), NT)
+        for i in range(rows):
+            staged[q % per, pl.ds((q // per) * rows + i, n_row, stride=SUBLANES)] = summed[
+                i * n_row : (i + 1) * n_row
+            ]
+    rim = taken[rows]
+    nothing = jnp.zeros((SUBLANES, LANES), F32)
+    from_before = jnp.concatenate([nothing, rim[:-SUBLANES]], axis=0)
+    from_after = jnp.concatenate([rim[SUBLANES:], nothing], axis=0)
+    share = 2 * SIDE // n_row
+    place = iota(rim.shape, 0) % SUBLANES
+    is_before = (place < share) | (place == 2 * share)
+    for k in range(per):
+        out_ref[:, k * LANES : (k + 1) * LANES] = staged[k].astype(BF16)
+    out_ref[:, per * LANES :] = jnp.where(is_before, from_before, from_after).astype(BF16)
+
+
+def finish_kernel(
+    n_row, got_ref, pair_ref, gate_ref, out_w_ref, qkv_ref, act_ref, token_ref, alive_ref, bias_w_ref,
+    attn_w_ref, ffn_in_ref, ffn_out_ref, agg_ref,
+    pair_out_ref, atom_out_ref, token_out_ref, taken, pair_new, sem,
+):
+    me = lax.axis_index("row")
+    rows, cols, channels = pair_ref.shape
+    half = SUBLANES // rows
+    per = channels // n_row // half
+    spread(got_ref, taken)
+    out_w = out_w_ref[...]
+    band_width = 3 * rows
+    band_pad = 2 * SUBLANES
+    target = (me - 1) * rows + iota((band_pad, cols), 0)
+    select = ((target == iota((band_pad, cols), 1)) & (iota((band_pad, cols), 0) < band_width)).astype(BF16)
+    bands = []
+    for i in range(rows):
+        sums = jnp.concatenate(
+            [
+                taken[k, pl.ds(h * rows + i, n_row, stride=SUBLANES)]
+                for h in range(half)
+                for k in range(per)
+            ],
+            axis=0,
+        )
+        update = matmul(normalize(sums, 0).astype(BF16), out_w, TN)
+        fresh = (pair_ref[i].astype(F32) + gate_ref[i * cols : (i + 1) * cols] * update).astype(BF16)
+        pair_new[i] = fresh
+        bands.append(matmul(select, fresh))
+    copy = pltpu.make_async_copy(pair_new, pair_out_ref, sem)
+    copy.start()
+    band_norm = normalize(jnp.concatenate(bands, axis=0), 1).astype(BF16)
+    heads = bias_w_ref.shape[0]
+    bias_rows = matmul(bias_w_ref[...], band_norm, NT).astype(BF16).astype(F32)
+    slab = act_ref.shape[0]
+    wide = act_ref.shape[1]
+    share = 2 * SIDE // n_row
+    token = token_ref[...] - me * rows
+    alive = alive_ref[...]
+    own_tag = pad_lanes(((token + 1) * alive).astype(F32))
+    before_tag = taken[per, 2 * share : 2 * share + 1]
+    after_tag = taken[per, 2 * share + 1 : 2 * share + 2]
+    flat = rows * band_pad
+    token_col = column_of(token.astype(F32), slab)
+    query_hot = (token_col == (iota((slab, flat), 1) // band_pad).astype(F32)).astype(F32)
+    rims = [
+        jnp.concatenate(
+            [taken[per, pl.ds(d * share + s, n_row, stride=SUBLANES)] for s in range(share)], axis=0
+        )
+        for d in range(2)
+    ]
+    own = qkv_ref[...].astype(F32)
+    keys_ext = jnp.concatenate([rims[0][:SIDE], own[:, wide : 2 * wide], rims[1][:SIDE]], axis=0)
+    values_ext = jnp.concatenate([rims[0][SIDE:], own[:, 2 * wide :], rims[1][SIDE:]], axis=0)
+    head_size = wide // heads
+    head_of = iota((QUERY_WINDOW, wide), 1) // head_size
+    slot = (iota((flat, KEYS), 0) % band_pad).astype(F32)
+    lane = iota((1, LANES), 1)
+    mixed = []
+    for w in range(slab // QUERY_WINDOW):
+        start = w * QUERY_WINDOW
+        before_end = SIDE - start
+        own_end = before_end + slab
+        tag = jnp.where(
+            lane < before_end,
+            pltpu.roll(before_tag, (SIDE - slab - start) % LANES, 1),
+            jnp.where(lane < own_end, pltpu.roll(own_tag, before_end % LANES, 1), pltpu.roll(after_tag, own_end % LANES, 1)),
+        )
+        offset = jnp.where(lane < before_end, 0.0, jnp.where(lane < own_end, 1.0 * rows, 2.0 * rows))
+        valid = tag > 0
+        key_slot = jnp.where(valid, tag - 1 + offset, -1.0)
+        key_hot = (slot == key_slot).astype(BF16)
+        hot = query_hot[start : start + QUERY_WINDOW]
+        hot_bias = jnp.concatenate([hot * bias_rows[h : h + 1] for h in range(heads)], axis=0).astype(BF16)
+        bias = matmul(hot_bias, key_hot)
+        query = own[start : start + QUERY_WINDOW, :wide]
+        split = jnp.concatenate([jnp.where(head_of == h, query, 0.0) for h in range(heads)], axis=0).astype(BF16)
+        scores = matmul(split, keys_ext[start : start + KEYS].astype(BF16), NT) * (1 / math.sqrt(head_size)) + bias
+        scores = jnp.where(valid, scores, -1e30)
+        powers = jnp.exp(scores - jnp.max(scores, axis=1, keepdims=True))
+        weights = (powers / jnp.sum(powers, axis=1, keepdims=True)).astype(BF16)
+        blend = matmul(weights, values_ext[start : start + KEYS].astype(BF16))
+        total = jnp.zeros((QUERY_WINDOW, wide), F32)
+        for h in range(heads):
+            total = jnp.where(head_of == h, blend[h * QUERY_WINDOW : (h + 1) * QUERY_WINDOW], total)
+        mixed.append(total)
+    attended = jnp.concatenate(mixed, axis=0).astype(BF16)
+    middle = act_ref[...].astype(F32) + matmul(attended, attn_w_ref[...])
+    expanded = matmul(normalize(middle, 1).astype(BF16), ffn_in_ref[...])
+    hidden = ffn_out_ref.shape[0]
+    inner = (jax.nn.silu(expanded[:, :hidden]) * expanded[:, hidden:]).astype(BF16)
+    alive_float = alive.astype(F32)
+    final = ((middle + matmul(inner, ffn_out_ref[...])) * column_of(alive_float, slab)).astype(BF16)
+    atom_out_ref[...] = final
+    features = jnp.maximum(matmul(final, agg_ref[...]), 0.0).astype(BF16)
+    member = jnp.where(iota((SUBLANES, slab), 0) == token, alive_float, 0.0)
+    sums = matmul(member.astype(BF16), features)
+    counts = jnp.maximum(jnp.sum(member, axis=1, keepdims=True), 1.0)
+    token_out_ref[...] = (sums / counts).astype(BF16)[:rows]
+    copy.wait()
+
+
+def whole(count):
+    return [pl.BlockSpec(memory_space=pltpu.VMEM)] * count
+
+
+def cost(flops, nbytes, exps=0):
+    return pl.CostEstimate(flops=flops, bytes_accessed=nbytes, transcendentals=exps)
+
+
+def by_kernels(
+    pair, token_mask, tri_in_weight, tri_gate_weight, tri_out_weight, atom_act, atom_cond, atom_token, atom_mask,
+    ada_weight, qkv_weight, bias_weight, attn_out_weight, ffn_in_weight, ffn_out_weight, agg_weight,
+):
+    n_row = lax.axis_size("row")
+    rows, cols, channels = pair.shape
+    slab, wide = atom_act.shape
+    width = rows * cols
+    per = channels // n_row * rows // SUBLANES
+    mask = token_mask.reshape(1, -1)
+    token = atom_token.reshape(1, -1)
+    alive = atom_mask.reshape(1, -1)
+    tile_rows = n_row * SUBLANES
+    terms, qkv = pl.pallas_call(
+        functools.partial(send_kernel, n_row),
+        out_shape=(
+            jax.ShapeDtypeStruct((tile_rows, width + LANES), BF16),
+            jax.ShapeDtypeStruct((slab, 3 * wide), BF16),
+        ),
+        in_specs=whole(9),
+        out_specs=tuple(whole(2)),
+        scratch_shapes=[pltpu.VMEM((width // LANES + 1, tile_rows, LANES), F32)],
+        cost_estimate=cost(8 * width * channels * channels, 1 << 20, 2 * width * channels),
+        name="send",
+    )(pair, mask, tri_in_weight, atom_act, atom_cond, token, alive, ada_weight, qkv_weight)
+    terms = terms.reshape(n_row, SUBLANES, width + LANES)
+    got = lax.all_to_all(terms, "row", split_axis=0, concat_axis=0, tiled=True).reshape(tile_rows, width + LANES)
+    gate = pl.pallas_call(
+        gate_kernel,
+        out_shape=jax.ShapeDtypeStruct((width, channels), F32),
+        in_specs=whole(2),
+        out_specs=whole(1)[0],
+        cost_estimate=cost(2 * width * channels * channels, 1 << 19, width * channels),
+        name="gate",
+    )(pair, tri_gate_weight)
+    out_width = per * cols + LANES
+    sums = pl.pallas_call(
+        functools.partial(triangle_kernel, n_row, rows),
+        out_shape=jax.ShapeDtypeStruct((tile_rows, out_width), BF16),
+        in_specs=whole(1),
+        out_specs=whole(1)[0],
+        scratch_shapes=[
+            pltpu.VMEM((rows + 1, tile_rows, LANES), F32),
+            pltpu.VMEM((channels // n_row, cols, cols), F32),
+            pltpu.VMEM((per, tile_rows, LANES), F32),
+        ],
+        cost_estimate=cost(2 * width * width, 1 << 19),
+        name="triangle",
+    )(got)
+    sums = sums.reshape(n_row, SUBLANES, out_width)
+    back = lax.all_to_all(sums, "row", split_axis=0, concat_axis=0, tiled=True).reshape(tile_rows, out_width)
+    return pl.pallas_call(
+        functools.partial(finish_kernel, n_row),
+        out_shape=(
+            jax.ShapeDtypeStruct(pair.shape, BF16),
+            jax.ShapeDtypeStruct(atom_act.shape, BF16),
+            jax.ShapeDtypeStruct((rows, agg_weight.shape[1]), BF16),
+        ),
+        in_specs=whole(13),
+        out_specs=(pl.BlockSpec(memory_space=pl.ANY), *whole(2)),
+        scratch_shapes=[
+            pltpu.VMEM((per + 1, tile_rows, LANES), F32),
+            pltpu.VMEM(pair.shape, BF16),
+            pltpu.SemaphoreType.DMA,
+        ],
+        cost_estimate=cost(4 * width * channels * channels, 1 << 20),
+        name="finish",
+    )(
+        back, pair, gate, tri_out_weight, qkv, atom_act, token, alive, bias_weight.T, attn_out_weight,
+        ffn_in_weight, ffn_out_weight, agg_weight,
+    )
+
+
+def kernels_fit(mesh, args):
+    pair, atom_act, bias_weight = args[0], args[5], args[11]
+    n_row = mesh.shape["row"]
+    n_group = mesh.shape["groups"]
+    cols, channels = pair.shape[1:]
+    rows = pair.shape[0] // (n_group * n_row)
+    slab = atom_act.shape[0] // (n_group * n_row)
+    wide = atom_act.shape[1]
+    share = 2 * SIDE // n_row
+    return (
+        mesh.shape["col"] == 1
+        and cols == LANES
+        and channels == LANES
+        and wide == LANES
+        and rows * 2 == SUBLANES
+        and 2 * channels == n_row * SUBLANES
+        and 2 * SIDE == share * n_row
+        and 2 * share + 2 == SUBLANES
+        and SIDE <= slab <= LANES
+        and slab % QUERY_WINDOW == 0
+        and slab + 2 * SIDE - KEYS == slab - QUERY_WINDOW
+        and QUERY_WINDOW % (2 * SUBLANES) == 0
+        and wide % bias_weight.shape[1] == 0
+    )
+
+
 def solution(mesh):
     in_specs = (
         P(("groups", "row"), "col", None),
@@ -224,6 +561,9 @@
         P(("groups", "row"), None),
         P(("groups", "row"), None),
     )
-    return jax.shard_map(
-        per_device, mesh=mesh, in_specs=in_specs, out_specs=out_specs, check_vma=False
-    )
+
+    def layer(*args):
+        body = by_kernels if kernels_fit(mesh, args) else per_device
+        return jax.shard_map(body, mesh=mesh, in_specs=in_specs, out_specs=out_specs, check_vma=False)(*args)
+
+    return layer

time: 61.9 us -> 41.2 us (0.67)
  starting transfers between devices: 28.7 us -> 2.58 us
  blocking collectives: 0 us -> 19.5 us
  local copies, waits for them, and re-layouts: 11.3 us -> 0.67 us
  Pallas kernels: 0 us -> 10.5 us
  waiting for transfers between devices: 12 us -> 6.99 us
  matrix products: 4.74 us -> 0 us
  other arithmetic: 3.08 us -> 0 us
    all_to_all x0 -> x1, blocking collectives: none -> 19.5 us  [by_kernels(): lax.all_to_all(terms, 'row', split_axis=0, concat_axis=0, tiled=True)]
    all_to_all x3 -> x1, starting transfers between devices: 19.8 us -> 2.58 us  [by_kernels(): lax.all_to_all(sums, 'row', split_axis=0, concat_axis=0, tiled=True)]
    pallas_call x0 -> x4, Pallas kernels: none -> 10.5 us  [the longest x1 4.19 us: by_kernels(): pl.pallas_call(functools.partial(finish_kernel, n_row), out_shape=(jax.Sh...]
    ppermute x4 -> x0, starting transfers between devices: 8.9 us -> none  [the longest x2 6.31 us: extended(): before = lax.ppermute(last, axis, up)]
    all_to_all x3 -> x1, waiting for transfers between devices: 12 us -> 6.99 us  [by_kernels(): lax.all_to_all(sums, 'row', split_axis=0, concat_axis=0, tiled=True)]
    dot_general x17 -> x0, matrix products: 4.74 us -> none  [the longest x1 0.85 us: per_device(): jnp.einsum('at,ac->tc', live_onehot, features, preferred_element_type=jnp...]
    gather x3 -> x0, local copies, waits for them, and re-layouts: 3.84 us -> none  [the longest x1 1.88 us: per_device(): window_valid = key_valid[key_index]]
    unnamed x40 -> x2, local copies, waits for them, and re-layouts: 4.36 us -> 0.67 us
  transfers between devices with their start and end apart: 7 -> 1, of which waited for: 2 -> 1; matrix products, arithmetic and copies ran while one was open for 13% -> 0% of each run, Pallas kernels for 0% -> 5%
where the time goes in v1:
time: 41.2 us; the launch traced here: 40.9 us
  blocking collectives  19.5 us (47%)
  Pallas kernels  10.5 us (25%)
  waiting for transfers between devices  6.99 us (17%)
  starting transfers between devices  2.58 us (6%)
  local copies, waits for them, and re-layouts  0.67 us (2%)
  between operations  0.64 us (2%)
    all_to_all x1, blocking collectives, by_kernels(): lax.all_to_all(terms, 'row', split_axis=0, concat_axis=0, tiled=True)  19.5 us
    all_to_all x1, waiting for transfers between devices, by_kernels(): lax.all_to_all(sums, 'row', split_axis=0, concat_axis=0, tiled=True)  6.99 us
    pallas_call x1, Pallas kernels, by_kernels(): pl.pallas_call(functools.partial(finish_kernel, n_row), out_shape=(jax.Sh...  4.19 us
    all_to_all x1, starting transfers between devices, by_kernels(): lax.all_to_all(sums, 'row', split_axis=0, concat_axis=0, tiled=True)  2.58 us
    pallas_call x1, Pallas kernels, by_kernels(): pl.pallas_call(functools.partial(send_kernel, n_row), out_shape=(jax.Shap...  2.43 us
    pallas_call x1, Pallas kernels, by_kernels(): pl.pallas_call(gate_kernel, out_shape=jax.ShapeDtypeStruct((width, channe...  1.96 us
    pallas_call x1, Pallas kernels, by_kernels(): pl.pallas_call(functools.partial(triangle_kernel, n_row, rows), out_shape...  1.93 us
  transfers between devices with their start and end apart: 1, of which 1 were waited for; matrix products, arithmetic and copies ran while one was open for 0% of the time, Pallas kernels for 5%

profile of v1, /device:TPU:0, one launch (start us, length us, event | category | flops | bytes accessed | tf_op | source)
XLA Modules:
  0.0 40.9 jit_solution(5226087512486627735)
XLA Ops:
  0.6 2.4 %send.1 = (bf16[256,640]{1,0:T(8,128)(2,1)}, bf16[64,384]{1,0:T(8,128)(2,1)}) custom-call(bf16[4,128,128]{2,1,0:T(8,128)(2,1)} %pair_ref.5, s32[1,128]{1,0:T(1,128)} %bitcast.17, bf16[128,512]{1,0:T(8,128)(2,1)} %in_w_ref.1, bf16[64,128]{1,0:T(8,128)(2,1)} %act_ref.3, bf16[64,128]{1,0:T(8,128)(2,1)} %cond_ref.1, s32[1,64]{1,0:T(1,128)} %bitcast.12, ...), custom_call_target="tpu_custom_call" | custom-call | flops 67108864 | bytes 1048576 | tf_op jit(solution)/shard_map/send/pallas_call | solution.py:454
  3.1 19.5 %all_to_all.10 = bf16[32,8,640]{2,1,0:T(8,128)(2,1)} all-to-all(bf16[32,8,640]{2,1,0:T(8,128)(2,1)} %bitcast.11), channel_id=1, replica_groups=mesh['groups'=1,'row'=32,'col'=1] {'row'}, dimensions={0} | all-to-all | bytes 655360 | tf_op jit(solution)/shard_map/all_to_all | solution.py:467
  22.5 1.9 %triangle.1 = bf16[256,384]{1,0:T(8,128)(2,1)} custom-call(bf16[256,640]{1,0:T(8,128)(2,1)} %bitcast.8), custom_call_target="tpu_custom_call" | custom-call | flops 524288 | bytes 524288 | tf_op jit(solution)/shard_map/triangle/pallas_call | solution.py:477
  24.5 2.6 %all-to-all-start.1 = ((bf16[32,8,384]{2,1,0:T(8,128)(2,1)}), bf16[32,8,384]{2,1,0:T(8,128)(2,1)S(1)}, u32[]{:S(2)}, u32[]{:S(2)}) async-start(bf16[32,8,384]{2,1,0:T(8,128)(2,1)} %bitcast.9), calls=%async_computation.1 | async-start | bytes 393216 | tf_op jit(solution)/shard_map/all_to_all | solution.py:491
  27.1 2.0 %gate.1.gate_ref = f32[512,128]{1,0:T(8,128)} custom-call(bf16[4,128,128]{2,1,0:T(8,128)(2,1)} %pair_ref.5, bf16[128,128]{1,0:T(8,128)(2,1)} %gate_w_ref.1), custom_call_target="tpu_custom_call" | custom-call | flops 16777216 | bytes 524288 | tf_op jit(solution)/shard_map/gate/pallas_call | solution.py:468
  29.0 7.0 %all-to-all-done.1 = bf16[32,8,384]{2,1,0:T(8,128)(2,1)S(1)} async-done(((bf16[32,8,384]{2,1,0:T(8,128)(2,1)}), bf16[32,8,384]{2,1,0:T(8,128)(2,1)S(1)}, u32[]{:S(2)}, u32[]{:S(2)}) %all-to-all-start.1) | async-done | bytes 196640 | tf_op jit(solution)/shard_map/all_to_all | solution.py:491
  36.0 0.0 copy-start
  36.0 0.7 %copy-done = bf16[32,8,384]{2,1,0:T(8,128)(2,1)} copy-done((bf16[32,8,384]{2,1,0:T(8,128)(2,1)}, bf16[32,8,384]{2,1,0:T(8,128)(2,1)S(1)}, u32[]{:S(2)}) %copy-start) | copy-done | bytes 196632
  36.7 4.2 %finish.1 = (bf16[4,128,128]{2,1,0:T(8,128)(2,1)}, bf16[64,128]{1,0:T(8,128)(2,1)}, bf16[4,384]{1,0:T(4,128)(2,1)}) custom-call(bf16[256,384]{1,0:T(8,128)(2,1)} %bitcast.10, bf16[4,128,128]{2,1,0:T(8,128)(2,1)} %pair_ref.5, f32[512,128]{1,0:T(8,128)} %gate.1.gate_ref, bf16[128,128]{1,0:T(8,128)(2,1)} %out_w_ref.1, ...), custom_call_target="tpu_custom_call" | custom-call | flops 33554432 | bytes 1048576 | tf_op jit(solution)/shard_map/finish/pallas_call | solution.py:492
Async XLA Ops:
  24.5 11.5 %all-to-all-start.1 = ((bf16[32,8,384]{2,1,0:T(8,128)(2,1)}), bf16[32,8,384]{2,1,0:T(8,128)(2,1)S(1)}, u32[]{:S(2)}, u32[]{:S(2)}) async-start(bf16[32,8,384]{2,1,0:T(8,128)(2,1)} %bitcast.9), calls=%async_computation.1 | async-start | bytes 393216 | tf_op jit(solution)/shard_map/all_to_all | solution.py:491
  36.0 0.7 %copy-start = (bf16[32,8,384]{2,1,0:T(8,128)(2,1)}, bf16[32,8,384]{2,1,0:T(8,128)(2,1)S(1)}, u32[]{:S(2)}) copy-start(bf16[32,8,384]{2,1,0:T(8,128)(2,1)S(1)} %all-to-all-done.1) | copy-start | bytes 589828

commit v2 on v1

--- a/solution.py
+++ b/solution.py
@@ -206,6 +206,7 @@
 LANES = 128
 SUBLANES = 8
 SIDE = (KEYS - QUERY_WINDOW) // 2
+LIMIT = pltpu.CompilerParams(vmem_limit_bytes=8 << 20)
 F32 = jnp.float32
 BF16 = jnp.bfloat16
 NT = (((1,), (1,)), ((), ()))
@@ -243,9 +244,17 @@
 
 
 def send_kernel(
-    n_row, pair_ref, mask_ref, in_w_ref, act_ref, cond_ref, token_ref, alive_ref, ada_w_ref, qkv_w_ref,
-    out_ref, qkv_ref, staged,
+    n_row, pair_hbm, in_w_hbm, cond_hbm, act_hbm, ada_w_hbm, qkv_w_hbm, mask_hbm, token_hbm, alive_hbm,
+    out_ref, qkv_ref,
+    pair_ref, in_w_ref, cond_ref, act_ref, ada_w_ref, qkv_w_ref, mask_ref, token_ref, alive_ref, staged, sems,
 ):
+    sources = (pair_hbm, cond_hbm, ada_w_hbm, act_hbm, qkv_w_hbm, in_w_hbm, mask_hbm, token_hbm, alive_hbm)
+    places = (pair_ref, cond_ref, ada_w_ref, act_ref, qkv_w_ref, in_w_ref, mask_ref, token_ref, alive_ref)
+    loads = [pltpu.make_async_copy(a, b, sems.at[i]) for i, (a, b) in enumerate(zip(sources, places))]
+    for load in loads:
+        load.start()
+    for load in loads:
+        load.wait()
     me = lax.axis_index("row")
     rows, cols, channels = pair_ref.shape
     part = channels // n_row
@@ -293,8 +302,21 @@
         out_ref[:, b * LANES : (b + 1) * LANES] = staged[b].astype(BF16)
 
 
-def gate_kernel(pair_ref, gate_w_ref, out_ref):
+def prepare_kernel(
+    band_pad, pair_ref, gate_w_ref, token_ref, alive_ref, bias_w_ref,
+    out_ref, tag_ref, query_hot_ref, live_ref, member_ref, bias_ref,
+):
     rows, cols, channels = pair_ref.shape
+    slab = token_ref.shape[1]
+    token = token_ref[...] - lax.axis_index("row") * rows
+    alive = alive_ref[...]
+    alive_float = alive.astype(F32)
+    tag_ref[...] = jnp.broadcast_to(pad_lanes(((token + 1) * alive).astype(F32)), tag_ref.shape)
+    token_col = column_of(token.astype(F32), slab)
+    query_hot_ref[...] = (token_col == (iota(query_hot_ref.shape, 1) // band_pad).astype(F32)).astype(F32)
+    live_ref[...] = jnp.broadcast_to(column_of(alive_float, slab), live_ref.shape)
+    member_ref[...] = jnp.where(iota(member_ref.shape, 0) == token, alive_float, 0.0)
+    bias_ref[...] = bias_w_ref[...]
     normed = normalize(pair_ref[...].reshape(rows * cols, channels).astype(F32), 1).astype(BF16)
     out_ref[...] = jax.nn.sigmoid(matmul(normed, gate_w_ref[...]))
 
@@ -329,8 +351,8 @@
 
 
 def finish_kernel(
-    n_row, got_ref, pair_ref, gate_ref, out_w_ref, qkv_ref, act_ref, token_ref, alive_ref, bias_w_ref,
-    attn_w_ref, ffn_in_ref, ffn_out_ref, agg_ref,
+    n_row, got_ref, pair_ref, gate_ref, out_w_ref, qkv_ref, act_ref, tag_ref, query_hot_ref, live_ref, member_ref,
+    bias_w_ref, attn_w_ref, ffn_in_ref, ffn_out_ref, agg_ref,
     pair_out_ref, atom_out_ref, token_out_ref, taken, pair_new, sem,
 ):
     me = lax.axis_index("row")
@@ -365,14 +387,11 @@
     slab = act_ref.shape[0]
     wide = act_ref.shape[1]
     share = 2 * SIDE // n_row
-    token = token_ref[...] - me * rows
-    alive = alive_ref[...]
-    own_tag = pad_lanes(((token + 1) * alive).astype(F32))
+    own_tag = tag_ref[:1]
     before_tag = taken[per, 2 * share : 2 * share + 1]
     after_tag = taken[per, 2 * share + 1 : 2 * share + 2]
     flat = rows * band_pad
-    token_col = column_of(token.astype(F32), slab)
-    query_hot = (token_col == (iota((slab, flat), 1) // band_pad).astype(F32)).astype(F32)
+    query_hot = query_hot_ref[...]
     rims = [
         jnp.concatenate(
             [taken[per, pl.ds(d * share + s, n_row, stride=SUBLANES)] for s in range(share)], axis=0
@@ -419,11 +438,10 @@
     expanded = matmul(normalize(middle, 1).astype(BF16), ffn_in_ref[...])
     hidden = ffn_out_ref.shape[0]
     inner = (jax.nn.silu(expanded[:, :hidden]) * expanded[:, hidden:]).astype(BF16)
-    alive_float = alive.astype(F32)
-    final = ((middle + matmul(inner, ffn_out_ref[...])) * column_of(alive_float, slab)).astype(BF16)
+    final = ((middle + matmul(inner, ffn_out_ref[...])) * live_ref[...]).astype(BF16)
     atom_out_ref[...] = final
     features = jnp.maximum(matmul(final, agg_ref[...]), 0.0).astype(BF16)
-    member = jnp.where(iota((SUBLANES, slab), 0) == token, alive_float, 0.0)
+    member = member_ref[...]
     sums = matmul(member.astype(BF16), features)
     counts = jnp.maximum(jnp.sum(member, axis=1, keepdims=True), 1.0)
     token_out_ref[...] = (sums / counts).astype(BF16)[:rows]
@@ -451,28 +469,44 @@
     token = atom_token.reshape(1, -1)
     alive = atom_mask.reshape(1, -1)
     tile_rows = n_row * SUBLANES
+    sources = (pair, tri_in_weight, atom_cond, atom_act, ada_weight, qkv_weight, mask, token, alive)
     terms, qkv = pl.pallas_call(
         functools.partial(send_kernel, n_row),
         out_shape=(
             jax.ShapeDtypeStruct((tile_rows, width + LANES), BF16),
             jax.ShapeDtypeStruct((slab, 3 * wide), BF16),
         ),
-        in_specs=whole(9),
+        in_specs=[pl.BlockSpec(memory_space=pltpu.HBM)] * len(sources),
         out_specs=tuple(whole(2)),
-        scratch_shapes=[pltpu.VMEM((width // LANES + 1, tile_rows, LANES), F32)],
+        scratch_shapes=[
+            *(pltpu.VMEM(a.shape, a.dtype) for a in sources),
+            pltpu.VMEM((width // LANES + 1, tile_rows, LANES), F32),
+            pltpu.SemaphoreType.DMA((len(sources),)),
+        ],
         cost_estimate=cost(8 * width * channels * channels, 1 << 20, 2 * width * channels),
+        compiler_params=LIMIT,
         name="send",
-    )(pair, mask, tri_in_weight, atom_act, atom_cond, token, alive, ada_weight, qkv_weight)
+    )(*(pltpu.with_memory_space_constraint(a, pltpu.HBM) for a in sources))
     terms = terms.reshape(n_row, SUBLANES, width + LANES)
     got = lax.all_to_all(terms, "row", split_axis=0, concat_axis=0, tiled=True).reshape(tile_rows, width + LANES)
-    gate = pl.pallas_call(
-        gate_kernel,
-        out_shape=jax.ShapeDtypeStruct((width, channels), F32),
-        in_specs=whole(2),
-        out_specs=whole(1)[0],
+    band_pad = 2 * SUBLANES
+    prepared = pl.pallas_call(
+        functools.partial(prepare_kernel, band_pad),
+        out_shape=(
+            jax.ShapeDtypeStruct((width, channels), F32),
+            jax.ShapeDtypeStruct((SUBLANES, LANES), F32),
+            jax.ShapeDtypeStruct((slab, rows * band_pad), F32),
+            jax.ShapeDtypeStruct((slab, wide), F32),
+            jax.ShapeDtypeStruct((SUBLANES, slab), F32),
+            jax.ShapeDtypeStruct(bias_weight.shape[::-1], BF16),
+        ),
+        in_specs=whole(5),
+        out_specs=tuple(whole(6)),
         cost_estimate=cost(2 * width * channels * channels, 1 << 19, width * channels),
-        name="gate",
-    )(pair, tri_gate_weight)
+        compiler_params=LIMIT,
+        name="prepare",
+    )(pair, tri_gate_weight, token, alive, bias_weight.T)
+    gate, *tables = prepared
     out_width = per * cols + LANES
     sums = pl.pallas_call(
         functools.partial(triangle_kernel, n_row, rows),
@@ -485,6 +519,7 @@
             pltpu.VMEM((per, tile_rows, LANES), F32),
         ],
         cost_estimate=cost(2 * width * width, 1 << 19),
+        compiler_params=LIMIT,
         name="triangle",
     )(got)
     sums = sums.reshape(n_row, SUBLANES, out_width)
@@ -496,7 +531,7 @@
             jax.ShapeDtypeStruct(atom_act.shape, BF16),
             jax.ShapeDtypeStruct((rows, agg_weight.shape[1]), BF16),
         ),
-        in_specs=whole(13),
+        in_specs=whole(15),
         out_specs=(pl.BlockSpec(memory_space=pl.ANY), *whole(2)),
         scratch_shapes=[
             pltpu.VMEM((per + 1, tile_rows, LANES), F32),
@@ -504,10 +539,11 @@
             pltpu.SemaphoreType.DMA,
         ],
         cost_estimate=cost(4 * width * channels * channels, 1 << 20),
+        compiler_params=LIMIT,
         name="finish",
     )(
-        back, pair, gate, tri_out_weight, qkv, atom_act, token, alive, bias_weight.T, attn_out_weight,
-        ffn_in_weight, ffn_out_weight, agg_weight,
+        back, pair, gate, tri_out_weight, qkv, atom_act, *tables, attn_out_weight, ffn_in_weight, ffn_out_weight,
+        agg_weight,
     )
 
 

time: 41.2 us -> 37.8 us (0.917)
  Pallas kernels: 10.5 us -> 6.29 us
  waiting for transfers between devices: 6.99 us -> 8.5 us
  local copies, waits for them, and re-layouts: 0.67 us -> 0.06 us
    pallas_call x1, Pallas kernels: 1.96 us -> 0.36 us  [by_kernels(): pl.pallas_call(functools.partial(prepare_kernel, band_pad), out_shape=(ja...]
    all_to_all x1, waiting for transfers between devices: 6.99 us -> 8.5 us  [by_kernels(): lax.all_to_all(sums, 'row', split_axis=0, concat_axis=0, tiled=True)]
    pallas_call x1, Pallas kernels: 4.19 us -> 3.22 us  [by_kernels(): pl.pallas_call(functools.partial(finish_kernel, n_row), out_shape=(jax.Sh...]
    pallas_call x1, Pallas kernels: 1.93 us -> 0.97 us  [by_kernels(): pl.pallas_call(functools.partial(triangle_kernel, n_row, rows), out_shape...]
    pallas_call x1, Pallas kernels: 2.43 us -> 1.74 us  [by_kernels(): pl.pallas_call(functools.partial(send_kernel, n_row), out_shape=(jax.Shap...]
    unnamed x2 -> x22, local copies, waits for them, and re-layouts: 0.67 us -> 0.06 us
  transfers between devices with their start and end apart: 1 -> 1, of which waited for: 1 -> 1; matrix products, arithmetic and copies ran while one was open for 0% -> 0% of each run, Pallas kernels for 5% -> 1%
where the time goes in v2:
time: 37.8 us; the launch traced here: 37.5 us
  blocking collectives  19.2 us (51%)
  waiting for transfers between devices  8.5 us (22%)
  Pallas kernels  6.29 us (17%)
  starting transfers between devices  2.73 us (7%)
  between operations  0.78 us (2%)
    all_to_all x1, blocking collectives, by_kernels(): lax.all_to_all(terms, 'row', split_axis=0, concat_axis=0, tiled=True)  19.2 us
    all_to_all x1, waiting for transfers between devices, by_kernels(): lax.all_to_all(sums, 'row', split_axis=0, concat_axis=0, tiled=True)  8.5 us
    pallas_call x1, Pallas kernels, by_kernels(): pl.pallas_call(functools.partial(finish_kernel, n_row), out_shape=(jax.Sh...  3.22 us
    all_to_all x1, starting transfers between devices, by_kernels(): lax.all_to_all(sums, 'row', split_axis=0, concat_axis=0, tiled=True)  2.73 us
    pallas_call x1, Pallas kernels, by_kernels(): pl.pallas_call(functools.partial(send_kernel, n_row), out_shape=(jax.Shap...  1.74 us
    pallas_call x1, Pallas kernels, by_kernels(): pl.pallas_call(functools.partial(triangle_kernel, n_row, rows), out_shape...  0.97 us
  transfers between devices with their start and end apart: 1, of which 1 were waited for; matrix products, arithmetic and copies ran while one was open for 0% of the time, Pallas kernels for 1%

profile of v2, /device:TPU:0, one launch (start us, length us, event | category | flops | bytes accessed | tf_op | source)
XLA Modules:
  0.0 37.5 jit_solution(17991714372990873905)
XLA Ops:
  0.6 1.7 %send.1 = (bf16[256,640]{1,0:T(8,128)(2,1)S(1)}, bf16[64,384]{1,0:T(8,128)(2,1)S(1)}) custom-call(bf16[4,128,128]{2,1,0:T(8,128)(2,1)} %pair_ref.3, bf16[128,512]{1,0:T(8,128)(2,1)} %in_w_hbm.1, bf16[64,128]{1,0:T(8,128)(2,1)} %cond_hbm.1, bf16[64,128]{1,0:T(8,128)(2,1)} %act_ref.1, bf16[128,256]{1,0:T(8,128)(2,1)} %ada_w_hbm.1, bf16[128,384]{1,0:T(8,128)(2,1)} %qkv_w_hbm.1, ...), custom_call_target="tpu_custom_call" | custom-call | flops 67108864 | bytes 1048576 | tf_op jit(solution)/shard_map/send/pallas_call | solution.py:473
  2.4 19.2 %all_to_all.10 = bf16[32,8,640]{2,1,0:T(8,128)(2,1)S(1)} all-to-all(bf16[32,8,640]{2,1,0:T(8,128)(2,1)S(1)} %bitcast.10), channel_id=1, replica_groups=mesh['groups'=1,'row'=32,'col'=1] {'row'}, dimensions={0} | all-to-all | bytes 655360 | tf_op jit(solution)/shard_map/all_to_all | solution.py:491
  21.6 1.0 %triangle.1 = bf16[256,384]{1,0:T(8,128)(2,1)} custom-call(bf16[256,640]{1,0:T(8,128)(2,1)S(1)} %bitcast.8), custom_call_target="tpu_custom_call" | custom-call | flops 524288 | bytes 524288 | tf_op jit(solution)/shard_map/triangle/pallas_call | solution.py:511
  22.5 0.0 copy-start.10
  22.6 0.0 copy-start.2
  22.6 0.0 copy-start.4
  22.6 0.0 copy-start.6
  22.6 2.7 %all-to-all-start.1 = ((bf16[32,8,384]{2,1,0:T(8,128)(2,1)}), bf16[32,8,384]{2,1,0:T(8,128)(2,1)S(1)}, u32[]{:S(2)}, u32[]{:S(2)}) async-start(bf16[32,8,384]{2,1,0:T(8,128)(2,1)} %bitcast.5), calls=%async_computation.1 | async-start | bytes 393216 | tf_op jit(solution)/shard_map/all_to_all | solution.py:526
  25.3 0.0 copy-start.1
  25.3 0.0 copy-done
  25.3 0.0 copy-done.7
  25.4 0.0 copy-done.8
  25.4 0.0 copy-done.9
  25.4 0.0 copy-done.10
  25.4 0.0 copy-start.3
  25.4 0.0 copy-start.5
  25.4 0.4 prepare.1
  25.8 8.5 %all-to-all-done.1 = bf16[32,8,384]{2,1,0:T(8,128)(2,1)S(1)} async-done(((bf16[32,8,384]{2,1,0:T(8,128)(2,1)}), bf16[32,8,384]{2,1,0:T(8,128)(2,1)S(1)}, u32[]{:S(2)}, u32[]{:S(2)}) %all-to-all-start.1) | async-done | bytes 196640 | tf_op jit(solution)/shard_map/all_to_all | solution.py:526
  34.3 0.0 copy-done.2
  34.3 0.0 copy-done.4
  34.3 0.0 copy-done.6
  34.3 0.0 copy-done.1
  34.3 0.0 copy-done.3
  34.3 3.2 %finish.1 = (bf16[4,128,128]{2,1,0:T(8,128)(2,1)}, bf16[64,128]{1,0:T(8,128)(2,1)}, bf16[4,384]{1,0:T(4,128)(2,1)}) custom-call(bf16[256,384]{1,0:T(8,128)(2,1)S(1)} %bitcast.9, bf16[4,128,128]{2,1,0:T(8,128)(2,1)S(1)} %copy-done, f32[512,128]{1,0:T(8,128)S(1)} %get-tuple-element.12.gate_ref, bf16[128,128]{1,0:T(8,128)(2,1)S(1)} %copy-done.5, ...), custom_call_target="tpu_custom_call" | custom-call | flops 33554432 | bytes 1048576 | tf_op jit(solution)/shard_map/finish/pallas_call | solution.py:527
  (5 shorter events, 0.0 us)
Async XLA Ops:
  22.5 2.8 %copy-start = (bf16[4,128,128]{2,1,0:T(8,128)(2,1)S(1)}, bf16[4,128,128]{2,1,0:T(8,128)(2,1)}, u32[]{:S(2)}) copy-start(bf16[4,128,128]{2,1,0:T(8,128)(2,1)} %pair_ref.3) | copy-start | bytes 393220
  22.5 2.8 %copy-start.7 = (bf16[128,128]{1,0:T(8,128)(2,1)S(1)}, bf16[128,128]{1,0:T(8,128)(2,1)}, u32[]{:S(2)}) copy-start(bf16[128,128]{1,0:T(8,128)(2,1)} %gate_w_ref.1) | copy-start | bytes 98308
  22.5 2.8 %copy-start.8 = (s32[64]{0:T(128)S(1)}, s32[64]{0:T(128)}, u32[]{:S(2)}) copy-start(s32[64]{0:T(128)} %param.23) | copy-start | bytes 772
  22.5 2.8 %copy-start.9 = (s32[64]{0:T(128)S(1)}, s32[64]{0:T(128)}, u32[]{:S(2)}) copy-start(s32[64]{0:T(128)} %param.24) | copy-start | bytes 772
  22.5 2.8 %copy-start.10 = (bf16[128,4]{0,1:T(4,128)(2,1)S(1)}, bf16[128,4]{0,1:T(4,128)(2,1)}, u32[]{:S(2)}) copy-start(bf16[128,4]{0,1:T(4,128)(2,1)} %param.27) | copy-start | bytes 3076
  22.6 11.7 %copy-start.2 = (bf16[128,384]{1,0:T(8,128)(2,1)S(1)}, bf16[128,384]{1,0:T(8,128)(2,1)}, u32[]{:S(2)}) copy-start(bf16[128,384]{1,0:T(8,128)(2,1)} %agg_ref.1) | copy-start | bytes 294916
  22.6 11.7 %copy-start.4 = (bf16[256,128]{1,0:T(8,128)(2,1)S(1)}, bf16[256,128]{1,0:T(8,128)(2,1)}, u32[]{:S(2)}) copy-start(bf16[256,128]{1,0:T(8,128)(2,1)} %ffn_out_ref.1) | copy-start | bytes 196612
  22.6 11.7 %copy-start.6 = (bf16[128,128]{1,0:T(8,128)(2,1)S(1)}, bf16[128,128]{1,0:T(8,128)(2,1)}, u32[]{:S(2)}) copy-start(bf16[128,128]{1,0:T(8,128)(2,1)} %attn_w_ref.1) | copy-start | bytes 98308
  22.6 11.7 %all-to-all-start.1 = ((bf16[32,8,384]{2,1,0:T(8,128)(2,1)}), bf16[32,8,384]{2,1,0:T(8,128)(2,1)S(1)}, u32[]{:S(2)}, u32[]{:S(2)}) async-start(bf16[32,8,384]{2,1,0:T(8,128)(2,1)} %bitcast.5), calls=%async_computation.1 | async-start | bytes 393216 | tf_op jit(solution)/shard_map/all_to_all | solution.py:526
  25.3 9.0 %copy-start.1 = (bf16[128,512]{1,0:T(8,128)(2,1)S(1)}, bf16[128,512]{1,0:T(8,128)(2,1)}, u32[]{:S(2)}) copy-start(bf16[128,512]{1,0:T(8,128)(2,1)} %ffn_in_ref.1) | copy-start | bytes 393220
  25.4 8.9 %copy-start.3 = (bf16[64,128]{1,0:T(8,128)(2,1)S(1)}, bf16[64,128]{1,0:T(8,128)(2,1)}, u32[]{:S(2)}) copy-start(bf16[64,128]{1,0:T(8,128)(2,1)} %act_ref.1) | copy-start | bytes 49156
  25.4 8.9 %copy-start.5 = (bf16[128,128]{1,0:T(8,128)(2,1)S(1)}, bf16[128,128]{1,0:T(8,128)(2,1)}, u32[]{:S(2)}) copy-start(bf16[128,128]{1,0:T(8,128)(2,1)} %out_w_ref.1) | copy-start | bytes 98308

commit v3 on v0

--- a/solution.py
+++ b/solution.py
@@ -1,8 +1,11 @@
+import functools
 import math
 
 import jax
 import jax.numpy as jnp
 from jax import lax
+from jax.experimental import pallas as pl
+from jax.experimental.pallas import tpu as pltpu
 from jax.sharding import PartitionSpec as P
 
 QUERY_WINDOW = 32
@@ -200,6 +203,400 @@
     return (pair_out, atom_out, token_out)
 
 
+LANES = 128
+SUBLANES = 8
+SIDE = (KEYS - QUERY_WINDOW) // 2
+RIM_ROWS = 4
+BAND_PAD = 2 * SUBLANES
+LIMIT = pltpu.CompilerParams(vmem_limit_bytes=8 << 20)
+F32 = jnp.float32
+BF16 = jnp.bfloat16
+NT = (((1,), (1,)), ((), ()))
+TN = (((0,), (0,)), ((), ()))
+TT = (((0,), (1,)), ((), ()))
+
+
+def matmul(a, b, dims=(((1,), (0,)), ((), ()))):
+    return lax.dot_general(a, b, dims, preferred_element_type=F32)
+
+
+def normalize(values, axis):
+    average = jnp.mean(values, axis=axis, keepdims=True)
+    centred = values - average
+    spread = jnp.mean(centred * centred, axis=axis, keepdims=True)
+    return centred * lax.rsqrt(spread + EPSILON)
+
+
+def iota(shape, dim):
+    return lax.broadcasted_iota(jnp.int32, shape, dim)
+
+
+def column_of(row, size):
+    eye = iota((size, size), 0) == iota((size, size), 1)
+    return jnp.sum(jnp.where(eye, row, 0.0), axis=1, keepdims=True)
+
+
+def pad_lanes(row):
+    return jnp.concatenate([row, jnp.zeros((row.shape[0], LANES - row.shape[1]), row.dtype)], axis=1)
+
+
+def strided(first, count, step):
+    return pl.ds(first, count, stride=step)
+
+
+def send_kernel(
+    n_row, pair_hbm, act_hbm, bias_w_hbm, in_w_hbm, cond_hbm, ada_w_hbm, mask_hbm, token_hbm, alive_hbm,
+    pair_ref, act_ref, bias_w_ref, out_ref, inputs_ref, slots_ref,
+    in_w_ref, cond_ref, ada_w_ref, mask_ref, token_ref, alive_ref, staged, sems,
+):
+    sources = (pair_hbm, cond_hbm, ada_w_hbm, act_hbm, in_w_hbm, mask_hbm, token_hbm, alive_hbm, bias_w_hbm)
+    places = (pair_ref, cond_ref, ada_w_ref, act_ref, in_w_ref, mask_ref, token_ref, alive_ref, bias_w_ref)
+    loads = [pltpu.make_async_copy(a, b, sems.at[i]) for i, (a, b) in enumerate(zip(sources, places))]
+    for load in loads:
+        load.start()
+    for load in loads:
+        load.wait()
+    me = lax.axis_index("row")
+    rows, cols, channels = pair_ref.shape
+    part = channels // n_row
+    width = rows * cols
+    step = 2 * part * rows + RIM_ROWS
+    normed = normalize(pair_ref[...].reshape(width, channels).astype(F32), 1).astype(BF16)
+    live = mask_ref[...].astype(F32)
+    lane = iota(live.shape, 1)
+    both = jnp.concatenate(
+        [live * jnp.sum(jnp.where(lane == me * rows + i, live, 0.0), axis=1, keepdims=True) for i in range(rows)],
+        axis=1,
+    )
+    for side in range(2):
+        first = 2 * side * channels
+        value = matmul(in_w_ref[:, first : first + channels], normed, TT)
+        gate = matmul(in_w_ref[:, first + channels : first + 2 * channels], normed, TT)
+        term = jax.nn.sigmoid(gate) * value * both
+        for q in range(part):
+            for i in range(rows):
+                staged[strided((side * part + q) * rows + i, n_row, step)] = term[
+                    q * n_row : (q + 1) * n_row, i * cols : (i + 1) * cols
+                ]
+    act = act_ref[...].astype(F32)
+    ada = matmul(cond_ref[...], ada_w_ref[...])
+    slab, wide = act.shape
+    inputs = (jax.nn.sigmoid(ada[:, :wide]) * normalize(act, 1) + ada[:, wide:]).astype(BF16)
+    inputs_ref[...] = inputs
+    inputs = inputs.astype(F32)
+    token = token_ref[...] - me * rows
+    alive = alive_ref[...]
+    tag = pad_lanes(((token + 1) * alive).astype(F32))
+    slots_ref[...] = jnp.zeros(slots_ref.shape, F32)
+    slots_ref[0:1] = pad_lanes(token.astype(F32))
+    slots_ref[1:2] = pad_lanes(alive.astype(F32))
+    slots_ref[2:3] = tag
+    tags = jnp.broadcast_to(tag, (2 * n_row - SIDE, LANES))
+    for d, rim in enumerate((inputs[slab - SIDE :], inputs[:SIDE])):
+        block = jnp.concatenate([rim, tags], axis=0)
+        for s in range(RIM_ROWS // 2):
+            staged[strided(step - RIM_ROWS + d * (RIM_ROWS // 2) + s, n_row, step)] = block[
+                s * n_row : (s + 1) * n_row
+            ]
+    out_ref[...] = staged[...].astype(BF16)
+
+
+def prepare(
+    pair_ref, gate_w_ref, inputs_ref, qkv_w_ref, slots_ref,
+    gate_ref, qkv_ref, query_hot_ref, live_ref, member_ref, select_ref, pair_band_ref, gate_band_ref,
+):
+    me = lax.axis_index("row")
+    rows, cols, channels = pair_ref.shape
+    slab = inputs_ref.shape[0]
+    token = slots_ref[0:1, :slab]
+    alive = slots_ref[1:2, :slab]
+    qkv_ref[...] = matmul(inputs_ref[...], qkv_w_ref[...]).astype(BF16)
+    token_col = column_of(token, slab)
+    query_hot_ref[...] = (token_col == (iota(query_hot_ref.shape, 1) // BAND_PAD).astype(F32)).astype(F32)
+    live_ref[...] = jnp.broadcast_to(column_of(alive, slab), live_ref.shape)
+    member_ref[...] = jnp.where(iota(member_ref.shape, 0).astype(F32) == token, alive, 0.0)
+    normed = normalize(pair_ref[...].reshape(rows * cols, channels).astype(F32), 1).astype(BF16)
+    gate_ref[...] = jax.nn.sigmoid(matmul(normed, gate_w_ref[...]))
+    place = iota((BAND_PAD, cols), 0)
+    target = (me - 1) * rows + place
+    select = ((target == iota((BAND_PAD, cols), 1)) & (place < 3 * rows)).astype(BF16)
+    select_ref[...] = select
+    pair_band_ref[...] = jnp.concatenate([matmul(select, pair_ref[i]) for i in range(rows)], axis=0)
+    normed_band = jnp.concatenate(
+        [matmul(select, normed[i * cols : (i + 1) * cols]) for i in range(rows)], axis=0
+    ).astype(BF16)
+    gate_band_ref[...] = jax.nn.sigmoid(matmul(normed_band, gate_w_ref[...]))
+
+
+def triangle_kernel(n_row, rows, got_ref, *refs):
+    out_ref = refs[5]
+    taken, right_terms, staged = refs[14:]
+    prepare(*refs[:5], *refs[6:14])
+    taken[...] = got_ref[...].astype(F32)
+    step = got_ref.shape[0] // n_row
+    part = right_terms.shape[0]
+    out_step = part * rows + RIM_ROWS
+    for q in range(part):
+        left = jnp.concatenate(
+            [taken[strided(q * rows + i, n_row, step)] for i in range(rows)], axis=0
+        ).astype(BF16)
+        for j in range(rows):
+            right_terms[q, strided(j, n_row, rows)] = taken[strided((part + q) * rows + j, n_row, step)]
+        summed = matmul(left, right_terms[q].astype(BF16), NT)
+        for i in range(rows):
+            staged[strided(q * rows + i, n_row, out_step)] = summed[i * n_row : (i + 1) * n_row]
+    nothing = jnp.zeros((1, LANES), F32)
+    for s in range(RIM_ROWS):
+        rim = taken[strided(step - RIM_ROWS + s, n_row, step)]
+        if s < RIM_ROWS // 2:
+            rim = jnp.concatenate([nothing, rim[:-1]], axis=0)
+        else:
+            rim = jnp.concatenate([rim[1:], nothing], axis=0)
+        staged[strided(out_step - RIM_ROWS + s, n_row, out_step)] = rim
+    out_ref[...] = staged[...].astype(BF16)
+
+
+def finish_kernel(
+    n_row, got_ref, pair_ref, out_w_ref, act_ref, slots_ref, bias_w_ref, gate_ref, qkv_ref, query_hot_ref, live_ref,
+    member_ref, select_ref, pair_band_ref, gate_band_ref, qkv_w_ref, attn_w_ref, ffn_in_ref, ffn_out_ref, agg_ref,
+    pair_out, atom_out, token_out, taken, pair_new, atom_new, token_new, bias_rows, products, values_ext, sems,
+):
+    me = lax.axis_index("row")
+    rows, cols, channels = pair_ref.shape
+    part = channels // n_row
+    step = part * rows + RIM_ROWS
+    half = RIM_ROWS // 2
+    slab, wide = act_ref.shape
+    heads = bias_w_ref.shape[0]
+    head_size = wide // heads
+    head_of = iota((QUERY_WINDOW, wide), 1) // head_size
+    windows = slab // QUERY_WINDOW
+    taken[...] = got_ref[...].astype(F32)
+    sums = [
+        jnp.concatenate([taken[strided(q * rows + i, n_row, step)] for q in range(part)], axis=0) for i in range(rows)
+    ]
+    band = jnp.concatenate([matmul(select_ref[...], s.astype(BF16), NT) for s in sums], axis=0)
+    band = matmul(normalize(band, 1).astype(BF16), out_w_ref[...])
+    band = (pair_band_ref[...] + gate_band_ref[...] * band).astype(BF16).astype(F32)
+    bias_rows[...] = matmul(bias_w_ref[...], normalize(band, 1).astype(BF16), NT).astype(BF16).astype(F32)
+    outer = jnp.concatenate(
+        [
+            taken[strided(step - RIM_ROWS + d * half + s, n_row, step)][: min(n_row, SIDE - s * n_row)]
+            for d in range(2)
+            for s in range(half)
+        ],
+        axis=0,
+    ).astype(BF16)
+    outer = matmul(outer, qkv_w_ref[:, wide:]).astype(BF16).astype(F32)
+    own = qkv_ref[...].astype(F32)
+    keys_ext, values = (
+        jnp.concatenate(
+            [outer[:SIDE, at : at + wide], own[:, wide + at : 2 * wide + at], outer[SIDE:, at : at + wide]], axis=0
+        )
+        for at in (0, wide)
+    )
+    values_ext[...] = values
+    for w in range(windows):
+        start = w * QUERY_WINDOW
+        query = own[start : start + QUERY_WINDOW, :wide]
+        split = jnp.concatenate([jnp.where(head_of == h, query, 0.0) for h in range(heads)], axis=0).astype(BF16)
+        products[w] = matmul(split, keys_ext[start : start + KEYS].astype(BF16), NT) * (1 / math.sqrt(head_size))
+    for i in range(rows):
+        update = matmul(normalize(sums[i], 0).astype(BF16), out_w_ref[...], TN)
+        pair_new[i] = (pair_ref[i].astype(F32) + gate_ref[i * cols : (i + 1) * cols] * update).astype(BF16)
+    pair_copy = pltpu.make_async_copy(pair_new, pair_out, sems.at[0])
+    atom_copy = pltpu.make_async_copy(atom_new, atom_out, sems.at[1])
+    token_copy = pltpu.make_async_copy(token_new, token_out, sems.at[2])
+    pair_copy.start()
+
+    @pl.when(me >= 0)
+    def _():
+        tag_at = [(step - RIM_ROWS + d * half + SIDE // n_row) + step * (SIDE % n_row) for d in range(2)]
+        before_tag, after_tag = (taken[at : at + 1] for at in tag_at)
+        own_tag = slots_ref[2:3]
+        query_hot = query_hot_ref[...]
+        flat = query_hot.shape[1]
+        slot = (iota((flat, KEYS), 0) % BAND_PAD).astype(F32)
+        lane = iota((1, LANES), 1)
+        mixed = []
+        for w in range(windows):
+            start = w * QUERY_WINDOW
+            before_end = SIDE - start
+            own_end = before_end + slab
+            is_before, is_own = lane < before_end, lane < own_end
+            tag = jnp.where(
+                is_before,
+                pltpu.roll(before_tag, (SIDE - slab - start) % LANES, 1),
+                jnp.where(
+                    is_own, pltpu.roll(own_tag, before_end % LANES, 1), pltpu.roll(after_tag, own_end % LANES, 1)
+                ),
+            )
+            offset = jnp.where(is_before, 0.0, jnp.where(is_own, 1.0 * rows, 2.0 * rows))
+            valid = tag > 0
+            key_slot = jnp.where(valid, tag - 1 + offset, -1.0)
+            key_hot = (slot == key_slot).astype(BF16)
+            hot = query_hot[start : start + QUERY_WINDOW]
+            hot_bias = jnp.concatenate([hot * bias_rows[h : h + 1] for h in range(heads)], axis=0).astype(BF16)
+            scores = jnp.where(valid, products[w] + matmul(hot_bias, key_hot), -1e30)
+            powers = jnp.exp(scores - jnp.max(scores, axis=1, keepdims=True))
+            weights = (powers / jnp.sum(powers, axis=1, keepdims=True)).astype(BF16)
+            blend = matmul(weights, values_ext[start : start + KEYS].astype(BF16))
+            total = jnp.zeros((QUERY_WINDOW, wide), F32)
+            for h in range(heads):
+                total = jnp.where(head_of == h, blend[h * QUERY_WINDOW : (h + 1) * QUERY_WINDOW], total)
+            mixed.append(total)
+        attended = jnp.concatenate(mixed, axis=0).astype(BF16)
+        middle = act_ref[...].astype(F32) + matmul(attended, attn_w_ref[...])
+        expanded = matmul(normalize(middle, 1).astype(BF16), ffn_in_ref[...])
+        hidden = ffn_out_ref.shape[0]
+        inner = (jax.nn.silu(expanded[:, :hidden]) * expanded[:, hidden:]).astype(BF16)
+        final = ((middle + matmul(inner, ffn_out_ref[...])) * live_ref[...]).astype(BF16)
+        atom_new[...] = final
+        atom_copy.start()
+        features = jnp.maximum(matmul(final, agg_ref[...]), 0.0).astype(BF16)
+        member = member_ref[...]
+        totals = matmul(member.astype(BF16), features)
+        counts = jnp.maximum(jnp.sum(member, axis=1, keepdims=True), 1.0)
+        token_new[...] = (totals / counts).astype(BF16)[:rows]
+        token_copy.start()
+
+    pair_copy.wait()
+    atom_copy.wait()
+    token_copy.wait()
+
+
+def in_vmem(count):
+    return [pl.BlockSpec(memory_space=pltpu.VMEM)] * count
+
+
+def in_hbm(arrays):
+    return [pltpu.with_memory_space_constraint(a, pltpu.HBM) for a in arrays]
+
+
+def cost(flops, nbytes, exps=0):
+    return pl.CostEstimate(flops=flops, bytes_accessed=nbytes, transcendentals=exps)
+
+
+def exchange(blocks, n_row):
+    grouped = blocks.reshape(n_row, -1, RIM_ROWS, LANES)
+    return lax.all_to_all(grouped, "row", split_axis=0, concat_axis=0, tiled=True).reshape(blocks.shape)
+
+
+def by_kernels(
+    pair, token_mask, tri_in_weight, tri_gate_weight, tri_out_weight, atom_act, atom_cond, atom_token, atom_mask,
+    ada_weight, qkv_weight, bias_weight, attn_out_weight, ffn_in_weight, ffn_out_weight, agg_weight,
+):
+    n_row = lax.axis_size("row")
+    rows, cols, channels = pair.shape
+    slab, wide = atom_act.shape
+    width = rows * cols
+    part = channels // n_row
+    mask = token_mask.reshape(1, -1)
+    token = atom_token.reshape(1, -1)
+    alive = atom_mask.reshape(1, -1)
+    sent = n_row * (2 * part * rows + RIM_ROWS)
+    back_rows = n_row * (part * rows + RIM_ROWS)
+    sources = (pair, atom_act, bias_weight.T, tri_in_weight, atom_cond, ada_weight, mask, token, alive)
+    kept = 3
+    pair, atom_act, bias_rows, terms, inputs, slots = pl.pallas_call(
+        functools.partial(send_kernel, n_row),
+        out_shape=(
+            *(jax.ShapeDtypeStruct(a.shape, a.dtype) for a in sources[:kept]),
+            jax.ShapeDtypeStruct((sent, LANES), BF16),
+            jax.ShapeDtypeStruct((slab, wide), BF16),
+            jax.ShapeDtypeStruct((SUBLANES, LANES), F32),
+        ),
+        in_specs=[pl.BlockSpec(memory_space=pltpu.HBM)] * len(sources),
+        out_specs=tuple(in_vmem(kept + 3)),
+        scratch_shapes=[
+            *(pltpu.VMEM(a.shape, a.dtype) for a in sources[kept:]),
+            pltpu.VMEM((sent, LANES), F32),
+            pltpu.SemaphoreType.DMA((len(sources),)),
+        ],
+        cost_estimate=cost(8 * width * channels * channels, 1 << 20, 2 * width * channels),
+        compiler_params=LIMIT,
+        name="send",
+    )(*in_hbm(sources))
+    got = exchange(terms, n_row)
+    band_shape = jax.ShapeDtypeStruct((rows * BAND_PAD, channels), F32)
+    sums, *prepared = pl.pallas_call(
+        functools.partial(triangle_kernel, n_row, rows),
+        out_shape=(
+            jax.ShapeDtypeStruct((back_rows, LANES), BF16),
+            jax.ShapeDtypeStruct((width, channels), F32),
+            jax.ShapeDtypeStruct((slab, 3 * wide), BF16),
+            jax.ShapeDtypeStruct((slab, rows * BAND_PAD), F32),
+            jax.ShapeDtypeStruct((slab, wide), F32),
+            jax.ShapeDtypeStruct((SUBLANES, slab), F32),
+            jax.ShapeDtypeStruct((BAND_PAD, cols), BF16),
+            band_shape,
+            band_shape,
+        ),
+        in_specs=in_vmem(6),
+        out_specs=tuple(in_vmem(9)),
+        scratch_shapes=[
+            pltpu.VMEM((sent, LANES), F32),
+            pltpu.VMEM((part, cols, cols), F32),
+            pltpu.VMEM((back_rows, LANES), F32),
+        ],
+        cost_estimate=cost(2 * width * width, 1 << 19),
+        compiler_params=LIMIT,
+        name="triangle",
+    )(got, pair, tri_gate_weight, inputs, qkv_weight, slots)
+    back = exchange(sums, n_row)
+    token_shape = (rows, agg_weight.shape[1])
+    return pl.pallas_call(
+        functools.partial(finish_kernel, n_row),
+        out_shape=(
+            jax.ShapeDtypeStruct(pair.shape, BF16),
+            jax.ShapeDtypeStruct(atom_act.shape, BF16),
+            jax.ShapeDtypeStruct(token_shape, BF16),
+        ),
+        in_specs=in_vmem(19),
+        out_specs=(pl.BlockSpec(memory_space=pltpu.HBM),) * 3,
+        scratch_shapes=[
+            pltpu.VMEM((back_rows, LANES), F32),
+            pltpu.VMEM(pair.shape, BF16),
+            pltpu.VMEM(atom_act.shape, BF16),
+            pltpu.VMEM(token_shape, BF16),
+            pltpu.VMEM((bias_weight.shape[1], rows * BAND_PAD), F32),
+            pltpu.VMEM((slab // QUERY_WINDOW, bias_weight.shape[1] * QUERY_WINDOW, KEYS), F32),
+            pltpu.VMEM((slab + 2 * SIDE, wide), F32),
+            pltpu.SemaphoreType.DMA((3,)),
+        ],
+        cost_estimate=cost(4 * width * channels * channels, 1 << 20),
+        compiler_params=LIMIT,
+        name="finish",
+    )(
+        back, pair, tri_out_weight, atom_act, slots, bias_rows, *prepared, qkv_weight, attn_out_weight, ffn_in_weight,
+        ffn_out_weight, agg_weight,
+    )
+
+
+def kernels_fit(mesh, args):
+    pair, atom_act, bias_weight = args[0], args[5], args[11]
+    n_row = mesh.shape["row"]
+    parts = mesh.shape["groups"] * n_row
+    cols, channels = pair.shape[1:]
+    rows = pair.shape[0] // parts
+    slab = atom_act.shape[0] // parts
+    wide = atom_act.shape[1]
+    return (
+        mesh.shape["col"] == 1
+        and cols == channels == wide == LANES
+        and cols == n_row * rows
+        and channels % n_row == 0
+        and n_row % SUBLANES == 0
+        and SIDE < RIM_ROWS // 2 * n_row
+        and 3 * rows <= BAND_PAD
+        and rows <= SUBLANES
+        and SIDE <= slab <= LANES
+        and slab % QUERY_WINDOW == 0
+        and slab - QUERY_WINDOW <= SIDE
+        and wide % bias_weight.shape[1] == 0
+    )
+
+
 def solution(mesh):
     in_specs = (
         P(("groups", "row"), "col", None),
@@ -224,6 +621,9 @@
         P(("groups", "row"), None),
         P(("groups", "row"), None),
     )
-    return jax.shard_map(
-        per_device, mesh=mesh, in_specs=in_specs, out_specs=out_specs, check_vma=False
-    )
+
+    def layer(*args):
+        body = by_kernels if kernels_fit(mesh, args) else per_device
+        return jax.shard_map(body, mesh=mesh, in_specs=in_specs, out_specs=out_specs, check_vma=False)(*args)
+
+    return layer

time: 61.9 us -> 35.3 us (0.57)
  blocking collectives: 0 us -> 29.2 us
  starting transfers between devices: 28.7 us -> 0 us
  waiting for transfers between devices: 12 us -> 0 us
  local copies, waits for them, and re-layouts: 11.3 us -> 0.04 us
  Pallas kernels: 0 us -> 5.08 us
  matrix products: 4.74 us -> 0 us
  other arithmetic: 3.08 us -> 0 us
    all_to_all x0 -> x2, blocking collectives: none -> 29.2 us  [exchange(): lax.all_to_all(grouped, 'row', split_axis=0, concat_axis=0, tiled=True)]
    all_to_all x3 -> x0, starting transfers between devices: 19.8 us -> none  [the longest x1 9.8 us: per_device(): lax.all_to_all(left, 'row', split_axis=0, concat_axis=1, tiled=True)]
    all_to_all x3 -> x0, waiting for transfers between devices: 12 us -> none  [the longest x1 6.72 us: per_device(): lax.all_to_all(tri_sum, 'row', split_axis=1, concat_axis=0, tiled=True)]
    ppermute x4 -> x0, starting transfers between devices: 8.9 us -> none  [the longest x2 6.31 us: extended(): before = lax.ppermute(last, axis, up)]
    pallas_call x0 -> x3, Pallas kernels: none -> 5.08 us  [the longest x1 2.77 us: by_kernels(): pl.pallas_call(functools.partial(finish_kernel, n_row), out_shape=(jax.Sh...]
    dot_general x17 -> x0, matrix products: 4.74 us -> none  [the longest x1 0.85 us: per_device(): jnp.einsum('at,ac->tc', live_onehot, features, preferred_element_type=jnp...]
    unnamed x40 -> x14, local copies, waits for them, and re-layouts: 4.36 us -> 0.04 us
    gather x3 -> x0, local copies, waits for them, and re-layouts: 3.84 us -> none  [the longest x1 1.88 us: per_device(): window_valid = key_valid[key_index]]
  transfers between devices with their start and end apart: 7 -> 0, of which waited for: 2 -> 0; matrix products, arithmetic and copies ran while one was open for 13% -> 0% of each run, Pallas kernels for 0% -> 0%
where the time goes in v3:
time: 35.3 us; the launch traced here: 35.1 us
  blocking collectives  29.2 us (83%)
  Pallas kernels  5.08 us (14%)
  between operations  0.72 us (2%)
    all_to_all x2, blocking collectives, exchange(): lax.all_to_all(grouped, 'row', split_axis=0, concat_axis=0, tiled=True)  29.2 us
    pallas_call x1, Pallas kernels, by_kernels(): pl.pallas_call(functools.partial(finish_kernel, n_row), out_shape=(jax.Sh...  2.77 us
    pallas_call x1, Pallas kernels, by_kernels(): pl.pallas_call(functools.partial(send_kernel, n_row), out_shape=(*(jax.Sh...  1.68 us

profile of v3, /device:TPU:0, one launch (start us, length us, event | category | flops | bytes accessed | tf_op | source)
XLA Modules:
  0.0 35.1 jit_solution(9624962965153129233)
XLA Ops:
  0.6 1.7 %send.1 = (bf16[4,128,128]{2,1,0:T(8,128)(2,1)S(1)}, bf16[64,128]{1,0:T(8,128)(2,1)S(1)}, bf16[4,128]{1,0:T(4,128)(2,1)S(1)}, bf16[1152,128]{1,0:T(8,128)(2,1)S(...) custom-call(bf16[4,128,128]{2,1,0:T(8,128)(2,1)} %pair_hbm.1, bf16[64,128]{1,0:T(8,128)(2,1)} %act_hbm.1, ...), custom_call_target="tpu_custom_call" | custom-call | flops 67108864 | bytes 1048576 | tf_op jit(solution)/shard_map/send/pallas_call | solution.py:501
  2.3 0.0 copy-start
  2.3 0.0 copy-start.4
  2.3 18.5 %all_to_all.10 = bf16[32,9,4,128]{3,2,1,0:T(4,128)(2,1)S(1)} all-to-all(bf16[32,9,4,128]{3,2,1,0:T(4,128)(2,1)S(1)} %bitcast.10), channel_id=1, replica_groups=mesh['groups'=1,'row'=32,'col'=1] {'row'}, dimensions={0} | all-to-all | bytes 589824 | tf_op jit(solution)/shard_map/all_to_all | solution.py:482
  20.9 0.0 copy-done
  20.9 0.0 copy-done.4
  20.9 0.0 copy-start.6
  20.9 0.6 %triangle.1 = (bf16[640,128]{1,0:T(8,128)(2,1)S(1)}, f32[512,128]{1,0:T(8,128)S(1)}, bf16[64,384]{1,0:T(8,128)(2,1)S(1)}, f32[64,64]{1,0:T(8,128)S(1)}, f32[64,1...) custom-call(bf16[1152,128]{1,0:T(8,128)(2,1)S(1)} %bitcast.8, ...), custom_call_target="tpu_custom_call" | custom-call | flops 524288 | bytes 524288 | tf_op jit(solution)/shard_map/triangle/pallas_call | solution.py:522
  21.5 0.0 copy-start.1
  21.5 0.0 copy-start.2
  21.5 0.0 copy-start.3
  21.6 0.0 copy-start.5
  21.6 10.7 %all_to_all.11 = bf16[32,5,4,128]{3,2,1,0:T(4,128)(2,1)S(1)} all-to-all(bf16[32,5,4,128]{3,2,1,0:T(4,128)(2,1)S(1)} %bitcast.11), channel_id=1, replica_groups=mesh['groups'=1,'row'=32,'col'=1] {'row'}, dimensions={0} | all-to-all | bytes 327680 | tf_op jit(solution)/shard_map/all_to_all | solution.py:482
  32.3 0.0 copy-done.6
  32.3 0.0 copy-done.1
  32.3 0.0 copy-done.2
  32.3 0.0 copy-done.3
  32.3 0.0 copy-done.5
  32.3 2.8 %finish.1 = (bf16[4,128,128]{2,1,0:T(8,128)(2,1)}, bf16[64,128]{1,0:T(8,128)(2,1)}, bf16[4,384]{1,0:T(4,128)(2,1)}) custom-call(bf16[640,128]{1,0:T(8,128)(2,1)S(1)} %bitcast.9, bf16[4,128,128]{2,1,0:T(8,128)(2,1)S(1)} %get-tuple-element.19.refs_0_.pair_ref, bf16[128,128]{1,0:T(8,128)(2,1)S(1)} %copy-done.5, bf16[64,128]{1,0:T(8,128)(2,1)S(1)} %get-tuple-element.23.act_ref, ...), custom_call_target="tpu_custom_call" | custom-call | flops 33554432 | bytes 1048576 | tf_op jit(solution)/shard_map/finish/pallas_call | solution.py:548
Async XLA Ops:
  2.3 18.6 %copy-start = (bf16[128,384]{1,0:T(8,128)(2,1)S(1)}, bf16[128,384]{1,0:T(8,128)(2,1)}, u32[]{:S(2)}) copy-start(bf16[128,384]{1,0:T(8,128)(2,1)} %qkv_w_ref.1) | copy-start | bytes 294916
  2.3 18.5 %copy-start.4 = (bf16[128,128]{1,0:T(8,128)(2,1)S(1)}, bf16[128,128]{1,0:T(8,128)(2,1)}, u32[]{:S(2)}) copy-start(bf16[128,128]{1,0:T(8,128)(2,1)} %refs_1_.1) | copy-start | bytes 98308
  20.9 11.4 %copy-start.6 = (bf16[128,128]{1,0:T(8,128)(2,1)S(1)}, bf16[128,128]{1,0:T(8,128)(2,1)}, u32[]{:S(2)}) copy-start(bf16[128,128]{1,0:T(8,128)(2,1)} %attn_w_ref.1) | copy-start | bytes 98308
  21.5 10.8 %copy-start.1 = (bf16[128,512]{1,0:T(8,128)(2,1)S(1)}, bf16[128,512]{1,0:T(8,128)(2,1)}, u32[]{:S(2)}) copy-start(bf16[128,512]{1,0:T(8,128)(2,1)} %ffn_in_ref.1) | copy-start | bytes 393220
  21.5 10.8 %copy-start.2 = (bf16[128,384]{1,0:T(8,128)(2,1)S(1)}, bf16[128,384]{1,0:T(8,128)(2,1)}, u32[]{:S(2)}) copy-start(bf16[128,384]{1,0:T(8,128)(2,1)} %agg_ref.1) | copy-start | bytes 294916
  21.5 10.7 %copy-start.3 = (bf16[256,128]{1,0:T(8,128)(2,1)S(1)}, bf16[256,128]{1,0:T(8,128)(2,1)}, u32[]{:S(2)}) copy-start(bf16[256,128]{1,0:T(8,128)(2,1)} %ffn_out_ref.1) | copy-start | bytes 196612
  21.6 10.7 %copy-start.5 = (bf16[128,128]{1,0:T(8,128)(2,1)S(1)}, bf16[128,128]{1,0:T(8,128)(2,1)}, u32[]{:S(2)}) copy-start(bf16[128,128]{1,0:T(8,128)(2,1)} %out_w_ref.1) | copy-start | bytes 98308

commit v4 on v3

--- a/solution.py
+++ b/solution.py
@@ -249,19 +249,20 @@
     pair_ref, act_ref, bias_w_ref, out_ref, inputs_ref, slots_ref,
     in_w_ref, cond_ref, ada_w_ref, mask_ref, token_ref, alive_ref, staged, sems,
 ):
-    sources = (pair_hbm, cond_hbm, ada_w_hbm, act_hbm, in_w_hbm, mask_hbm, token_hbm, alive_hbm, bias_w_hbm)
-    places = (pair_ref, cond_ref, ada_w_ref, act_ref, in_w_ref, mask_ref, token_ref, alive_ref, bias_w_ref)
+    sources = (pair_hbm, cond_hbm, act_hbm, mask_hbm, token_hbm, alive_hbm, bias_w_hbm, ada_w_hbm, in_w_hbm)
+    places = (pair_ref, cond_ref, act_ref, mask_ref, token_ref, alive_ref, bias_w_ref, ada_w_ref, in_w_ref)
     loads = [pltpu.make_async_copy(a, b, sems.at[i]) for i, (a, b) in enumerate(zip(sources, places))]
     for load in loads:
         load.start()
-    for load in loads:
-        load.wait()
+    loads[0].wait()
     me = lax.axis_index("row")
     rows, cols, channels = pair_ref.shape
     part = channels // n_row
     width = rows * cols
     step = 2 * part * rows + RIM_ROWS
     normed = normalize(pair_ref[...].reshape(width, channels).astype(F32), 1).astype(BF16)
+    for load in loads[1:]:
+        load.wait()
     live = mask_ref[...].astype(F32)
     lane = iota(live.shape, 1)
     both = jnp.concatenate(
@@ -303,9 +304,8 @@
 
 def prepare(
     pair_ref, gate_w_ref, inputs_ref, qkv_w_ref, slots_ref,
-    gate_ref, qkv_ref, query_hot_ref, live_ref, member_ref, select_ref, pair_band_ref, gate_band_ref,
+    gate_ref, qkv_ref, query_hot_ref, live_ref, member_ref,
 ):
-    me = lax.axis_index("row")
     rows, cols, channels = pair_ref.shape
     slab = inputs_ref.shape[0]
     token = slots_ref[0:1, :slab]
@@ -317,21 +317,12 @@
     member_ref[...] = jnp.where(iota(member_ref.shape, 0).astype(F32) == token, alive, 0.0)
     normed = normalize(pair_ref[...].reshape(rows * cols, channels).astype(F32), 1).astype(BF16)
     gate_ref[...] = jax.nn.sigmoid(matmul(normed, gate_w_ref[...]))
-    place = iota((BAND_PAD, cols), 0)
-    target = (me - 1) * rows + place
-    select = ((target == iota((BAND_PAD, cols), 1)) & (place < 3 * rows)).astype(BF16)
-    select_ref[...] = select
-    pair_band_ref[...] = jnp.concatenate([matmul(select, pair_ref[i]) for i in range(rows)], axis=0)
-    normed_band = jnp.concatenate(
-        [matmul(select, normed[i * cols : (i + 1) * cols]) for i in range(rows)], axis=0
-    ).astype(BF16)
-    gate_band_ref[...] = jax.nn.sigmoid(matmul(normed_band, gate_w_ref[...]))
 
 
 def triangle_kernel(n_row, rows, got_ref, *refs):
     out_ref = refs[5]
-    taken, right_terms, staged = refs[14:]
-    prepare(*refs[:5], *refs[6:14])
+    taken, right_terms, staged = refs[11:]
+    prepare(*refs[:5], *refs[6:11])
     taken[...] = got_ref[...].astype(F32)
     step = got_ref.shape[0] // n_row
     part = right_terms.shape[0]
@@ -358,8 +349,8 @@
 
 def finish_kernel(
     n_row, got_ref, pair_ref, out_w_ref, act_ref, slots_ref, bias_w_ref, gate_ref, qkv_ref, query_hot_ref, live_ref,
-    member_ref, select_ref, pair_band_ref, gate_band_ref, qkv_w_ref, attn_w_ref, ffn_in_ref, ffn_out_ref, agg_ref,
-    pair_out, atom_out, token_out, taken, pair_new, atom_new, token_new, bias_rows, products, values_ext, sems,
+    member_ref, qkv_w_ref, attn_w_ref, ffn_in_ref, ffn_out_ref, agg_ref,
+    pair_out, atom_out, token_out, taken, pair_new, atom_new, token_new, padded, products, values_ext, sems,
 ):
     me = lax.axis_index("row")
     rows, cols, channels = pair_ref.shape
@@ -375,10 +366,6 @@
     sums = [
         jnp.concatenate([taken[strided(q * rows + i, n_row, step)] for q in range(part)], axis=0) for i in range(rows)
     ]
-    band = jnp.concatenate([matmul(select_ref[...], s.astype(BF16), NT) for s in sums], axis=0)
-    band = matmul(normalize(band, 1).astype(BF16), out_w_ref[...])
-    band = (pair_band_ref[...] + gate_band_ref[...] * band).astype(BF16).astype(F32)
-    bias_rows[...] = matmul(bias_w_ref[...], normalize(band, 1).astype(BF16), NT).astype(BF16).astype(F32)
     outer = jnp.concatenate(
         [
             taken[strided(step - RIM_ROWS + d * half + s, n_row, step)][: min(n_row, SIDE - s * n_row)]
@@ -403,7 +390,11 @@
         products[w] = matmul(split, keys_ext[start : start + KEYS].astype(BF16), NT) * (1 / math.sqrt(head_size))
     for i in range(rows):
         update = matmul(normalize(sums[i], 0).astype(BF16), out_w_ref[...], TN)
-        pair_new[i] = (pair_ref[i].astype(F32) + gate_ref[i * cols : (i + 1) * cols] * update).astype(BF16)
+        fresh = (pair_ref[i].astype(F32) + gate_ref[i * cols : (i + 1) * cols] * update).astype(BF16)
+        pair_new[i] = fresh
+        padded[i, :SUBLANES] = jnp.zeros((SUBLANES, channels), F32)
+        padded[i, SUBLANES : SUBLANES + cols] = fresh.astype(F32)
+        padded[i, SUBLANES + cols :] = jnp.zeros((BAND_PAD, channels), F32)
     pair_copy = pltpu.make_async_copy(pair_new, pair_out, sems.at[0])
     atom_copy = pltpu.make_async_copy(atom_new, atom_out, sems.at[1])
     token_copy = pltpu.make_async_copy(token_new, token_out, sems.at[2])
@@ -411,6 +402,9 @@
 
     @pl.when(me >= 0)
     def _():
+        band = [padded[i, pl.ds(SUBLANES + (me - 1) * rows, BAND_PAD)] for i in range(rows)]
+        band = normalize(jnp.concatenate(band, axis=0), 1).astype(BF16)
+        bias_rows = matmul(bias_w_ref[...], band, NT).astype(BF16).astype(F32)
         tag_at = [(step - RIM_ROWS + d * half + SIDE // n_row) + step * (SIDE % n_row) for d in range(2)]
         before_tag, after_tag = (taken[at : at + 1] for at in tag_at)
         own_tag = slots_ref[2:3]
@@ -439,8 +433,8 @@
             hot_bias = jnp.concatenate([hot * bias_rows[h : h + 1] for h in range(heads)], axis=0).astype(BF16)
             scores = jnp.where(valid, products[w] + matmul(hot_bias, key_hot), -1e30)
             powers = jnp.exp(scores - jnp.max(scores, axis=1, keepdims=True))
-            weights = (powers / jnp.sum(powers, axis=1, keepdims=True)).astype(BF16)
-            blend = matmul(weights, values_ext[start : start + KEYS].astype(BF16))
+            blend = matmul(powers.astype(BF16), values_ext[start : start + KEYS].astype(BF16))
+            blend = blend / jnp.sum(powers, axis=1, keepdims=True)
             total = jnp.zeros((QUERY_WINDOW, wide), F32)
             for h in range(heads):
                 total = jnp.where(head_of == h, blend[h * QUERY_WINDOW : (h + 1) * QUERY_WINDOW], total)
@@ -518,7 +512,6 @@
         name="send",
     )(*in_hbm(sources))
     got = exchange(terms, n_row)
-    band_shape = jax.ShapeDtypeStruct((rows * BAND_PAD, channels), F32)
     sums, *prepared = pl.pallas_call(
         functools.partial(triangle_kernel, n_row, rows),
         out_shape=(
@@ -528,12 +521,9 @@
             jax.ShapeDtypeStruct((slab, rows * BAND_PAD), F32),
             jax.ShapeDtypeStruct((slab, wide), F32),
             jax.ShapeDtypeStruct((SUBLANES, slab), F32),
-            jax.ShapeDtypeStruct((BAND_PAD, cols), BF16),
-            band_shape,
-            band_shape,
         ),
         in_specs=in_vmem(6),
-        out_specs=tuple(in_vmem(9)),
+        out_specs=tuple(in_vmem(6)),
         scratch_shapes=[
             pltpu.VMEM((sent, LANES), F32),
             pltpu.VMEM((part, cols, cols), F32),
@@ -552,14 +542,14 @@
             jax.ShapeDtypeStruct(atom_act.shape, BF16),
             jax.ShapeDtypeStruct(token_shape, BF16),
         ),
-        in_specs=in_vmem(19),
+        in_specs=in_vmem(16),
         out_specs=(pl.BlockSpec(memory_space=pltpu.HBM),) * 3,
         scratch_shapes=[
             pltpu.VMEM((back_rows, LANES), F32),
             pltpu.VMEM(pair.shape, BF16),
             pltpu.VMEM(atom_act.shape, BF16),
             pltpu.VMEM(token_shape, BF16),
-            pltpu.VMEM((bias_weight.shape[1], rows * BAND_PAD), F32),
+            pltpu.VMEM((rows, SUBLANES + cols + BAND_PAD, channels), F32),
             pltpu.VMEM((slab // QUERY_WINDOW, bias_weight.shape[1] * QUERY_WINDOW, KEYS), F32),
             pltpu.VMEM((slab + 2 * SIDE, wide), F32),
             pltpu.SemaphoreType.DMA((3,)),

time: 35.3 us -> 34.7 us (0.983)
  Pallas kernels: 5.08 us -> 4.49 us
where the time goes in v4:
time: 34.7 us; the launch traced here: 34.5 us
  blocking collectives  29.2 us (84%)
  Pallas kernels  4.49 us (13%)
  between operations  0.72 us (2%)
    all_to_all x2, blocking collectives, exchange(): lax.all_to_all(grouped, 'row', split_axis=0, concat_axis=0, tiled=True)  29.2 us
    pallas_call x1, Pallas kernels, by_kernels(): pl.pallas_call(functools.partial(finish_kernel, n_row), out_shape=(jax.Sh...  2.42 us
    pallas_call x1, Pallas kernels, by_kernels(): pl.pallas_call(functools.partial(send_kernel, n_row), out_shape=(*(jax.Sh...  1.61 us

profile of v4, /device:TPU:0, one launch (start us, length us, event | category | flops | bytes accessed | tf_op | source)
XLA Modules:
  0.0 34.5 jit_solution(4677299867845150019)
XLA Ops:
  0.6 1.6 %send.1 = (bf16[4,128,128]{2,1,0:T(8,128)(2,1)S(1)}, bf16[64,128]{1,0:T(8,128)(2,1)S(1)}, bf16[4,128]{1,0:T(4,128)(2,1)S(1)}, bf16[1152,128]{1,0:T(8,128)(2,1)S(...) custom-call(bf16[4,128,128]{2,1,0:T(8,128)(2,1)} %pair_hbm.1, bf16[64,128]{1,0:T(8,128)(2,1)} %act_hbm.1, ...), custom_call_target="tpu_custom_call" | custom-call | flops 67108864 | bytes 1048576 | tf_op jit(solution)/shard_map/send/pallas_call | solution.py:495
  2.3 0.0 copy-start
  2.3 0.0 copy-start.4
  2.3 18.5 %all_to_all.10 = bf16[32,9,4,128]{3,2,1,0:T(4,128)(2,1)S(1)} all-to-all(bf16[32,9,4,128]{3,2,1,0:T(4,128)(2,1)S(1)} %bitcast.10), channel_id=1, replica_groups=mesh['groups'=1,'row'=32,'col'=1] {'row'}, dimensions={0} | all-to-all | bytes 589824 | tf_op jit(solution)/shard_map/all_to_all | solution.py:476
  20.8 0.0 copy-done
  20.8 0.0 copy-done.4
  20.8 0.0 copy-start.6
  20.8 0.5 %triangle.1 = (bf16[640,128]{1,0:T(8,128)(2,1)S(1)}, f32[512,128]{1,0:T(8,128)S(1)}, bf16[64,384]{1,0:T(8,128)(2,1)S(1)}, f32[64,64]{1,0:T(8,128)S(1)}, f32[64,128]{1,0:T(8,128)S(1)}, /*index=5*/f32[8,64]{1,0:T(8,128)S(1)}) custom-call(bf16[1152,128]{1,0:T(8,128)(2,1)S(1)} %bitcast.8, bf16[4,128,128]{2,1,0:T(8,128)(2,1)S(1)} %get-tuple-element.16.refs_0_.pair_ref, ...), custom_call_target="tpu_custom_call" | custom-call | flops 524288 | bytes 524288 | tf_op jit(solution)/shard_map/triangle/pallas_call | solution.py:515
  21.3 0.0 copy-start.1
  21.3 0.0 copy-start.2
  21.3 0.0 copy-start.3
  21.3 0.0 copy-start.5
  21.3 10.7 %all_to_all.11 = bf16[32,5,4,128]{3,2,1,0:T(4,128)(2,1)S(1)} all-to-all(bf16[32,5,4,128]{3,2,1,0:T(4,128)(2,1)S(1)} %bitcast.11), channel_id=1, replica_groups=mesh['groups'=1,'row'=32,'col'=1] {'row'}, dimensions={0} | all-to-all | bytes 327680 | tf_op jit(solution)/shard_map/all_to_all | solution.py:476
  32.0 0.0 copy-done.6
  32.1 0.0 copy-done.1
  32.1 0.0 copy-done.2
  32.1 0.0 copy-done.3
  32.1 0.0 copy-done.5
  32.1 2.4 %finish.1 = (bf16[4,128,128]{2,1,0:T(8,128)(2,1)}, bf16[64,128]{1,0:T(8,128)(2,1)}, bf16[4,384]{1,0:T(4,128)(2,1)}) custom-call(bf16[640,128]{1,0:T(8,128)(2,1)S(1)} %bitcast.9, bf16[4,128,128]{2,1,0:T(8,128)(2,1)S(1)} %get-tuple-element.16.refs_0_.pair_ref, bf16[128,128]{1,0:T(8,128)(2,1)S(1)} %copy-done.5, bf16[64,128]{1,0:T(8,128)(2,1)S(1)} %get-tuple-element.20.act_ref, ...), custom_call_target="tpu_custom_call" | custom-call | flops 33554432 | bytes 1048576 | tf_op jit(solution)/shard_map/finish/pallas_call | solution.py:538
Async XLA Ops:
  2.3 18.6 %copy-start = (bf16[128,384]{1,0:T(8,128)(2,1)S(1)}, bf16[128,384]{1,0:T(8,128)(2,1)}, u32[]{:S(2)}) copy-start(bf16[128,384]{1,0:T(8,128)(2,1)} %qkv_w_ref.1) | copy-start | bytes 294916
  2.3 18.6 %copy-start.4 = (bf16[128,128]{1,0:T(8,128)(2,1)S(1)}, bf16[128,128]{1,0:T(8,128)(2,1)}, u32[]{:S(2)}) copy-start(bf16[128,128]{1,0:T(8,128)(2,1)} %refs_1_.1) | copy-start | bytes 98308
  20.8 11.2 %copy-start.6 = (bf16[128,128]{1,0:T(8,128)(2,1)S(1)}, bf16[128,128]{1,0:T(8,128)(2,1)}, u32[]{:S(2)}) copy-start(bf16[128,128]{1,0:T(8,128)(2,1)} %attn_w_ref.1) | copy-start | bytes 98308
  21.3 10.8 %copy-start.1 = (bf16[128,512]{1,0:T(8,128)(2,1)S(1)}, bf16[128,512]{1,0:T(8,128)(2,1)}, u32[]{:S(2)}) copy-start(bf16[128,512]{1,0:T(8,128)(2,1)} %ffn_in_ref.1) | copy-start | bytes 393220
  21.3 10.8 %copy-start.2 = (bf16[128,384]{1,0:T(8,128)(2,1)S(1)}, bf16[128,384]{1,0:T(8,128)(2,1)}, u32[]{:S(2)}) copy-start(bf16[128,384]{1,0:T(8,128)(2,1)} %agg_ref.1) | copy-start | bytes 294916
  21.3 10.7 %copy-start.3 = (bf16[256,128]{1,0:T(8,128)(2,1)S(1)}, bf16[256,128]{1,0:T(8,128)(2,1)}, u32[]{:S(2)}) copy-start(bf16[256,128]{1,0:T(8,128)(2,1)} %ffn_out_ref.1) | copy-start | bytes 196612
  21.3 10.7 %copy-start.5 = (bf16[128,128]{1,0:T(8,128)(2,1)S(1)}, bf16[128,128]{1,0:T(8,128)(2,1)}, u32[]{:S(2)}) copy-start(bf16[128,128]{1,0:T(8,128)(2,1)} %out_w_ref.1) | copy-start | bytes 98308

commit v5 on v4

--- a/solution.py
+++ b/solution.py
@@ -303,8 +303,8 @@
 
 
 def prepare(
-    pair_ref, gate_w_ref, inputs_ref, qkv_w_ref, slots_ref,
-    gate_ref, qkv_ref, query_hot_ref, live_ref, member_ref,
+    pair_ref, gate_w_ref, inputs_ref, qkv_w_ref, slots_ref, act_ref, attn_w_ref,
+    gate_ref, qkv_ref, query_hot_ref, live_ref, member_ref, counts_ref, act_mean_ref, attn_wide_ref,
 ):
     rows, cols, channels = pair_ref.shape
     slab = inputs_ref.shape[0]
@@ -314,15 +314,27 @@
     token_col = column_of(token, slab)
     query_hot_ref[...] = (token_col == (iota(query_hot_ref.shape, 1) // BAND_PAD).astype(F32)).astype(F32)
     live_ref[...] = jnp.broadcast_to(column_of(alive, slab), live_ref.shape)
-    member_ref[...] = jnp.where(iota(member_ref.shape, 0).astype(F32) == token, alive, 0.0)
+    live_col = column_of(alive, slab)
+    for t in range(rows):
+        member_ref[t] = jnp.broadcast_to(jnp.where(token_col == t, live_col, 0.0), member_ref.shape[1:])
+    counts = jnp.sum(jnp.where(iota((SUBLANES, slab), 0).astype(F32) == token, alive, 0.0), axis=1, keepdims=True)
+    counts_ref[...] = jnp.broadcast_to(jnp.maximum(counts, 1.0), counts_ref.shape)
+    act_mean_ref[...] = jnp.broadcast_to(jnp.mean(act_ref[...].astype(F32), axis=1, keepdims=True), act_mean_ref.shape)
+    wide = attn_w_ref.shape[1]
+    attn_wide_ref[:, :wide] = attn_w_ref[...]
+    rest = jnp.broadcast_to(jnp.mean(attn_w_ref[...].astype(F32), axis=1, keepdims=True), attn_w_ref.shape)
+    for k in range(1, 4):
+        piece = rest.astype(BF16)
+        attn_wide_ref[:, k * wide : (k + 1) * wide] = piece
+        rest = rest - piece.astype(F32)
     normed = normalize(pair_ref[...].reshape(rows * cols, channels).astype(F32), 1).astype(BF16)
     gate_ref[...] = jax.nn.sigmoid(matmul(normed, gate_w_ref[...]))
 
 
 def triangle_kernel(n_row, rows, got_ref, *refs):
-    out_ref = refs[5]
-    taken, right_terms, staged = refs[11:]
-    prepare(*refs[:5], *refs[6:11])
+    out_ref = refs[7]
+    taken, right_terms, staged = refs[16:]
+    prepare(*refs[:7], *refs[8:16])
     taken[...] = got_ref[...].astype(F32)
     step = got_ref.shape[0] // n_row
     part = right_terms.shape[0]
@@ -349,8 +361,8 @@
 
 def finish_kernel(
     n_row, got_ref, pair_ref, out_w_ref, act_ref, slots_ref, bias_w_ref, gate_ref, qkv_ref, query_hot_ref, live_ref,
-    member_ref, qkv_w_ref, attn_w_ref, ffn_in_ref, ffn_out_ref, agg_ref,
-    pair_out, atom_out, token_out, taken, pair_new, atom_new, token_new, padded, products, values_ext, sems,
+    member_ref, counts_ref, act_mean_ref, attn_wide_ref, qkv_w_ref, ffn_in_ref, ffn_out_ref, agg_ref,
+    pair_out, atom_out, token_out, taken, pair_new, atom_new, token_new, padded, products, values_ext, key_slots, sems,
 ):
     me = lax.axis_index("row")
     rows, cols, channels = pair_ref.shape
@@ -383,11 +395,31 @@
         for at in (0, wide)
     )
     values_ext[...] = values
+    tag_at = [(step - RIM_ROWS + d * half + SIDE // n_row) + step * (SIDE % n_row) for d in range(2)]
+    before_tag, after_tag = (taken[at : at + 1] for at in tag_at)
+    own_tag = slots_ref[2:3]
+    lane = iota((1, LANES), 1)
     for w in range(windows):
         start = w * QUERY_WINDOW
         query = own[start : start + QUERY_WINDOW, :wide]
         split = jnp.concatenate([jnp.where(head_of == h, query, 0.0) for h in range(heads)], axis=0).astype(BF16)
-        products[w] = matmul(split, keys_ext[start : start + KEYS].astype(BF16), NT) * (1 / math.sqrt(head_size))
+        before_end = SIDE - start
+        own_end = before_end + slab
+        is_before, is_own = lane < before_end, lane < own_end
+        tag = jnp.where(
+            is_before,
+            pltpu.roll(before_tag, (SIDE - slab - start) % LANES, 1),
+            jnp.where(
+                is_own, pltpu.roll(own_tag, before_end % LANES, 1), pltpu.roll(after_tag, own_end % LANES, 1)
+            ),
+        )
+        offset = jnp.where(is_before, 0.0, jnp.where(is_own, 1.0 * rows, 2.0 * rows))
+        valid = tag > 0
+        key_slot = jnp.where(valid, tag - 1 + offset, -1.0)
+        key_slots[w : w + 1] = key_slot
+        product = matmul(split, keys_ext[start : start + KEYS].astype(BF16), NT) * (1 / math.sqrt(head_size))
+        product = jnp.where(valid, product, -1e30)
+        products[w] = product - jnp.max(product, axis=1, keepdims=True)
     for i in range(rows):
         update = matmul(normalize(sums[i], 0).astype(BF16), out_w_ref[...], TN)
         fresh = (pair_ref[i].astype(F32) + gate_ref[i * cols : (i + 1) * cols] * update).astype(BF16)
@@ -405,34 +437,16 @@
         band = [padded[i, pl.ds(SUBLANES + (me - 1) * rows, BAND_PAD)] for i in range(rows)]
         band = normalize(jnp.concatenate(band, axis=0), 1).astype(BF16)
         bias_rows = matmul(bias_w_ref[...], band, NT).astype(BF16).astype(F32)
-        tag_at = [(step - RIM_ROWS + d * half + SIDE // n_row) + step * (SIDE % n_row) for d in range(2)]
-        before_tag, after_tag = (taken[at : at + 1] for at in tag_at)
-        own_tag = slots_ref[2:3]
         query_hot = query_hot_ref[...]
         flat = query_hot.shape[1]
         slot = (iota((flat, KEYS), 0) % BAND_PAD).astype(F32)
-        lane = iota((1, LANES), 1)
         mixed = []
         for w in range(windows):
             start = w * QUERY_WINDOW
-            before_end = SIDE - start
-            own_end = before_end + slab
-            is_before, is_own = lane < before_end, lane < own_end
-            tag = jnp.where(
-                is_before,
-                pltpu.roll(before_tag, (SIDE - slab - start) % LANES, 1),
-                jnp.where(
-                    is_own, pltpu.roll(own_tag, before_end % LANES, 1), pltpu.roll(after_tag, own_end % LANES, 1)
-                ),
-            )
-            offset = jnp.where(is_before, 0.0, jnp.where(is_own, 1.0 * rows, 2.0 * rows))
-            valid = tag > 0
-            key_slot = jnp.where(valid, tag - 1 + offset, -1.0)
-            key_hot = (slot == key_slot).astype(BF16)
+            key_hot = (slot == key_slots[w : w + 1]).astype(BF16)
             hot = query_hot[start : start + QUERY_WINDOW]
             hot_bias = jnp.concatenate([hot * bias_rows[h : h + 1] for h in range(heads)], axis=0).astype(BF16)
-            scores = jnp.where(valid, products[w] + matmul(hot_bias, key_hot), -1e30)
-            powers = jnp.exp(scores - jnp.max(scores, axis=1, keepdims=True))
+            powers = jnp.exp(products[w] + matmul(hot_bias, key_hot))
             blend = matmul(powers.astype(BF16), values_ext[start : start + KEYS].astype(BF16))
             blend = blend / jnp.sum(powers, axis=1, keepdims=True)
             total = jnp.zeros((QUERY_WINDOW, wide), F32)
@@ -440,18 +454,24 @@
                 total = jnp.where(head_of == h, blend[h * QUERY_WINDOW : (h + 1) * QUERY_WINDOW], total)
             mixed.append(total)
         attended = jnp.concatenate(mixed, axis=0).astype(BF16)
-        middle = act_ref[...].astype(F32) + matmul(attended, attn_w_ref[...])
-        expanded = matmul(normalize(middle, 1).astype(BF16), ffn_in_ref[...])
+        mixture = matmul(attended, attn_wide_ref[...])
+        middle = act_ref[...].astype(F32) + mixture[:, :wide]
+        shift = mixture[:, wide : 2 * wide] + mixture[:, 2 * wide : 3 * wide] + mixture[:, 3 * wide :]
+        centred = middle - (act_mean_ref[...] + shift)
+        spread = jnp.mean(centred * centred, axis=1, keepdims=True)
+        expanded = matmul((centred * lax.rsqrt(spread + EPSILON)).astype(BF16), ffn_in_ref[...])
         hidden = ffn_out_ref.shape[0]
         inner = (jax.nn.silu(expanded[:, :hidden]) * expanded[:, hidden:]).astype(BF16)
         final = ((middle + matmul(inner, ffn_out_ref[...])) * live_ref[...]).astype(BF16)
         atom_new[...] = final
         atom_copy.start()
-        features = jnp.maximum(matmul(final, agg_ref[...]), 0.0).astype(BF16)
-        member = member_ref[...]
-        totals = matmul(member.astype(BF16), features)
-        counts = jnp.maximum(jnp.sum(member, axis=1, keepdims=True), 1.0)
-        token_new[...] = (totals / counts).astype(BF16)[:rows]
+        features = jnp.maximum(matmul(final, agg_ref[...]), 0.0).astype(BF16).astype(F32)
+        for b in range(features.shape[1] // LANES):
+            block = features[:, b * LANES : (b + 1) * LANES]
+            totals = [jnp.sum(block * member_ref[t], axis=0, keepdims=True) for t in range(rows)]
+            token_new[:, b * LANES : (b + 1) * LANES] = (
+                jnp.concatenate(totals, axis=0) / counts_ref[:rows]
+            ).astype(BF16)
         token_copy.start()
 
     pair_copy.wait()
@@ -520,10 +540,13 @@
             jax.ShapeDtypeStruct((slab, 3 * wide), BF16),
             jax.ShapeDtypeStruct((slab, rows * BAND_PAD), F32),
             jax.ShapeDtypeStruct((slab, wide), F32),
-            jax.ShapeDtypeStruct((SUBLANES, slab), F32),
+            jax.ShapeDtypeStruct((rows, slab, LANES), F32),
+            jax.ShapeDtypeStruct((SUBLANES, LANES), F32),
+            jax.ShapeDtypeStruct((slab, wide), F32),
+            jax.ShapeDtypeStruct((wide, 4 * wide), BF16),
         ),
-        in_specs=in_vmem(6),
-        out_specs=tuple(in_vmem(6)),
+        in_specs=in_vmem(8),
+        out_specs=tuple(in_vmem(9)),
         scratch_shapes=[
             pltpu.VMEM((sent, LANES), F32),
             pltpu.VMEM((part, cols, cols), F32),
@@ -532,7 +555,7 @@
         cost_estimate=cost(2 * width * width, 1 << 19),
         compiler_params=LIMIT,
         name="triangle",
-    )(got, pair, tri_gate_weight, inputs, qkv_weight, slots)
+    )(got, pair, tri_gate_weight, inputs, qkv_weight, slots, atom_act, attn_out_weight)
     back = exchange(sums, n_row)
     token_shape = (rows, agg_weight.shape[1])
     return pl.pallas_call(
@@ -542,7 +565,7 @@
             jax.ShapeDtypeStruct(atom_act.shape, BF16),
             jax.ShapeDtypeStruct(token_shape, BF16),
         ),
-        in_specs=in_vmem(16),
+        in_specs=in_vmem(18),
         out_specs=(pl.BlockSpec(memory_space=pltpu.HBM),) * 3,
         scratch_shapes=[
             pltpu.VMEM((back_rows, LANES), F32),
@@ -552,13 +575,14 @@
             pltpu.VMEM((rows, SUBLANES + cols + BAND_PAD, channels), F32),
             pltpu.VMEM((slab // QUERY_WINDOW, bias_weight.shape[1] * QUERY_WINDOW, KEYS), F32),
             pltpu.VMEM((slab + 2 * SIDE, wide), F32),
+            pltpu.VMEM((SUBLANES, LANES), F32),
             pltpu.SemaphoreType.DMA((3,)),
         ],
         cost_estimate=cost(4 * width * channels * channels, 1 << 20),
         compiler_params=LIMIT,
         name="finish",
     )(
-        back, pair, tri_out_weight, atom_act, slots, bias_rows, *prepared, qkv_weight, attn_out_weight, ffn_in_weight,
+        back, pair, tri_out_weight, atom_act, slots, bias_rows, *prepared, qkv_weight, ffn_in_weight,
         ffn_out_weight, agg_weight,
     )
 
@@ -580,6 +604,7 @@
         and SIDE < RIM_ROWS // 2 * n_row
         and 3 * rows <= BAND_PAD
         and rows <= SUBLANES
+        and slab // QUERY_WINDOW <= SUBLANES
         and SIDE <= slab <= LANES
         and slab % QUERY_WINDOW == 0
         and slab - QUERY_WINDOW <= SIDE

time: 34.7 us -> 34.5 us (level)
  no operation moved by 1% of the time
where the time goes in v5:
time: 34.5 us; the launch traced here: 34.3 us
  blocking collectives  29.2 us (85%)
  Pallas kernels  4.31 us (12%)
  between operations  0.72 us (2%)
    all_to_all x2, blocking collectives, exchange(): lax.all_to_all(grouped, 'row', split_axis=0, concat_axis=0, tiled=True)  29.2 us
    pallas_call x1, Pallas kernels, by_kernels(): pl.pallas_call(functools.partial(finish_kernel, n_row), out_shape=(jax.Sh...  2.23 us
    pallas_call x1, Pallas kernels, by_kernels(): pl.pallas_call(functools.partial(send_kernel, n_row), out_shape=(*(jax.Sh...  1.61 us

profile of v5, /device:TPU:0, one launch (start us, length us, event | category | flops | bytes accessed | tf_op | source)
XLA Modules:
  0.0 34.3 jit_solution(3767727273882039708)
XLA Ops:
  0.6 1.6 %send.1 = (bf16[4,128,128]{2,1,0:T(8,128)(2,1)S(1)}, bf16[64,128]{1,0:T(8,128)(2,1)S(1)}, bf16[4,128]{1,0:T(4,128)(2,1)S(1)}, bf16[1152,128]{1,0:T(8,128)(2,1)S(...) custom-call(bf16[4,128,128]{2,1,0:T(8,128)(2,1)} %pair_hbm.1, bf16[64,128]{1,0:T(8,128)(2,1)} %act_hbm.1, ...), custom_call_target="tpu_custom_call" | custom-call | flops 67108864 | bytes 1048576 | tf_op jit(solution)/shard_map/send/pallas_call | solution.py:515
  2.2 0.0 copy-start
  2.3 0.0 copy-start.4
  2.3 0.0 copy-start.5
  2.3 18.5 %all_to_all.10 = bf16[32,9,4,128]{3,2,1,0:T(4,128)(2,1)S(1)} all-to-all(bf16[32,9,4,128]{3,2,1,0:T(4,128)(2,1)S(1)} %bitcast.10), channel_id=1, replica_groups=mesh['groups'=1,'row'=32,'col'=1] {'row'}, dimensions={0} | all-to-all | bytes 589824 | tf_op jit(solution)/shard_map/all_to_all | solution.py:496
  20.8 0.0 copy-done
  20.8 0.0 copy-done.4
  20.8 0.0 copy-done.5
  20.8 0.5 %triangle.1 = (bf16[640,128]{1,0:T(8,128)(2,1)S(1)}, f32[512,128]{1,0:T(8,128)S(1)}, bf16[64,384]{1,0:T(8,128)(2,1)S(1)}, f32[64,64]{1,0:T(8,128)S(1)}, f32[64,1...) custom-call(bf16[1152,128]{1,0:T(8,128)(2,1)S(1)} %bitcast.8, ...), custom_call_target="tpu_custom_call" | custom-call | flops 524288 | bytes 524288 | tf_op jit(solution)/shard_map/triangle/pallas_call | solution.py:535
  21.3 0.0 copy-start.1
  21.3 0.0 copy-start.2
  21.3 0.0 copy-start.3
  21.3 0.0 copy-start.6
  21.4 10.7 %all_to_all.11 = bf16[32,5,4,128]{3,2,1,0:T(4,128)(2,1)S(1)} all-to-all(bf16[32,5,4,128]{3,2,1,0:T(4,128)(2,1)S(1)} %bitcast.11), channel_id=1, replica_groups=mesh['groups'=1,'row'=32,'col'=1] {'row'}, dimensions={0} | all-to-all | bytes 327680 | tf_op jit(solution)/shard_map/all_to_all | solution.py:496
  32.1 0.0 copy-done.1
  32.1 0.0 copy-done.2
  32.1 0.0 copy-done.3
  32.1 0.0 copy-done.6
  32.1 2.2 %finish.1 = (bf16[4,128,128]{2,1,0:T(8,128)(2,1)}, bf16[64,128]{1,0:T(8,128)(2,1)}, bf16[4,384]{1,0:T(4,128)(2,1)}) custom-call(bf16[640,128]{1,0:T(8,128)(2,1)S(1)} %bitcast.9, bf16[4,128,128]{2,1,0:T(8,128)(2,1)S(1)} %get-tuple-element.19.refs_0_.pair_ref, bf16[128,128]{1,0:T(8,128)(2,1)S(1)} %copy-done.6, ...), custom_call_target="tpu_custom_call" | custom-call | flops 33554432 | bytes 1048576 | tf_op jit(solution)/shard_map/finish/pallas_call | solution.py:561
Async XLA Ops:
  2.2 18.6 %copy-start = (bf16[128,384]{1,0:T(8,128)(2,1)S(1)}, bf16[128,384]{1,0:T(8,128)(2,1)}, u32[]{:S(2)}) copy-start(bf16[128,384]{1,0:T(8,128)(2,1)} %qkv_w_ref.1) | copy-start | bytes 294916
  2.3 18.6 %copy-start.4 = (bf16[128,128]{1,0:T(8,128)(2,1)S(1)}, bf16[128,128]{1,0:T(8,128)(2,1)}, u32[]{:S(2)}) copy-start(bf16[128,128]{1,0:T(8,128)(2,1)} %refs_1_.1) | copy-start | bytes 98308
  2.3 18.5 %copy-start.5 = (bf16[128,128]{1,0:T(8,128)(2,1)S(1)}, bf16[128,128]{1,0:T(8,128)(2,1)}, u32[]{:S(2)}) copy-start(bf16[128,128]{1,0:T(8,128)(2,1)} %refs_6_.1) | copy-start | bytes 98308
  21.3 10.8 %copy-start.1 = (bf16[128,512]{1,0:T(8,128)(2,1)S(1)}, bf16[128,512]{1,0:T(8,128)(2,1)}, u32[]{:S(2)}) copy-start(bf16[128,512]{1,0:T(8,128)(2,1)} %ffn_in_ref.1) | copy-start | bytes 393220
  21.3 10.8 %copy-start.2 = (bf16[128,384]{1,0:T(8,128)(2,1)S(1)}, bf16[128,384]{1,0:T(8,128)(2,1)}, u32[]{:S(2)}) copy-start(bf16[128,384]{1,0:T(8,128)(2,1)} %agg_ref.1) | copy-start | bytes 294916
  21.3 10.7 %copy-start.3 = (bf16[256,128]{1,0:T(8,128)(2,1)S(1)}, bf16[256,128]{1,0:T(8,128)(2,1)}, u32[]{:S(2)}) copy-start(bf16[256,128]{1,0:T(8,128)(2,1)} %ffn_out_ref.1) | copy-start | bytes 196612
  21.3 10.7 %copy-start.6 = (bf16[128,128]{1,0:T(8,128)(2,1)S(1)}, bf16[128,128]{1,0:T(8,128)(2,1)}, u32[]{:S(2)}) copy-start(bf16[128,128]{1,0:T(8,128)(2,1)} %out_w_ref.1) | copy-start | bytes 98308

commit v6 on v5

--- a/solution.py
+++ b/solution.py
@@ -246,7 +246,7 @@
 
 def send_kernel(
     n_row, pair_hbm, act_hbm, bias_w_hbm, in_w_hbm, cond_hbm, ada_w_hbm, mask_hbm, token_hbm, alive_hbm,
-    pair_ref, act_ref, bias_w_ref, out_ref, inputs_ref, slots_ref,
+    pair_ref, act_ref, bias_w_ref, out_ref, normed_ref, inputs_ref, slots_ref,
     in_w_ref, cond_ref, ada_w_ref, mask_ref, token_ref, alive_ref, staged, sems,
 ):
     sources = (pair_hbm, cond_hbm, act_hbm, mask_hbm, token_hbm, alive_hbm, bias_w_hbm, ada_w_hbm, in_w_hbm)
@@ -261,6 +261,7 @@
     width = rows * cols
     step = 2 * part * rows + RIM_ROWS
     normed = normalize(pair_ref[...].reshape(width, channels).astype(F32), 1).astype(BF16)
+    normed_ref[...] = normed
     for load in loads[1:]:
         load.wait()
     live = mask_ref[...].astype(F32)
@@ -303,10 +304,10 @@
 
 
 def prepare(
-    pair_ref, gate_w_ref, inputs_ref, qkv_w_ref, slots_ref, act_ref, attn_w_ref,
-    gate_ref, qkv_ref, query_hot_ref, live_ref, member_ref, counts_ref, act_mean_ref, attn_wide_ref,
+    inputs_ref, qkv_w_ref, slots_ref, act_ref, attn_w_ref,
+    qkv_ref, query_hot_ref, live_ref, member_ref, counts_ref, act_mean_ref, attn_wide_ref,
 ):
-    rows, cols, channels = pair_ref.shape
+    rows = member_ref.shape[0]
     slab = inputs_ref.shape[0]
     token = slots_ref[0:1, :slab]
     alive = slots_ref[1:2, :slab]
@@ -327,14 +328,10 @@
         piece = rest.astype(BF16)
         attn_wide_ref[:, k * wide : (k + 1) * wide] = piece
         rest = rest - piece.astype(F32)
-    normed = normalize(pair_ref[...].reshape(rows * cols, channels).astype(F32), 1).astype(BF16)
-    gate_ref[...] = jax.nn.sigmoid(matmul(normed, gate_w_ref[...]))
-
-
-def triangle_kernel(n_row, rows, got_ref, *refs):
-    out_ref = refs[7]
-    taken, right_terms, staged = refs[16:]
-    prepare(*refs[:7], *refs[8:16])
+
+
+def triangle_kernel(n_row, rows, got_ref, normed_ref, gate_w_ref, out_ref, gate_ref, taken, right_terms, staged):
+    gate_ref[...] = jax.nn.sigmoid(matmul(normed_ref[...], gate_w_ref[...]))
     taken[...] = got_ref[...].astype(F32)
     step = got_ref.shape[0] // n_row
     part = right_terms.shape[0]
@@ -360,9 +357,10 @@
 
 
 def finish_kernel(
-    n_row, got_ref, pair_ref, out_w_ref, act_ref, slots_ref, bias_w_ref, gate_ref, qkv_ref, query_hot_ref, live_ref,
-    member_ref, counts_ref, act_mean_ref, attn_wide_ref, qkv_w_ref, ffn_in_ref, ffn_out_ref, agg_ref,
-    pair_out, atom_out, token_out, taken, pair_new, atom_new, token_new, padded, products, values_ext, key_slots, sems,
+    n_row, got_ref, pair_ref, out_w_ref, act_ref, slots_ref, bias_w_ref, gate_ref, inputs_ref, qkv_w_ref, attn_w_ref,
+    ffn_in_ref, ffn_out_ref, agg_ref,
+    pair_out, atom_out, token_out, taken, pair_new, atom_new, token_new, padded, products, values_ext, key_slots,
+    qkv_ref, query_hot_ref, live_ref, member_ref, counts_ref, act_mean_ref, attn_wide_ref, sems,
 ):
     me = lax.axis_index("row")
     rows, cols, channels = pair_ref.shape
@@ -375,6 +373,10 @@
     head_of = iota((QUERY_WINDOW, wide), 1) // head_size
     windows = slab // QUERY_WINDOW
     taken[...] = got_ref[...].astype(F32)
+    prepare(
+        inputs_ref, qkv_w_ref, slots_ref, act_ref, attn_w_ref,
+        qkv_ref, query_hot_ref, live_ref, member_ref, counts_ref, act_mean_ref, attn_wide_ref,
+    )
     sums = [
         jnp.concatenate([taken[strided(q * rows + i, n_row, step)] for q in range(part)], axis=0) for i in range(rows)
     ]
@@ -512,16 +514,17 @@
     back_rows = n_row * (part * rows + RIM_ROWS)
     sources = (pair, atom_act, bias_weight.T, tri_in_weight, atom_cond, ada_weight, mask, token, alive)
     kept = 3
-    pair, atom_act, bias_rows, terms, inputs, slots = pl.pallas_call(
+    pair, atom_act, bias_rows, terms, normed, inputs, slots = pl.pallas_call(
         functools.partial(send_kernel, n_row),
         out_shape=(
             *(jax.ShapeDtypeStruct(a.shape, a.dtype) for a in sources[:kept]),
             jax.ShapeDtypeStruct((sent, LANES), BF16),
+            jax.ShapeDtypeStruct((width, channels), BF16),
             jax.ShapeDtypeStruct((slab, wide), BF16),
             jax.ShapeDtypeStruct((SUBLANES, LANES), F32),
         ),
         in_specs=[pl.BlockSpec(memory_space=pltpu.HBM)] * len(sources),
-        out_specs=tuple(in_vmem(kept + 3)),
+        out_specs=tuple(in_vmem(kept + 4)),
         scratch_shapes=[
             *(pltpu.VMEM(a.shape, a.dtype) for a in sources[kept:]),
             pltpu.VMEM((sent, LANES), F32),
@@ -532,21 +535,14 @@
         name="send",
     )(*in_hbm(sources))
     got = exchange(terms, n_row)
-    sums, *prepared = pl.pallas_call(
+    sums, gate = pl.pallas_call(
         functools.partial(triangle_kernel, n_row, rows),
         out_shape=(
             jax.ShapeDtypeStruct((back_rows, LANES), BF16),
             jax.ShapeDtypeStruct((width, channels), F32),
-            jax.ShapeDtypeStruct((slab, 3 * wide), BF16),
-            jax.ShapeDtypeStruct((slab, rows * BAND_PAD), F32),
-            jax.ShapeDtypeStruct((slab, wide), F32),
-            jax.ShapeDtypeStruct((rows, slab, LANES), F32),
-            jax.ShapeDtypeStruct((SUBLANES, LANES), F32),
-            jax.ShapeDtypeStruct((slab, wide), F32),
-            jax.ShapeDtypeStruct((wide, 4 * wide), BF16),
         ),
-        in_specs=in_vmem(8),
-        out_specs=tuple(in_vmem(9)),
+        in_specs=in_vmem(3),
+        out_specs=tuple(in_vmem(2)),
         scratch_shapes=[
             pltpu.VMEM((sent, LANES), F32),
             pltpu.VMEM((part, cols, cols), F32),
@@ -555,7 +551,7 @@
         cost_estimate=cost(2 * width * width, 1 << 19),
         compiler_params=LIMIT,
         name="triangle",
-    )(got, pair, tri_gate_weight, inputs, qkv_weight, slots, atom_act, attn_out_weight)
+    )(got, normed, tri_gate_weight)
     back = exchange(sums, n_row)
     token_shape = (rows, agg_weight.shape[1])
     return pl.pallas_call(
@@ -565,7 +561,7 @@
             jax.ShapeDtypeStruct(atom_act.shape, BF16),
             jax.ShapeDtypeStruct(token_shape, BF16),
         ),
-        in_specs=in_vmem(18),
+        in_specs=in_vmem(13),
         out_specs=(pl.BlockSpec(memory_space=pltpu.HBM),) * 3,
         scratch_shapes=[
             pltpu.VMEM((back_rows, LANES), F32),
@@ -576,14 +572,21 @@
             pltpu.VMEM((slab // QUERY_WINDOW, bias_weight.shape[1] * QUERY_WINDOW, KEYS), F32),
             pltpu.VMEM((slab + 2 * SIDE, wide), F32),
             pltpu.VMEM((SUBLANES, LANES), F32),
+            pltpu.VMEM((slab, 3 * wide), BF16),
+            pltpu.VMEM((slab, rows * BAND_PAD), F32),
+            pltpu.VMEM((slab, wide), F32),
+            pltpu.VMEM((rows, slab, LANES), F32),
+            pltpu.VMEM((SUBLANES, LANES), F32),
+            pltpu.VMEM((slab, wide), F32),
+            pltpu.VMEM((wide, 4 * wide), BF16),
             pltpu.SemaphoreType.DMA((3,)),
         ],
         cost_estimate=cost(4 * width * channels * channels, 1 << 20),
         compiler_params=LIMIT,
         name="finish",
     )(
-        back, pair, tri_out_weight, atom_act, slots, bias_rows, *prepared, qkv_weight, ffn_in_weight,
-        ffn_out_weight, agg_weight,
+        back, pair, tri_out_weight, atom_act, slots, bias_rows, gate, inputs, qkv_weight, attn_out_weight,
+        ffn_in_weight, ffn_out_weight, agg_weight,
     )
 
 

time: 34.5 us -> 34.4 us (level)
  no operation moved by 1% of the time
where the time goes in v6:
time: 34.4 us; the launch traced here: 34.1 us
  blocking collectives  29.2 us (85%)
  Pallas kernels  4.13 us (12%)
  between operations  0.72 us (2%)
    all_to_all x2, blocking collectives, exchange(): lax.all_to_all(grouped, 'row', split_axis=0, concat_axis=0, tiled=True)  29.2 us
    pallas_call x1, Pallas kernels, by_kernels(): pl.pallas_call(functools.partial(finish_kernel, n_row), out_shape=(jax.Sh...  2.24 us
    pallas_call x1, Pallas kernels, by_kernels(): pl.pallas_call(functools.partial(send_kernel, n_row), out_shape=(*(jax.Sh...  1.61 us

profile of v6, /device:TPU:0, one launch (start us, length us, event | category | flops | bytes accessed | tf_op | source)
XLA Modules:
  0.0 34.1 jit_solution(7060742568124941960)
XLA Ops:
  0.6 1.6 %send.1 = (bf16[4,128,128]{2,1,0:T(8,128)(2,1)S(1)}, bf16[64,128]{1,0:T(8,128)(2,1)S(1)}, bf16[4,128]{1,0:T(4,128)(2,1)S(1)}, bf16[1152,128]{1,0:T(8,128)(2,1)S(...) custom-call(bf16[4,128,128]{2,1,0:T(8,128)(2,1)} %pair_hbm.1, ...), custom_call_target="tpu_custom_call" | custom-call | flops 67108864 | bytes 1048576 | tf_op jit(solution)/shard_map/send/pallas_call | solution.py:517
  2.3 0.0 copy-start.4
  2.3 18.5 %all_to_all.10 = bf16[32,9,4,128]{3,2,1,0:T(4,128)(2,1)S(1)} all-to-all(bf16[32,9,4,128]{3,2,1,0:T(4,128)(2,1)S(1)} %bitcast.10), channel_id=1, replica_groups=mesh['groups'=1,'row'=32,'col'=1] {'row'}, dimensions={0} | all-to-all | bytes 589824 | tf_op jit(solution)/shard_map/all_to_all | solution.py:498
  20.8 0.0 copy-done.4
  20.8 0.0 copy-start.3
  20.8 0.0 copy-start.5
  20.8 0.0 copy-start.6
  20.8 0.3 triangle.1
  21.1 0.0 copy-start
  21.1 0.0 copy-start.1
  21.1 0.0 copy-start.2
  21.1 10.7 %all_to_all.11 = bf16[32,5,4,128]{3,2,1,0:T(4,128)(2,1)S(1)} all-to-all(bf16[32,5,4,128]{3,2,1,0:T(4,128)(2,1)S(1)} %bitcast.11), channel_id=1, replica_groups=mesh['groups'=1,'row'=32,'col'=1] {'row'}, dimensions={0} | all-to-all | bytes 327680 | tf_op jit(solution)/shard_map/all_to_all | solution.py:498
  31.8 0.0 copy-done.3
  31.8 0.0 copy-done.5
  31.8 0.0 copy-done.6
  31.9 0.0 copy-done
  31.9 0.0 copy-done.1
  31.9 0.0 copy-done.2
  31.9 2.2 %finish.1 = (bf16[4,128,128]{2,1,0:T(8,128)(2,1)}, bf16[64,128]{1,0:T(8,128)(2,1)}, bf16[4,384]{1,0:T(4,128)(2,1)}) custom-call(bf16[640,128]{1,0:T(8,128)(2,1)S(1)} %bitcast.9, bf16[4,128,128]{2,1,0:T(8,128)(2,1)S(1)} %get-tuple-element.15.pair_ref, bf16[128,128]{1,0:T(8,128)(2,1)S(1)} %copy-done.5, bf16[64,128]{1,0:T(8,128)(2,1)S(1)} %get-tuple-element.16.act_ref, ...), custom_call_target="tpu_custom_call" | custom-call | flops 33554432 | bytes 1048576 | tf_op jit(solution)/shard_map/finish/pallas_call | solution.py:557
Async XLA Ops:
  2.3 18.5 %copy-start.4 = (bf16[128,128]{1,0:T(8,128)(2,1)S(1)}, bf16[128,128]{1,0:T(8,128)(2,1)}, u32[]{:S(2)}) copy-start(bf16[128,128]{1,0:T(8,128)(2,1)} %gate_w_ref.1) | copy-start | bytes 98308
  20.8 11.0 %copy-start.3 = (bf16[256,128]{1,0:T(8,128)(2,1)S(1)}, bf16[256,128]{1,0:T(8,128)(2,1)}, u32[]{:S(2)}) copy-start(bf16[256,128]{1,0:T(8,128)(2,1)} %ffn_out_ref.1) | copy-start | bytes 196612
  20.8 11.0 %copy-start.5 = (bf16[128,128]{1,0:T(8,128)(2,1)S(1)}, bf16[128,128]{1,0:T(8,128)(2,1)}, u32[]{:S(2)}) copy-start(bf16[128,128]{1,0:T(8,128)(2,1)} %out_w_ref.1) | copy-start | bytes 98308
  20.8 11.0 %copy-start.6 = (bf16[128,128]{1,0:T(8,128)(2,1)S(1)}, bf16[128,128]{1,0:T(8,128)(2,1)}, u32[]{:S(2)}) copy-start(bf16[128,128]{1,0:T(8,128)(2,1)} %attn_w_ref.1) | copy-start | bytes 98308
  21.1 10.8 %copy-start = (bf16[128,512]{1,0:T(8,128)(2,1)S(1)}, bf16[128,512]{1,0:T(8,128)(2,1)}, u32[]{:S(2)}) copy-start(bf16[128,512]{1,0:T(8,128)(2,1)} %ffn_in_ref.1) | copy-start | bytes 393220
  21.1 10.8 %copy-start.1 = (bf16[128,384]{1,0:T(8,128)(2,1)S(1)}, bf16[128,384]{1,0:T(8,128)(2,1)}, u32[]{:S(2)}) copy-start(bf16[128,384]{1,0:T(8,128)(2,1)} %qkv_w_ref.1) | copy-start | bytes 294916
  21.1 10.8 %copy-start.2 = (bf16[128,384]{1,0:T(8,128)(2,1)S(1)}, bf16[128,384]{1,0:T(8,128)(2,1)}, u32[]{:S(2)}) copy-start(bf16[128,384]{1,0:T(8,128)(2,1)} %agg_ref.1) | copy-start | bytes 294916

commit v7 on v4

--- a/solution.py
+++ b/solution.py
@@ -246,7 +246,7 @@
 
 def send_kernel(
     n_row, pair_hbm, act_hbm, bias_w_hbm, in_w_hbm, cond_hbm, ada_w_hbm, mask_hbm, token_hbm, alive_hbm,
-    pair_ref, act_ref, bias_w_ref, out_ref, inputs_ref, slots_ref,
+    pair_ref, act_ref, bias_w_ref, out_ref, normed_ref, inputs_ref, slots_ref,
     in_w_ref, cond_ref, ada_w_ref, mask_ref, token_ref, alive_ref, staged, sems,
 ):
     sources = (pair_hbm, cond_hbm, act_hbm, mask_hbm, token_hbm, alive_hbm, bias_w_hbm, ada_w_hbm, in_w_hbm)
@@ -261,6 +261,7 @@
     width = rows * cols
     step = 2 * part * rows + RIM_ROWS
     normed = normalize(pair_ref[...].reshape(width, channels).astype(F32), 1).astype(BF16)
+    normed_ref[...] = normed
     for load in loads[1:]:
         load.wait()
     live = mask_ref[...].astype(F32)
@@ -302,27 +303,29 @@
     out_ref[...] = staged[...].astype(BF16)
 
 
-def prepare(
-    pair_ref, gate_w_ref, inputs_ref, qkv_w_ref, slots_ref,
-    gate_ref, qkv_ref, query_hot_ref, live_ref, member_ref,
-):
-    rows, cols, channels = pair_ref.shape
-    slab = inputs_ref.shape[0]
+def tables(inputs_ref, qkv_w_ref, slots_ref, act_ref, attn_w_ref, rows):
+    slab, wide = inputs_ref.shape
     token = slots_ref[0:1, :slab]
     alive = slots_ref[1:2, :slab]
-    qkv_ref[...] = matmul(inputs_ref[...], qkv_w_ref[...]).astype(BF16)
+    own = matmul(inputs_ref[...], qkv_w_ref[...]).astype(BF16).astype(F32)
     token_col = column_of(token, slab)
-    query_hot_ref[...] = (token_col == (iota(query_hot_ref.shape, 1) // BAND_PAD).astype(F32)).astype(F32)
-    live_ref[...] = jnp.broadcast_to(column_of(alive, slab), live_ref.shape)
-    member_ref[...] = jnp.where(iota(member_ref.shape, 0).astype(F32) == token, alive, 0.0)
-    normed = normalize(pair_ref[...].reshape(rows * cols, channels).astype(F32), 1).astype(BF16)
-    gate_ref[...] = jax.nn.sigmoid(matmul(normed, gate_w_ref[...]))
-
-
-def triangle_kernel(n_row, rows, got_ref, *refs):
-    out_ref = refs[5]
-    taken, right_terms, staged = refs[11:]
-    prepare(*refs[:5], *refs[6:11])
+    live_col = column_of(alive, slab)
+    query_hot = (token_col == (iota((slab, rows * BAND_PAD), 1) // BAND_PAD).astype(F32)).astype(F32)
+    members = [jnp.broadcast_to(jnp.where(token_col == t, live_col, 0.0), (slab, LANES)) for t in range(rows)]
+    counts = jnp.sum(jnp.where(iota((SUBLANES, slab), 0).astype(F32) == token, alive, 0.0), axis=1, keepdims=True)
+    act_mean = jnp.mean(act_ref[...].astype(F32), axis=1, keepdims=True)
+    attn_w = attn_w_ref[...]
+    pieces = [attn_w]
+    rest = jnp.broadcast_to(jnp.mean(attn_w.astype(F32), axis=1, keepdims=True), attn_w.shape)
+    for _ in range(3):
+        pieces.append(rest.astype(BF16))
+        rest = rest - pieces[-1].astype(F32)
+    attn_wide = jnp.concatenate(pieces, axis=1)
+    return own, query_hot, live_col, members, jnp.maximum(counts, 1.0), act_mean, attn_wide
+
+
+def triangle_kernel(n_row, rows, got_ref, normed_ref, gate_w_ref, out_ref, gate_ref, taken, right_terms, staged):
+    gate_ref[...] = jax.nn.sigmoid(matmul(normed_ref[...], gate_w_ref[...]))
     taken[...] = got_ref[...].astype(F32)
     step = got_ref.shape[0] // n_row
     part = right_terms.shape[0]
@@ -348,9 +351,9 @@
 
 
 def finish_kernel(
-    n_row, got_ref, pair_ref, out_w_ref, act_ref, slots_ref, bias_w_ref, gate_ref, qkv_ref, query_hot_ref, live_ref,
-    member_ref, qkv_w_ref, attn_w_ref, ffn_in_ref, ffn_out_ref, agg_ref,
-    pair_out, atom_out, token_out, taken, pair_new, atom_new, token_new, padded, products, values_ext, sems,
+    n_row, got_ref, pair_ref, out_w_ref, act_ref, slots_ref, bias_w_ref, gate_ref, inputs_ref, qkv_w_ref, attn_w_ref,
+    ffn_in_ref, ffn_out_ref, agg_ref,
+    pair_out, atom_out, token_out, taken, pair_new, atom_new, token_new, padded, sems,
 ):
     me = lax.axis_index("row")
     rows, cols, channels = pair_ref.shape
@@ -360,36 +363,10 @@
     slab, wide = act_ref.shape
     heads = bias_w_ref.shape[0]
     head_size = wide // heads
-    head_of = iota((QUERY_WINDOW, wide), 1) // head_size
-    windows = slab // QUERY_WINDOW
     taken[...] = got_ref[...].astype(F32)
-    sums = [
-        jnp.concatenate([taken[strided(q * rows + i, n_row, step)] for q in range(part)], axis=0) for i in range(rows)
-    ]
-    outer = jnp.concatenate(
-        [
-            taken[strided(step - RIM_ROWS + d * half + s, n_row, step)][: min(n_row, SIDE - s * n_row)]
-            for d in range(2)
-            for s in range(half)
-        ],
-        axis=0,
-    ).astype(BF16)
-    outer = matmul(outer, qkv_w_ref[:, wide:]).astype(BF16).astype(F32)
-    own = qkv_ref[...].astype(F32)
-    keys_ext, values = (
-        jnp.concatenate(
-            [outer[:SIDE, at : at + wide], own[:, wide + at : 2 * wide + at], outer[SIDE:, at : at + wide]], axis=0
-        )
-        for at in (0, wide)
-    )
-    values_ext[...] = values
-    for w in range(windows):
-        start = w * QUERY_WINDOW
-        query = own[start : start + QUERY_WINDOW, :wide]
-        split = jnp.concatenate([jnp.where(head_of == h, query, 0.0) for h in range(heads)], axis=0).astype(BF16)
-        products[w] = matmul(split, keys_ext[start : start + KEYS].astype(BF16), NT) * (1 / math.sqrt(head_size))
     for i in range(rows):
-        update = matmul(normalize(sums[i], 0).astype(BF16), out_w_ref[...], TN)
+        sums = jnp.concatenate([taken[strided(q * rows + i, n_row, step)] for q in range(part)], axis=0)
+        update = matmul(normalize(sums, 0).astype(BF16), out_w_ref[...], TN)
         fresh = (pair_ref[i].astype(F32) + gate_ref[i * cols : (i + 1) * cols] * update).astype(BF16)
         pair_new[i] = fresh
         padded[i, :SUBLANES] = jnp.zeros((SUBLANES, channels), F32)
@@ -405,15 +382,33 @@
         band = [padded[i, pl.ds(SUBLANES + (me - 1) * rows, BAND_PAD)] for i in range(rows)]
         band = normalize(jnp.concatenate(band, axis=0), 1).astype(BF16)
         bias_rows = matmul(bias_w_ref[...], band, NT).astype(BF16).astype(F32)
+        own, query_hot, live_col, members, counts, act_mean, attn_wide = tables(
+            inputs_ref, qkv_w_ref, slots_ref, act_ref, attn_w_ref, rows
+        )
+        outer = jnp.concatenate(
+            [
+                taken[strided(step - RIM_ROWS + d * half + s, n_row, step)][: min(n_row, SIDE - s * n_row)]
+                for d in range(2)
+                for s in range(half)
+            ],
+            axis=0,
+        ).astype(BF16)
+        outer = matmul(outer, qkv_w_ref[:, wide:]).astype(BF16).astype(F32)
+        keys_ext, values_ext = (
+            jnp.concatenate(
+                [outer[:SIDE, at : at + wide], own[:, wide + at : 2 * wide + at], outer[SIDE:, at : at + wide]], axis=0
+            ).astype(BF16)
+            for at in (0, wide)
+        )
         tag_at = [(step - RIM_ROWS + d * half + SIDE // n_row) + step * (SIDE % n_row) for d in range(2)]
         before_tag, after_tag = (taken[at : at + 1] for at in tag_at)
         own_tag = slots_ref[2:3]
-        query_hot = query_hot_ref[...]
+        lane = iota((1, LANES), 1)
         flat = query_hot.shape[1]
         slot = (iota((flat, KEYS), 0) % BAND_PAD).astype(F32)
-        lane = iota((1, LANES), 1)
+        head_of = iota((QUERY_WINDOW, wide), 1) // head_size
         mixed = []
-        for w in range(windows):
+        for w in range(slab // QUERY_WINDOW):
             start = w * QUERY_WINDOW
             before_end = SIDE - start
             own_end = before_end + slab
@@ -429,29 +424,39 @@
             valid = tag > 0
             key_slot = jnp.where(valid, tag - 1 + offset, -1.0)
             key_hot = (slot == key_slot).astype(BF16)
+            query = own[start : start + QUERY_WINDOW, :wide]
+            split = jnp.concatenate([jnp.where(head_of == h, query, 0.0) for h in range(heads)], axis=0).astype(BF16)
+            product = matmul(split, keys_ext[start : start + KEYS], NT) * (1 / math.sqrt(head_size))
+            product = jnp.where(valid, product, -1e30)
+            product = product - jnp.max(product, axis=1, keepdims=True)
             hot = query_hot[start : start + QUERY_WINDOW]
             hot_bias = jnp.concatenate([hot * bias_rows[h : h + 1] for h in range(heads)], axis=0).astype(BF16)
-            scores = jnp.where(valid, products[w] + matmul(hot_bias, key_hot), -1e30)
-            powers = jnp.exp(scores - jnp.max(scores, axis=1, keepdims=True))
-            blend = matmul(powers.astype(BF16), values_ext[start : start + KEYS].astype(BF16))
+            powers = jnp.exp(product + matmul(hot_bias, key_hot))
+            blend = matmul(powers.astype(BF16), values_ext[start : start + KEYS])
             blend = blend / jnp.sum(powers, axis=1, keepdims=True)
             total = jnp.zeros((QUERY_WINDOW, wide), F32)
             for h in range(heads):
                 total = jnp.where(head_of == h, blend[h * QUERY_WINDOW : (h + 1) * QUERY_WINDOW], total)
             mixed.append(total)
         attended = jnp.concatenate(mixed, axis=0).astype(BF16)
-        middle = act_ref[...].astype(F32) + matmul(attended, attn_w_ref[...])
-        expanded = matmul(normalize(middle, 1).astype(BF16), ffn_in_ref[...])
+        mixture = matmul(attended, attn_wide)
+        middle = act_ref[...].astype(F32) + mixture[:, :wide]
+        shift = mixture[:, wide : 2 * wide] + mixture[:, 2 * wide : 3 * wide] + mixture[:, 3 * wide :]
+        centred = middle - (act_mean + shift)
+        spread = jnp.mean(centred * centred, axis=1, keepdims=True)
+        expanded = matmul((centred * lax.rsqrt(spread + EPSILON)).astype(BF16), ffn_in_ref[...])
         hidden = ffn_out_ref.shape[0]
         inner = (jax.nn.silu(expanded[:, :hidden]) * expanded[:, hidden:]).astype(BF16)
-        final = ((middle + matmul(inner, ffn_out_ref[...])) * live_ref[...]).astype(BF16)
+        final = ((middle + matmul(inner, ffn_out_ref[...])) * live_col).astype(BF16)
         atom_new[...] = final
         atom_copy.start()
-        features = jnp.maximum(matmul(final, agg_ref[...]), 0.0).astype(BF16)
-        member = member_ref[...]
-        totals = matmul(member.astype(BF16), features)
-        counts = jnp.maximum(jnp.sum(member, axis=1, keepdims=True), 1.0)
-        token_new[...] = (totals / counts).astype(BF16)[:rows]
+        features = jnp.maximum(matmul(final, agg_ref[...]), 0.0).astype(BF16).astype(F32)
+        for b in range(features.shape[1] // LANES):
+            block = features[:, b * LANES : (b + 1) * LANES]
+            totals = [jnp.sum(block * members[t], axis=0, keepdims=True) for t in range(rows)]
+            token_new[:, b * LANES : (b + 1) * LANES] = (
+                jnp.concatenate(totals, axis=0) / counts[:rows]
+            ).astype(BF16)
         token_copy.start()
 
     pair_copy.wait()
@@ -492,16 +497,17 @@
     back_rows = n_row * (part * rows + RIM_ROWS)
     sources = (pair, atom_act, bias_weight.T, tri_in_weight, atom_cond, ada_weight, mask, token, alive)
     kept = 3
-    pair, atom_act, bias_rows, terms, inputs, slots = pl.pallas_call(
+    pair, atom_act, bias_rows, terms, normed, inputs, slots = pl.pallas_call(
         functools.partial(send_kernel, n_row),
         out_shape=(
             *(jax.ShapeDtypeStruct(a.shape, a.dtype) for a in sources[:kept]),
             jax.ShapeDtypeStruct((sent, LANES), BF16),
+            jax.ShapeDtypeStruct((width, channels), BF16),
             jax.ShapeDtypeStruct((slab, wide), BF16),
             jax.ShapeDtypeStruct((SUBLANES, LANES), F32),
         ),
         in_specs=[pl.BlockSpec(memory_space=pltpu.HBM)] * len(sources),
-        out_specs=tuple(in_vmem(kept + 3)),
+        out_specs=tuple(in_vmem(kept + 4)),
         scratch_shapes=[
             *(pltpu.VMEM(a.shape, a.dtype) for a in sources[kept:]),
             pltpu.VMEM((sent, LANES), F32),
@@ -512,18 +518,14 @@
         name="send",
     )(*in_hbm(sources))
     got = exchange(terms, n_row)
-    sums, *prepared = pl.pallas_call(
+    sums, gate = pl.pallas_call(
         functools.partial(triangle_kernel, n_row, rows),
         out_shape=(
             jax.ShapeDtypeStruct((back_rows, LANES), BF16),
             jax.ShapeDtypeStruct((width, channels), F32),
-            jax.ShapeDtypeStruct((slab, 3 * wide), BF16),
-            jax.ShapeDtypeStruct((slab, rows * BAND_PAD), F32),
-            jax.ShapeDtypeStruct((slab, wide), F32),
-            jax.ShapeDtypeStruct((SUBLANES, slab), F32),
         ),
-        in_specs=in_vmem(6),
-        out_specs=tuple(in_vmem(6)),
+        in_specs=in_vmem(3),
+        out_specs=tuple(in_vmem(2)),
         scratch_shapes=[
             pltpu.VMEM((sent, LANES), F32),
             pltpu.VMEM((part, cols, cols), F32),
@@ -532,7 +534,7 @@
         cost_estimate=cost(2 * width * width, 1 << 19),
         compiler_params=LIMIT,
         name="triangle",
-    )(got, pair, tri_gate_weight, inputs, qkv_weight, slots)
+    )(got, normed, tri_gate_weight)
     back = exchange(sums, n_row)
     token_shape = (rows, agg_weight.shape[1])
     return pl.pallas_call(
@@ -542,7 +544,7 @@
             jax.ShapeDtypeStruct(atom_act.shape, BF16),
             jax.ShapeDtypeStruct(token_shape, BF16),
         ),
-        in_specs=in_vmem(16),
+        in_specs=in_vmem(13),
         out_specs=(pl.BlockSpec(memory_space=pltpu.HBM),) * 3,
         scratch_shapes=[
             pltpu.VMEM((back_rows, LANES), F32),
@@ -550,16 +552,14 @@
             pltpu.VMEM(atom_act.shape, BF16),
             pltpu.VMEM(token_shape, BF16),
             pltpu.VMEM((rows, SUBLANES + cols + BAND_PAD, channels), F32),
-            pltpu.VMEM((slab // QUERY_WINDOW, bias_weight.shape[1] * QUERY_WINDOW, KEYS), F32),
-            pltpu.VMEM((slab + 2 * SIDE, wide), F32),
             pltpu.SemaphoreType.DMA((3,)),
         ],
         cost_estimate=cost(4 * width * channels * channels, 1 << 20),
         compiler_params=LIMIT,
         name="finish",
     )(
-        back, pair, tri_out_weight, atom_act, slots, bias_rows, *prepared, qkv_weight, attn_out_weight, ffn_in_weight,
-        ffn_out_weight, agg_weight,
+        back, pair, tri_out_weight, atom_act, slots, bias_rows, gate, inputs, qkv_weight, attn_out_weight,
+        ffn_in_weight, ffn_out_weight, agg_weight,
     )
 
 
@@ -580,6 +580,7 @@
         and SIDE < RIM_ROWS // 2 * n_row
         and 3 * rows <= BAND_PAD
         and rows <= SUBLANES
+        and slab // QUERY_WINDOW <= SUBLANES
         and SIDE <= slab <= LANES
         and slab % QUERY_WINDOW == 0
         and slab - QUERY_WINDOW <= SIDE

time: 34.7 us -> 34.4 us (level)
  no operation moved by 1% of the time
where the time goes in v7:
time: 34.4 us; the launch traced here: 34.2 us
  blocking collectives  29.2 us (85%)
  Pallas kernels  4.17 us (12%)
  between operations  0.72 us (2%)
    all_to_all x2, blocking collectives, exchange(): lax.all_to_all(grouped, 'row', split_axis=0, concat_axis=0, tiled=True)  29.2 us
    pallas_call x1, Pallas kernels, by_kernels(): pl.pallas_call(functools.partial(finish_kernel, n_row), out_shape=(jax.Sh...  2.28 us
    pallas_call x1, Pallas kernels, by_kernels(): pl.pallas_call(functools.partial(send_kernel, n_row), out_shape=(*(jax.Sh...  1.61 us

profile of v7, /device:TPU:0, one launch (start us, length us, event | category | flops | bytes accessed | tf_op | source)
XLA Modules:
  0.0 34.2 jit_solution(2965130746770592130)
XLA Ops:
  0.6 1.6 %send.1 = (bf16[4,128,128]{2,1,0:T(8,128)(2,1)S(1)}, bf16[64,128]{1,0:T(8,128)(2,1)S(1)}, bf16[4,128]{1,0:T(4,128)(2,1)S(1)}, bf16[1152,128]{1,0:T(8,128)(2,1)S(...) custom-call(bf16[4,128,128]{2,1,0:T(8,128)(2,1)} %pair_hbm.1, ...), custom_call_target="tpu_custom_call" | custom-call | flops 67108864 | bytes 1048576 | tf_op jit(solution)/shard_map/send/pallas_call | solution.py:500
  2.3 0.0 copy-start.4
  2.3 18.5 %all_to_all.10 = bf16[32,9,4,128]{3,2,1,0:T(4,128)(2,1)S(1)} all-to-all(bf16[32,9,4,128]{3,2,1,0:T(4,128)(2,1)S(1)} %bitcast.10), channel_id=1, replica_groups=mesh['groups'=1,'row'=32,'col'=1] {'row'}, dimensions={0} | all-to-all | bytes 589824 | tf_op jit(solution)/shard_map/all_to_all | solution.py:481
  20.8 0.0 copy-done.4
  20.8 0.0 copy-start.3
  20.8 0.0 copy-start.5
  20.8 0.0 copy-start.6
  20.8 0.3 triangle.1
  21.1 0.0 copy-start
  21.1 0.0 copy-start.1
  21.1 0.0 copy-start.2
  21.1 10.7 %all_to_all.11 = bf16[32,5,4,128]{3,2,1,0:T(4,128)(2,1)S(1)} all-to-all(bf16[32,5,4,128]{3,2,1,0:T(4,128)(2,1)S(1)} %bitcast.11), channel_id=1, replica_groups=mesh['groups'=1,'row'=32,'col'=1] {'row'}, dimensions={0} | all-to-all | bytes 327680 | tf_op jit(solution)/shard_map/all_to_all | solution.py:481
  31.8 0.0 copy-done.3
  31.8 0.0 copy-done.5
  31.8 0.0 copy-done.6
  31.9 0.0 copy-done
  31.9 0.0 copy-done.1
  31.9 0.0 copy-done.2
  31.9 2.3 %finish.1 = (bf16[4,128,128]{2,1,0:T(8,128)(2,1)}, bf16[64,128]{1,0:T(8,128)(2,1)}, bf16[4,384]{1,0:T(4,128)(2,1)}) custom-call(bf16[640,128]{1,0:T(8,128)(2,1)S(1)} %bitcast.9, bf16[4,128,128]{2,1,0:T(8,128)(2,1)S(1)} %get-tuple-element.15.pair_ref, bf16[128,128]{1,0:T(8,128)(2,1)S(1)} %copy-done.5, bf16[64,128]{1,0:T(8,128)(2,1)S(1)} %get-tuple-element.16.act_ref, ...), custom_call_target="tpu_custom_call" | custom-call | flops 33554432 | bytes 1048576 | tf_op jit(solution)/shard_map/finish/pallas_call | solution.py:540
Async XLA Ops:
  2.3 18.5 %copy-start.4 = (bf16[128,128]{1,0:T(8,128)(2,1)S(1)}, bf16[128,128]{1,0:T(8,128)(2,1)}, u32[]{:S(2)}) copy-start(bf16[128,128]{1,0:T(8,128)(2,1)} %gate_w_ref.1) | copy-start | bytes 98308
  20.8 11.0 %copy-start.3 = (bf16[256,128]{1,0:T(8,128)(2,1)S(1)}, bf16[256,128]{1,0:T(8,128)(2,1)}, u32[]{:S(2)}) copy-start(bf16[256,128]{1,0:T(8,128)(2,1)} %ffn_out_ref.1) | copy-start | bytes 196612
  20.8 11.0 %copy-start.5 = (bf16[128,128]{1,0:T(8,128)(2,1)S(1)}, bf16[128,128]{1,0:T(8,128)(2,1)}, u32[]{:S(2)}) copy-start(bf16[128,128]{1,0:T(8,128)(2,1)} %out_w_ref.1) | copy-start | bytes 98308
  20.8 11.0 %copy-start.6 = (bf16[128,128]{1,0:T(8,128)(2,1)S(1)}, bf16[128,128]{1,0:T(8,128)(2,1)}, u32[]{:S(2)}) copy-start(bf16[128,128]{1,0:T(8,128)(2,1)} %attn_w_ref.1) | copy-start | bytes 98308
  21.1 10.8 %copy-start = (bf16[128,512]{1,0:T(8,128)(2,1)S(1)}, bf16[128,512]{1,0:T(8,128)(2,1)}, u32[]{:S(2)}) copy-start(bf16[128,512]{1,0:T(8,128)(2,1)} %ffn_in_ref.1) | copy-start | bytes 393220
  21.1 10.8 %copy-start.1 = (bf16[128,384]{1,0:T(8,128)(2,1)S(1)}, bf16[128,384]{1,0:T(8,128)(2,1)}, u32[]{:S(2)}) copy-start(bf16[128,384]{1,0:T(8,128)(2,1)} %qkv_w_ref.1) | copy-start | bytes 294916
  21.1 10.8 %copy-start.2 = (bf16[128,384]{1,0:T(8,128)(2,1)S(1)}, bf16[128,384]{1,0:T(8,128)(2,1)}, u32[]{:S(2)}) copy-start(bf16[128,384]{1,0:T(8,128)(2,1)} %agg_ref.1) | copy-start | bytes 294916

commit v8 on v7

--- a/solution.py
+++ b/solution.py
@@ -380,8 +380,15 @@
     @pl.when(me >= 0)
     def _():
         band = [padded[i, pl.ds(SUBLANES + (me - 1) * rows, BAND_PAD)] for i in range(rows)]
-        band = normalize(jnp.concatenate(band, axis=0), 1).astype(BF16)
-        bias_rows = matmul(bias_w_ref[...], band, NT).astype(BF16).astype(F32)
+        band = jnp.concatenate(band, axis=0)
+        band = band - jnp.mean(band, axis=1, keepdims=True)
+        squares = band * band
+        high = squares.astype(BF16)
+        low = (squares - high.astype(F32)).astype(BF16)
+        share = jnp.full(bias_w_ref.shape, 1 / channels, BF16)
+        spread = matmul(share, high, NT) + matmul(share, low, NT)
+        bias_rows = matmul(bias_w_ref[...], band.astype(BF16), NT) * lax.rsqrt(spread + EPSILON)
+        bias_rows = bias_rows.astype(BF16).astype(F32)
         own, query_hot, live_col, members, counts, act_mean, attn_wide = tables(
             inputs_ref, qkv_w_ref, slots_ref, act_ref, attn_w_ref, rows
         )
@@ -444,7 +451,7 @@
         shift = mixture[:, wide : 2 * wide] + mixture[:, 2 * wide : 3 * wide] + mixture[:, 3 * wide :]
         centred = middle - (act_mean + shift)
         spread = jnp.mean(centred * centred, axis=1, keepdims=True)
-        expanded = matmul((centred * lax.rsqrt(spread + EPSILON)).astype(BF16), ffn_in_ref[...])
+        expanded = matmul(centred.astype(BF16), ffn_in_ref[...]) * lax.rsqrt(spread + EPSILON)
         hidden = ffn_out_ref.shape[0]
         inner = (jax.nn.silu(expanded[:, :hidden]) * expanded[:, hidden:]).astype(BF16)
         final = ((middle + matmul(inner, ffn_out_ref[...])) * live_col).astype(BF16)

time: 34.4 us -> 34.4 us (level)
  no operation moved by 1% of the time
where the time goes in v8:
time: 34.4 us; the launch traced here: 34.1 us
  blocking collectives  29.2 us (85%)
  Pallas kernels  4.13 us (12%)
  between operations  0.72 us (2%)
    all_to_all x2, blocking collectives, exchange(): lax.all_to_all(grouped, 'row', split_axis=0, concat_axis=0, tiled=True)  29.2 us
    pallas_call x1, Pallas kernels, by_kernels(): pl.pallas_call(functools.partial(finish_kernel, n_row), out_shape=(jax.Sh...  2.24 us
    pallas_call x1, Pallas kernels, by_kernels(): pl.pallas_call(functools.partial(send_kernel, n_row), out_shape=(*(jax.Sh...  1.61 us

profile of v8, /device:TPU:0, one launch (start us, length us, event | category | flops | bytes accessed | tf_op | source)
XLA Modules:
  0.0 34.1 jit_solution(10641589490860125108)
XLA Ops:
  0.6 1.6 %send.1 = (bf16[4,128,128]{2,1,0:T(8,128)(2,1)S(1)}, bf16[64,128]{1,0:T(8,128)(2,1)S(1)}, bf16[4,128]{1,0:T(4,128)(2,1)S(1)}, bf16[1152,128]{1,0:T(8,128)(2,1)S(...) custom-call(bf16[4,128,128]{2,1,0:T(8,128)(2,1)} %pair_hbm.1, ...), custom_call_target="tpu_custom_call" | custom-call | flops 67108864 | bytes 1048576 | tf_op jit(solution)/shard_map/send/pallas_call | solution.py:507
  2.3 0.0 copy-start.4
  2.3 18.5 %all_to_all.10 = bf16[32,9,4,128]{3,2,1,0:T(4,128)(2,1)S(1)} all-to-all(bf16[32,9,4,128]{3,2,1,0:T(4,128)(2,1)S(1)} %bitcast.10), channel_id=1, replica_groups=mesh['groups'=1,'row'=32,'col'=1] {'row'}, dimensions={0} | all-to-all | bytes 589824 | tf_op jit(solution)/shard_map/all_to_all | solution.py:488
  20.8 0.0 copy-done.4
  20.8 0.0 copy-start.3
  20.8 0.0 copy-start.5
  20.8 0.0 copy-start.6
  20.8 0.3 triangle.1
  21.1 0.0 copy-start
  21.1 0.0 copy-start.1
  21.1 0.0 copy-start.2
  21.1 10.7 %all_to_all.11 = bf16[32,5,4,128]{3,2,1,0:T(4,128)(2,1)S(1)} all-to-all(bf16[32,5,4,128]{3,2,1,0:T(4,128)(2,1)S(1)} %bitcast.11), channel_id=1, replica_groups=mesh['groups'=1,'row'=32,'col'=1] {'row'}, dimensions={0} | all-to-all | bytes 327680 | tf_op jit(solution)/shard_map/all_to_all | solution.py:488
  31.8 0.0 copy-done.3
  31.8 0.0 copy-done.5
  31.8 0.0 copy-done.6
  31.9 0.0 copy-done
  31.9 0.0 copy-done.1
  31.9 0.0 copy-done.2
  31.9 2.2 %finish.1 = (bf16[4,128,128]{2,1,0:T(8,128)(2,1)}, bf16[64,128]{1,0:T(8,128)(2,1)}, bf16[4,384]{1,0:T(4,128)(2,1)}) custom-call(bf16[640,128]{1,0:T(8,128)(2,1)S(1)} %bitcast.9, bf16[4,128,128]{2,1,0:T(8,128)(2,1)S(1)} %get-tuple-element.15.pair_ref, bf16[128,128]{1,0:T(8,128)(2,1)S(1)} %copy-done.5, bf16[64,128]{1,0:T(8,128)(2,1)S(1)} %get-tuple-element.16.act_ref, ...), custom_call_target="tpu_custom_call" | custom-call | flops 33554432 | bytes 1048576 | tf_op jit(solution)/shard_map/finish/pallas_call | solution.py:547
Async XLA Ops:
  2.3 18.5 %copy-start.4 = (bf16[128,128]{1,0:T(8,128)(2,1)S(1)}, bf16[128,128]{1,0:T(8,128)(2,1)}, u32[]{:S(2)}) copy-start(bf16[128,128]{1,0:T(8,128)(2,1)} %gate_w_ref.1) | copy-start | bytes 98308
  20.8 11.0 %copy-start.3 = (bf16[256,128]{1,0:T(8,128)(2,1)S(1)}, bf16[256,128]{1,0:T(8,128)(2,1)}, u32[]{:S(2)}) copy-start(bf16[256,128]{1,0:T(8,128)(2,1)} %ffn_out_ref.1) | copy-start | bytes 196612
  20.8 11.0 %copy-start.5 = (bf16[128,128]{1,0:T(8,128)(2,1)S(1)}, bf16[128,128]{1,0:T(8,128)(2,1)}, u32[]{:S(2)}) copy-start(bf16[128,128]{1,0:T(8,128)(2,1)} %out_w_ref.1) | copy-start | bytes 98308
  20.8 11.0 %copy-start.6 = (bf16[128,128]{1,0:T(8,128)(2,1)S(1)}, bf16[128,128]{1,0:T(8,128)(2,1)}, u32[]{:S(2)}) copy-start(bf16[128,128]{1,0:T(8,128)(2,1)} %attn_w_ref.1) | copy-start | bytes 98308
  21.1 10.8 %copy-start = (bf16[128,512]{1,0:T(8,128)(2,1)S(1)}, bf16[128,512]{1,0:T(8,128)(2,1)}, u32[]{:S(2)}) copy-start(bf16[128,512]{1,0:T(8,128)(2,1)} %ffn_in_ref.1) | copy-start | bytes 393220
  21.1 10.8 %copy-start.1 = (bf16[128,384]{1,0:T(8,128)(2,1)S(1)}, bf16[128,384]{1,0:T(8,128)(2,1)}, u32[]{:S(2)}) copy-start(bf16[128,384]{1,0:T(8,128)(2,1)} %qkv_w_ref.1) | copy-start | bytes 294916
  21.1 10.8 %copy-start.2 = (bf16[128,384]{1,0:T(8,128)(2,1)S(1)}, bf16[128,384]{1,0:T(8,128)(2,1)}, u32[]{:S(2)}) copy-start(bf16[128,384]{1,0:T(8,128)(2,1)} %agg_ref.1) | copy-start | bytes 294916

commit v9 on v7

--- a/solution.py
+++ b/solution.py
@@ -444,7 +444,7 @@
         shift = mixture[:, wide : 2 * wide] + mixture[:, 2 * wide : 3 * wide] + mixture[:, 3 * wide :]
         centred = middle - (act_mean + shift)
         spread = jnp.mean(centred * centred, axis=1, keepdims=True)
-        expanded = matmul((centred * lax.rsqrt(spread + EPSILON)).astype(BF16), ffn_in_ref[...])
+        expanded = matmul(centred.astype(BF16), ffn_in_ref[...]) * lax.rsqrt(spread + EPSILON)
         hidden = ffn_out_ref.shape[0]
         inner = (jax.nn.silu(expanded[:, :hidden]) * expanded[:, hidden:]).astype(BF16)
         final = ((middle + matmul(inner, ffn_out_ref[...])) * live_col).astype(BF16)

time: 34.4 us -> 34.3 us (level)
  no operation moved by 1% of the time
where the time goes in v9:
time: 34.3 us; the launch traced here: 34.1 us
  blocking collectives  29.2 us (85%)
  Pallas kernels  4.09 us (12%)
  between operations  0.72 us (2%)
    all_to_all x2, blocking collectives, exchange(): lax.all_to_all(grouped, 'row', split_axis=0, concat_axis=0, tiled=True)  29.2 us
    pallas_call x1, Pallas kernels, by_kernels(): pl.pallas_call(functools.partial(finish_kernel, n_row), out_shape=(jax.Sh...  2.2 us
    pallas_call x1, Pallas kernels, by_kernels(): pl.pallas_call(functools.partial(send_kernel, n_row), out_shape=(*(jax.Sh...  1.61 us

profile of v9, /device:TPU:0, one launch (start us, length us, event | category | flops | bytes accessed | tf_op | source)
XLA Modules:
  0.0 34.1 jit_solution(9400668385658331242)
XLA Ops:
  0.6 1.6 %send.1 = (bf16[4,128,128]{2,1,0:T(8,128)(2,1)S(1)}, bf16[64,128]{1,0:T(8,128)(2,1)S(1)}, bf16[4,128]{1,0:T(4,128)(2,1)S(1)}, bf16[1152,128]{1,0:T(8,128)(2,1)S(...) custom-call(bf16[4,128,128]{2,1,0:T(8,128)(2,1)} %pair_hbm.1, ...), custom_call_target="tpu_custom_call" | custom-call | flops 67108864 | bytes 1048576 | tf_op jit(solution)/shard_map/send/pallas_call | solution.py:500
  2.3 0.0 copy-start.4
  2.3 18.5 %all_to_all.10 = bf16[32,9,4,128]{3,2,1,0:T(4,128)(2,1)S(1)} all-to-all(bf16[32,9,4,128]{3,2,1,0:T(4,128)(2,1)S(1)} %bitcast.10), channel_id=1, replica_groups=mesh['groups'=1,'row'=32,'col'=1] {'row'}, dimensions={0} | all-to-all | bytes 589824 | tf_op jit(solution)/shard_map/all_to_all | solution.py:481
  20.8 0.0 copy-done.4
  20.8 0.0 copy-start.3
  20.8 0.0 copy-start.5
  20.8 0.0 copy-start.6
  20.8 0.3 triangle.1
  21.1 0.0 copy-start
  21.1 0.0 copy-start.1
  21.1 0.0 copy-start.2
  21.1 10.7 %all_to_all.11 = bf16[32,5,4,128]{3,2,1,0:T(4,128)(2,1)S(1)} all-to-all(bf16[32,5,4,128]{3,2,1,0:T(4,128)(2,1)S(1)} %bitcast.11), channel_id=1, replica_groups=mesh['groups'=1,'row'=32,'col'=1] {'row'}, dimensions={0} | all-to-all | bytes 327680 | tf_op jit(solution)/shard_map/all_to_all | solution.py:481
  31.8 0.0 copy-done.3
  31.8 0.0 copy-done.5
  31.8 0.0 copy-done.6
  31.9 0.0 copy-done
  31.9 0.0 copy-done.1
  31.9 0.0 copy-done.2
  31.9 2.2 %finish.1 = (bf16[4,128,128]{2,1,0:T(8,128)(2,1)}, bf16[64,128]{1,0:T(8,128)(2,1)}, bf16[4,384]{1,0:T(4,128)(2,1)}) custom-call(bf16[640,128]{1,0:T(8,128)(2,1)S(1)} %bitcast.9, bf16[4,128,128]{2,1,0:T(8,128)(2,1)S(1)} %get-tuple-element.15.pair_ref, bf16[128,128]{1,0:T(8,128)(2,1)S(1)} %copy-done.5, bf16[64,128]{1,0:T(8,128)(2,1)S(1)} %get-tuple-element.16.act_ref, ...), custom_call_target="tpu_custom_call" | custom-call | flops 33554432 | bytes 1048576 | tf_op jit(solution)/shard_map/finish/pallas_call | solution.py:540
Async XLA Ops:
  2.3 18.5 %copy-start.4 = (bf16[128,128]{1,0:T(8,128)(2,1)S(1)}, bf16[128,128]{1,0:T(8,128)(2,1)}, u32[]{:S(2)}) copy-start(bf16[128,128]{1,0:T(8,128)(2,1)} %gate_w_ref.1) | copy-start | bytes 98308
  20.8 11.0 %copy-start.3 = (bf16[256,128]{1,0:T(8,128)(2,1)S(1)}, bf16[256,128]{1,0:T(8,128)(2,1)}, u32[]{:S(2)}) copy-start(bf16[256,128]{1,0:T(8,128)(2,1)} %ffn_out_ref.1) | copy-start | bytes 196612
  20.8 11.0 %copy-start.5 = (bf16[128,128]{1,0:T(8,128)(2,1)S(1)}, bf16[128,128]{1,0:T(8,128)(2,1)}, u32[]{:S(2)}) copy-start(bf16[128,128]{1,0:T(8,128)(2,1)} %out_w_ref.1) | copy-start | bytes 98308
  20.8 11.0 %copy-start.6 = (bf16[128,128]{1,0:T(8,128)(2,1)S(1)}, bf16[128,128]{1,0:T(8,128)(2,1)}, u32[]{:S(2)}) copy-start(bf16[128,128]{1,0:T(8,128)(2,1)} %attn_w_ref.1) | copy-start | bytes 98308
  21.1 10.8 %copy-start = (bf16[128,512]{1,0:T(8,128)(2,1)S(1)}, bf16[128,512]{1,0:T(8,128)(2,1)}, u32[]{:S(2)}) copy-start(bf16[128,512]{1,0:T(8,128)(2,1)} %ffn_in_ref.1) | copy-start | bytes 393220
  21.1 10.8 %copy-start.1 = (bf16[128,384]{1,0:T(8,128)(2,1)S(1)}, bf16[128,384]{1,0:T(8,128)(2,1)}, u32[]{:S(2)}) copy-start(bf16[128,384]{1,0:T(8,128)(2,1)} %qkv_w_ref.1) | copy-start | bytes 294916
  21.1 10.8 %copy-start.2 = (bf16[128,384]{1,0:T(8,128)(2,1)S(1)}, bf16[128,384]{1,0:T(8,128)(2,1)}, u32[]{:S(2)}) copy-start(bf16[128,384]{1,0:T(8,128)(2,1)} %agg_ref.1) | copy-start | bytes 294916
